TPU v7x, 32 devices: a whole 2x2x4 slice. The times are simulated.
32 devices in a mesh: wide: 16 (over z, x, core), narrow: 2 (over y).
Axes of the slice: x: 2, y: 2, z: 4, core: 2. Of those that a mesh axis runs over, the one named last changes fastest.
Arguments:
- projections: float32 [8, 1152, 1152], P(None, 'wide', 'narrow'), may hold values from -0.1875 to 0.1875
- qkv_weights: float32 [2, 1152, 3456], P(None, 'wide', 'narrow'), may hold values from -0.1875 to 0.1875
- mlp_weights: float32 [2, 1152, 4608], P(None, 'wide', 'narrow'), may hold values from -0.1875 to 0.1875
- ada_weights: float32 [1152, 6912], P('wide', 'narrow'), may hold values from -0.1875 to 0.1875
- entry_weights: float32 [4352, 1152], P('wide', 'narrow'), may hold values from -0.09375 to 0.09375
- patch_weights: float32 [2, 1152, 16], P(None, 'wide', 'narrow'), may hold values from -1.5 to 1.5
- shift_tables: float32 [8, 1152], P('narrow', 'wide'), may hold values from -0.5 to 0.5
- first_projections: float32 [8, 1152, 1152], P(None, 'wide', 'narrow'), may hold values from -1.9073486e-06 to 1.9073486e-06
- first_qkv_weights: float32 [2, 1152, 3456], P(None, 'wide', 'narrow'), may hold values from -1.9073486e-06 to 1.9073486e-06
- first_mlp_weights: float32 [2, 1152, 4608], P(None, 'wide', 'narrow'), may hold values from -1.9073486e-06 to 1.9073486e-06
- first_ada_weights: float32 [1152, 6912], P('wide', 'narrow'), may hold values from -1.9073486e-06 to 1.9073486e-06
- first_entry_weights: float32 [4352, 1152], P('wide', 'narrow'), may hold values from -1.9073486e-06 to 1.9073486e-06
- first_patch_weights: float32 [2, 1152, 16], P(None, 'wide', 'narrow'), may hold values from -1.9073486e-06 to 1.9073486e-06
- first_shift_tables: float32 [8, 1152], P('narrow', 'wide'), may hold values from -1.5258789e-05 to 1.5258789e-05
- second_projections: float32 [8, 1152, 1152], P(None, 'wide', 'narrow'), may hold values from 7.2284855e-16 to 1.1565577e-14
- second_qkv_weights: float32 [2, 1152, 3456], P(None, 'wide', 'narrow'), may hold values from 7.2284855e-16 to 1.1565577e-14
- second_mlp_weights: float32 [2, 1152, 4608], P(None, 'wide', 'narrow'), may hold values from 7.2284855e-16 to 1.1565577e-14
- second_ada_weights: float32 [1152, 6912], P('wide', 'narrow'), may hold values from 7.2284855e-16 to 1.1565577e-14
- second_entry_weights: float32 [4352, 1152], P('wide', 'narrow'), may hold values from 7.2284855e-16 to 1.1565577e-14
- second_patch_weights: float32 [2, 1152, 16], P(None, 'wide', 'narrow'), may hold values from 7.2284855e-16 to 1.1565577e-14
- second_shift_tables: float32 [8, 1152], P('narrow', 'wide'), may hold values from 4.6262307e-14 to 7.401969e-13
- latents: bfloat16 [64, 256, 16], P(('wide', 'narrow')), may hold values from -6 to 6
- noise: bfloat16 [64, 256, 16], P(('wide', 'narrow')), may hold values from -6 to 6
- captions: bfloat16 [64, 120, 4096], P(('wide', 'narrow')), may hold values from -6 to 6
- cap_len: int32 [64], P(('wide', 'narrow')), may hold values from 5 to 120, as said below
- timesteps: int32 [64], P(('wide', 'narrow')), may hold values from 0 to 999
- step_count: int32 [1], replicated, may hold values from 2 to 20
Outputs:
- new_projections: float32 [8, 1152, 1152], P(None, 'wide', 'narrow')
- new_qkv_weights: float32 [2, 1152, 3456], P(None, 'wide', 'narrow')
- new_mlp_weights: float32 [2, 1152, 4608], P(None, 'wide', 'narrow')
- new_ada_weights: float32 [1152, 6912], P('wide', 'narrow')
- new_entry_weights: float32 [4352, 1152], P('wide', 'narrow')
- new_patch_weights: float32 [2, 1152, 16], P(None, 'wide', 'narrow')
- new_shift_tables: float32 [8, 1152], P('narrow', 'wide')
- new_first_projections: float32 [8, 1152, 1152], P(None, 'wide', 'narrow')
- new_first_qkv_weights: float32 [2, 1152, 3456], P(None, 'wide', 'narrow')
- new_first_mlp_weights: float32 [2, 1152, 4608], P(None, 'wide', 'narrow')
- new_first_ada_weights: float32 [1152, 6912], P('wide', 'narrow')
- new_first_entry_weights: float32 [4352, 1152], P('wide', 'narrow')
- new_first_patch_weights: float32 [2, 1152, 16], P(None, 'wide', 'narrow')
- new_first_shift_tables: float32 [8, 1152], P('narrow', 'wide')
- new_second_projections: float32 [8, 1152, 1152], P(None, 'wide', 'narrow')
- new_second_qkv_weights: float32 [2, 1152, 3456], P(None, 'wide', 'narrow')
- new_second_mlp_weights: float32 [2, 1152, 4608], P(None, 'wide', 'narrow')
- new_second_ada_weights: float32 [1152, 6912], P('wide', 'narrow')
- new_second_entry_weights: float32 [4352, 1152], P('wide', 'narrow')
- new_second_patch_weights: float32 [2, 1152, 16], P(None, 'wide', 'narrow')
- new_second_shift_tables: float32 [8, 1152], P('narrow', 'wide')
- loss: float32 [], replicated
- grad_norm: float32 [], replicated
Inputs may be any that keep to these rules, and one draw needn't show every extreme that they name: `cap_len`: clip 0 has all 120 caption tokens.
All inputs are finite; a program needn't handle non-finite values.
Results may differ from a plain program's by a relative error of at most 0.0058.
Values may be sent and summed in bfloat16 or wider, within the bound.
No kernel may reach another device: no remote copies, remote signals or barrier semaphores. Data moves between devices by JAX's collectives and lax.ppermute only.
A program may use at most 576 MiB of HBM per device.

v0:
```python
import math

import jax
import jax.numpy as jnp
from jax import lax
from jax.sharding import PartitionSpec as P

D = 1152
HEADS = 16
HEAD_DIM = 72
CAP = 4096
FREQ = 256
F = 16
S = 16
LCAP = 120


LEARNING_RATE = 0.04


def rounded(values):
    return values.astype(jnp.bfloat16)


def matmul(operand, matrix):
    return jnp.dot(operand, matrix, preferred_element_type=jnp.float32)


def matmul_tn(operand, matrix):
    return lax.dot_general(
        operand, matrix, (((0,), (0,)), ((), ())), preferred_element_type=jnp.float32
    )


def matmul_nt(operand, matrix):
    return lax.dot_general(
        operand, matrix, (((1,), (1,)), ((), ())), preferred_element_type=jnp.float32
    )


def sinusoid(places, feature):
    half_width = feature // 2
    freqs_row = jnp.exp(-math.log(10000.0) * jnp.arange(half_width, dtype=jnp.float32) / half_width)
    angles = places[:, None] * freqs_row[None, :]
    return jnp.concatenate([jnp.cos(angles), jnp.sin(angles)], axis=1)


def layer_norm(values):
    centred = values - jnp.mean(values, axis=-1, keepdims=True)
    return centred * lax.rsqrt(jnp.mean(centred * centred, axis=-1, keepdims=True) + 1e-06)


def modulate(values, shift_row, scale_row):
    return layer_norm(values) * (1.0 + scale_row) + shift_row


def split_heads(values):
    return values.reshape(values.shape[0], values.shape[1], HEADS, HEAD_DIM)


def head_scores(query_heads, key_heads, allowed):
    scores = jnp.einsum(
        "bnhd,bmhd->bhnm", query_heads, key_heads, preferred_element_type=jnp.float32
    ) * HEAD_DIM ** (-0.5)
    if allowed is not None:
        scores = jnp.where(allowed, scores, -1000000000.0)
    return scores


def attend_forward(queries, key_rows, value_rows, allowed):
    scores = head_scores(split_heads(queries), split_heads(key_rows), allowed)
    highest = jnp.max(scores, axis=-1, keepdims=True)
    log_total = highest + jnp.log(jnp.sum(jnp.exp(scores - highest), axis=-1, keepdims=True))
    attention = rounded(jnp.exp(scores - log_total))
    mixture = jnp.einsum(
        "bhnm,bmhd->bnhd", attention, split_heads(value_rows), preferred_element_type=jnp.float32
    )
    return (rounded(mixture.reshape(queries.shape)), log_total)


def attend_backward(queries, key_rows, value_rows, allowed, log_total, grad_mixture):
    query_heads = split_heads(queries)
    key_heads = split_heads(key_rows)
    value_heads = split_heads(value_rows)
    attention = jnp.exp(head_scores(query_heads, key_heads, allowed) - log_total)
    grad_heads = split_heads(grad_mixture)
    grad_values = jnp.einsum(
        "bhnm,bnhd->bmhd", rounded(attention), grad_heads, preferred_element_type=jnp.float32
    )
    grad_weights = jnp.einsum(
        "bnhd,bmhd->bhnm", grad_heads, value_heads, preferred_element_type=jnp.float32
    )
    grad_scores = attention * (
        grad_weights - jnp.sum(grad_weights * attention, axis=-1, keepdims=True)
    )
    grad_low = rounded(grad_scores * HEAD_DIM ** (-0.5))
    grad_queries = jnp.einsum(
        "bhnm,bmhd->bnhd", grad_low, key_heads, preferred_element_type=jnp.float32
    )
    grad_keys = jnp.einsum(
        "bhnm,bnhd->bmhd", grad_low, query_heads, preferred_element_type=jnp.float32
    )
    return (
        grad_queries.reshape(queries.shape),
        grad_keys.reshape(key_rows.shape),
        grad_values.reshape(value_rows.shape),
    )


def gather_all(shards):
    proj_low, qkv_low, mlp_low, ada_low, entry_low, patch_low, table_low = (
        rounded(shard) for shard in shards
    )
    widened = (
        lax.all_gather(proj_low, "narrow", axis=2, tiled=True),
        lax.all_gather(qkv_low, "narrow", axis=2, tiled=True),
        lax.all_gather(mlp_low, "narrow", axis=2, tiled=True),
        lax.all_gather(ada_low, "narrow", axis=1, tiled=True),
        lax.all_gather(entry_low, "narrow", axis=1, tiled=True),
        lax.all_gather(patch_low, "narrow", axis=2, tiled=True),
        lax.all_gather(table_low, "narrow", axis=0, tiled=True),
    )
    proj_cols, qkv_cols, mlp_cols, ada_cols, entry_cols, patch_cols, table_cols = widened
    return (
        lax.all_gather(proj_cols, "wide", axis=1, tiled=True),
        lax.all_gather(qkv_cols, "wide", axis=1, tiled=True),
        lax.all_gather(mlp_cols, "wide", axis=1, tiled=True),
        lax.all_gather(ada_cols, "wide", axis=0, tiled=True),
        lax.all_gather(entry_cols, "wide", axis=0, tiled=True),
        lax.all_gather(patch_cols, "wide", axis=1, tiled=True),
        lax.all_gather(table_cols, "wide", axis=1, tiled=True),
    )


def reduce_all(gradients):
    proj_grad, qkv_grad, mlp_grad, ada_grad, entry_grad, patch_grad, table_grad = gradients
    row_parts = (
        lax.psum_scatter(proj_grad, "wide", scatter_dimension=1, tiled=True),
        lax.psum_scatter(qkv_grad, "wide", scatter_dimension=1, tiled=True),
        lax.psum_scatter(mlp_grad, "wide", scatter_dimension=1, tiled=True),
        lax.psum_scatter(ada_grad, "wide", scatter_dimension=0, tiled=True),
        lax.psum_scatter(entry_grad, "wide", scatter_dimension=0, tiled=True),
        lax.psum_scatter(patch_grad, "wide", scatter_dimension=1, tiled=True),
        lax.psum_scatter(table_grad, "wide", scatter_dimension=1, tiled=True),
    )
    proj_rows, qkv_rows, mlp_rows, ada_rows, entry_rows, patch_rows, table_rows = row_parts
    return (
        lax.psum_scatter(proj_rows, "narrow", scatter_dimension=2, tiled=True),
        lax.psum_scatter(qkv_rows, "narrow", scatter_dimension=2, tiled=True),
        lax.psum_scatter(mlp_rows, "narrow", scatter_dimension=2, tiled=True),
        lax.psum_scatter(ada_rows, "narrow", scatter_dimension=1, tiled=True),
        lax.psum_scatter(entry_rows, "narrow", scatter_dimension=1, tiled=True),
        lax.psum_scatter(patch_rows, "narrow", scatter_dimension=2, tiled=True),
        lax.psum_scatter(table_rows, "narrow", scatter_dimension=0, tiled=True),
    )


def video_gradients(fetcher, latent, noise_row, caption, length, timestep, video_count):
    gathered = fetcher(latent)
    (
        projections,
        qkv_weights,
        mlp_weights,
        ada_weights,
        entry_weights,
        patch_weights,
        shift_tables,
    ) = gathered
    tokens = F * S
    time_value = timestep.astype(jnp.float32)
    signal = jnp.cos((time_value / 1000.0 + 0.008) / 1.008 * (math.pi / 2)) ** 2
    noised = jnp.sqrt(signal) * latent.astype(jnp.float32) + jnp.sqrt(
        1.0 - signal
    ) * noise_row.astype(jnp.float32)
    noised_low = rounded(noised)
    spatial_pos = jnp.tile(sinusoid(jnp.arange(S, dtype=jnp.float32), D), (F, 1))
    frame_pos = sinusoid(jnp.arange(F, dtype=jnp.float32), D)
    hidden = matmul_nt(noised_low, patch_weights[0]) + spatial_pos
    embed_low = rounded(sinusoid(time_value.reshape(1), FREQ))
    time_inner = matmul(embed_low, entry_weights[CAP:])
    inner_low = rounded(jax.nn.silu(time_inner))
    time_embed = matmul(inner_low, projections[0])
    embed_act = rounded(jax.nn.silu(time_embed))
    modulations = matmul(embed_act, ada_weights).reshape(6, D) + shift_tables[:6].astype(
        jnp.float32
    )
    caption_inner = matmul(caption, entry_weights[:CAP])
    caption_act = rounded(jax.nn.gelu(caption_inner))
    context_low = rounded(matmul(caption_act, projections[1]))
    normed_spatial = rounded(modulate(hidden, modulations[0], modulations[1]))
    spatial_qkv = rounded(matmul(normed_spatial, qkv_weights[0])).reshape(F, S, 3 * D)
    spatial_mix, spatial_lse = attend_forward(
        spatial_qkv[..., :D], spatial_qkv[..., D : 2 * D], spatial_qkv[..., 2 * D :], None
    )
    spatial_flat = spatial_mix.reshape(tokens, D)
    spatial_out = matmul(spatial_flat, projections[2])
    hidden_one = hidden + modulations[2] * spatial_out
    temporal_in = rounded((hidden_one.reshape(F, S, D) + frame_pos[:, None, :]).reshape(tokens, D))
    temporal_qkv = (
        rounded(matmul(temporal_in, qkv_weights[1])).reshape(F, S, 3 * D).transpose(1, 0, 2)
    )
    temporal_mix, temporal_lse = attend_forward(
        temporal_qkv[..., :D], temporal_qkv[..., D : 2 * D], temporal_qkv[..., 2 * D :], None
    )
    temporal_flat = temporal_mix.transpose(1, 0, 2).reshape(tokens, D)
    temporal_out = matmul(temporal_flat, projections[3])
    hidden_two = hidden_one + modulations[2] * temporal_out
    hidden_two_low = rounded(hidden_two)
    cross_query = rounded(matmul(hidden_two_low, projections[4]))
    pair_weight = jnp.concatenate([projections[5], projections[6]], axis=1)
    cross_pairs = rounded(matmul(context_low, pair_weight))
    allowed = (jnp.arange(LCAP) < length)[None, None, None, :]
    cross_mix, cross_lse = attend_forward(
        cross_query[None], cross_pairs[None, :, :D], cross_pairs[None, :, D:], allowed
    )
    cross_out = matmul(cross_mix[0], projections[7])
    hidden_three = hidden_two + cross_out
    normed_mlp = rounded(modulate(hidden_three, modulations[3], modulations[4]))
    expand = matmul(normed_mlp, mlp_weights[0])
    expand_act = rounded(jax.nn.gelu(expand))
    contract = matmul_nt(expand_act, mlp_weights[1])
    hidden_four = hidden_three + modulations[5] * contract
    final_shift = time_embed[0] + shift_tables[6].astype(jnp.float32)
    final_scale = time_embed[0] + shift_tables[7].astype(jnp.float32)
    final_low = rounded(modulate(hidden_four, final_shift, final_scale))
    misfit = matmul(final_low, patch_weights[1]) - noise_row.astype(jnp.float32)
    loss_value = jnp.mean(misfit * misfit) / video_count
    gathered = fetcher(loss_value)
    (
        projections,
        qkv_weights,
        mlp_weights,
        ada_weights,
        entry_weights,
        patch_weights,
        shift_tables,
    ) = gathered
    pair_weight = jnp.concatenate([projections[5], projections[6]], axis=1)
    grad_pred = rounded(2.0 * misfit / (misfit.size * video_count))
    grad_patch_out = matmul_tn(final_low, grad_pred)
    _, pull_final = jax.vjp(modulate, hidden_four, final_shift, final_scale)
    grad_four, grad_fshift, grad_fscale = pull_final(matmul_nt(grad_pred, patch_weights[1]))
    grad_contract = rounded(grad_four * modulations[5])
    grad_gate_mlp = jnp.sum(grad_four * contract, axis=0)
    grad_mlp_out = matmul_tn(grad_contract, expand_act)
    _, pull_gelu = jax.vjp(jax.nn.gelu, expand)
    grad_expand = rounded(pull_gelu(matmul(grad_contract, mlp_weights[1]))[0])
    grad_mlp_in = matmul_tn(normed_mlp, grad_expand)
    _, pull_mlp_norm = jax.vjp(modulate, hidden_three, modulations[3], modulations[4])
    grad_three_part, grad_shift_mlp, grad_scale_mlp = pull_mlp_norm(
        matmul_nt(grad_expand, mlp_weights[0])
    )
    grad_three = grad_four + grad_three_part
    grad_cross_out = rounded(grad_three)
    grad_proj_seven = matmul_tn(cross_mix[0], grad_cross_out)
    grad_cross_mix = rounded(matmul_nt(grad_cross_out, projections[7]))
    grad_cq, grad_ck, grad_cv = attend_backward(
        cross_query[None],
        cross_pairs[None, :, :D],
        cross_pairs[None, :, D:],
        allowed,
        cross_lse,
        grad_cross_mix[None],
    )
    grad_query_low = rounded(grad_cq[0])
    grad_pairs_low = rounded(jnp.concatenate([grad_ck[0], grad_cv[0]], axis=1))
    grad_proj_four = matmul_tn(hidden_two_low, grad_query_low)
    grad_pair = matmul_tn(context_low, grad_pairs_low)
    grad_context = rounded(matmul_nt(grad_pairs_low, pair_weight))
    grad_proj_one = matmul_tn(caption_act, grad_context)
    _, pull_caption = jax.vjp(jax.nn.gelu, caption_inner)
    grad_caption_inner = rounded(pull_caption(matmul_nt(grad_context, projections[1]))[0])
    grad_entry_caption = matmul_tn(caption, grad_caption_inner)
    grad_two = grad_three + matmul_nt(grad_query_low, projections[4])
    grad_temporal_out = rounded(grad_two * modulations[2])
    grad_gate_attn = jnp.sum(grad_two * temporal_out, axis=0)
    grad_proj_three = matmul_tn(temporal_flat, grad_temporal_out)
    grad_temporal_mix = (
        rounded(matmul_nt(grad_temporal_out, projections[3])).reshape(F, S, D).transpose(1, 0, 2)
    )
    grad_tq, grad_tk, grad_tv = attend_backward(
        temporal_qkv[..., :D],
        temporal_qkv[..., D : 2 * D],
        temporal_qkv[..., 2 * D :],
        None,
        temporal_lse,
        grad_temporal_mix,
    )
    grad_temporal_qkv = rounded(
        jnp.concatenate([grad_tq, grad_tk, grad_tv], axis=2)
        .transpose(1, 0, 2)
        .reshape(tokens, 3 * D)
    )
    grad_qkv_temporal = matmul_tn(temporal_in, grad_temporal_qkv)
    grad_one = grad_two + matmul_nt(grad_temporal_qkv, qkv_weights[1])
    grad_spatial_out = rounded(grad_one * modulations[2])
    grad_gate_attn = grad_gate_attn + jnp.sum(grad_one * spatial_out, axis=0)
    grad_proj_two = matmul_tn(spatial_flat, grad_spatial_out)
    grad_spatial_mix = rounded(matmul_nt(grad_spatial_out, projections[2])).reshape(F, S, D)
    grad_sq, grad_sk, grad_sv = attend_backward(
        spatial_qkv[..., :D],
        spatial_qkv[..., D : 2 * D],
        spatial_qkv[..., 2 * D :],
        None,
        spatial_lse,
        grad_spatial_mix,
    )
    grad_spatial_qkv = rounded(
        jnp.concatenate([grad_sq, grad_sk, grad_sv], axis=2).reshape(tokens, 3 * D)
    )
    grad_qkv_spatial = matmul_tn(normed_spatial, grad_spatial_qkv)
    _, pull_spatial_norm = jax.vjp(modulate, hidden, modulations[0], modulations[1])
    grad_hidden_part, grad_shift_attn, grad_scale_attn = pull_spatial_norm(
        matmul_nt(grad_spatial_qkv, qkv_weights[0])
    )
    grad_hidden = rounded(grad_one + grad_hidden_part)
    grad_patch_in = matmul_tn(grad_hidden, noised_low)
    grad_modulations = jnp.stack(
        [
            grad_shift_attn,
            grad_scale_attn,
            grad_gate_attn,
            grad_shift_mlp,
            grad_scale_mlp,
            grad_gate_mlp,
        ]
    )
    grad_ada_out = rounded(grad_modulations.reshape(1, 6 * D))
    grad_ada = matmul_tn(embed_act, grad_ada_out)
    _, pull_embed = jax.vjp(jax.nn.silu, time_embed)
    grad_time_embed = rounded(
        pull_embed(matmul_nt(grad_ada_out, ada_weights))[0] + (grad_fshift + grad_fscale)[None, :]
    )
    grad_proj_zero = matmul_tn(inner_low, grad_time_embed)
    _, pull_inner = jax.vjp(jax.nn.silu, time_inner)
    grad_time_inner = rounded(pull_inner(matmul_nt(grad_time_embed, projections[0]))[0])
    grad_entry_time = matmul_tn(embed_low, grad_time_inner)
    grad_tables = jnp.concatenate(
        [grad_modulations, grad_fshift[None, :], grad_fscale[None, :]], axis=0
    )
    grad_projections = jnp.stack(
        [
            grad_proj_zero,
            grad_proj_one,
            grad_proj_two,
            grad_proj_three,
            grad_proj_four,
            grad_pair[:, :D],
            grad_pair[:, D:],
            grad_proj_seven,
        ]
    )
    gradients = (
        grad_projections,
        jnp.stack([grad_qkv_spatial, grad_qkv_temporal]),
        jnp.stack([grad_mlp_in, grad_mlp_out]),
        grad_ada,
        jnp.concatenate([grad_entry_caption, grad_entry_time], axis=0),
        jnp.stack([grad_patch_in, grad_patch_out]),
        grad_tables,
    )
    return (loss_value, gradients)


def adam_update(master, first_moment, second_moment, gradient, step_value):
    first_new = 0.9 * first_moment + 0.1 * gradient
    second_new = 0.999 * second_moment + 0.001 * gradient * gradient
    first_hat = first_new / (1.0 - 0.9**step_value)
    second_hat = second_new / (1.0 - 0.999**step_value)
    master_new = master - LEARNING_RATE * (
        first_hat / (jnp.sqrt(second_hat) + 1e-08) + 0.01 * master
    )
    return (master_new, first_new, second_new)


def body(
    projections,
    qkv_weights,
    mlp_weights,
    ada_weights,
    entry_weights,
    patch_weights,
    shift_tables,
    first_projections,
    first_qkv_weights,
    first_mlp_weights,
    first_ada_weights,
    first_entry_weights,
    first_patch_weights,
    first_shift_tables,
    second_projections,
    second_qkv_weights,
    second_mlp_weights,
    second_ada_weights,
    second_entry_weights,
    second_patch_weights,
    second_shift_tables,
    latents,
    noise,
    captions,
    cap_len,
    timesteps,
    step_count,
):
    shards = (
        projections,
        qkv_weights,
        mlp_weights,
        ada_weights,
        entry_weights,
        patch_weights,
        shift_tables,
    )
    firsts = (
        first_projections,
        first_qkv_weights,
        first_mlp_weights,
        first_ada_weights,
        first_entry_weights,
        first_patch_weights,
        first_shift_tables,
    )
    seconds = (
        second_projections,
        second_qkv_weights,
        second_mlp_weights,
        second_ada_weights,
        second_entry_weights,
        second_patch_weights,
        second_shift_tables,
    )
    video_count = latents.shape[0] * lax.axis_size("wide") * lax.axis_size("narrow")
    kept_whole = gather_all(shards)

    def fetcher(anchor):
        return kept_whole

    summed = None
    loss_sum = jnp.zeros((), jnp.float32)
    for batch_index in range(latents.shape[0]):
        loss_value, gradients = video_gradients(
            fetcher,
            latents[batch_index],
            noise[batch_index],
            captions[batch_index],
            cap_len[batch_index],
            timesteps[batch_index],
            video_count,
        )
        loss_sum = loss_sum + loss_value
        summed = (
            gradients
            if summed is None
            else tuple((left_part + right_part for left_part, right_part in zip(summed, gradients)))
        )
    summed = reduce_all(summed)
    square_part = sum((jnp.sum(piece * piece) for piece in summed))
    loss_total, square_total = lax.psum((loss_sum, square_part), ("wide", "narrow"))
    grad_norm = jnp.sqrt(square_total)
    threshold = (video_count * latents.shape[1]) ** (-0.5)
    factor = threshold / jnp.maximum(grad_norm, threshold)
    step_value = step_count[0].astype(jnp.float32)
    updated = [
        adam_update(master, first_moment, second_moment, gradient * factor, step_value)
        for master, first_moment, second_moment, gradient in zip(shards, firsts, seconds, summed)
    ]
    return (
        updated[0][0],
        updated[1][0],
        updated[2][0],
        updated[3][0],
        updated[4][0],
        updated[5][0],
        updated[6][0],
        updated[0][1],
        updated[1][1],
        updated[2][1],
        updated[3][1],
        updated[4][1],
        updated[5][1],
        updated[6][1],
        updated[0][2],
        updated[1][2],
        updated[2][2],
        updated[3][2],
        updated[4][2],
        updated[5][2],
        updated[6][2],
        loss_total,
        grad_norm,
    )


def solution(mesh):
    return jax.shard_map(
        body,
        mesh=mesh,
        in_specs=(
            P(None, "wide", "narrow"),
            P(None, "wide", "narrow"),
            P(None, "wide", "narrow"),
            P("wide", "narrow"),
            P("wide", "narrow"),
            P(None, "wide", "narrow"),
            P("narrow", "wide"),
            P(None, "wide", "narrow"),
            P(None, "wide", "narrow"),
            P(None, "wide", "narrow"),
            P("wide", "narrow"),
            P("wide", "narrow"),
            P(None, "wide", "narrow"),
            P("narrow", "wide"),
            P(None, "wide", "narrow"),
            P(None, "wide", "narrow"),
            P(None, "wide", "narrow"),
            P("wide", "narrow"),
            P("wide", "narrow"),
            P(None, "wide", "narrow"),
            P("narrow", "wide"),
            P(("wide", "narrow"), None, None),
            P(("wide", "narrow"), None, None),
            P(("wide", "narrow"), None, None),
            P(("wide", "narrow")),
            P(("wide", "narrow")),
            P(),
        ),
        out_specs=(
            P(None, "wide", "narrow"),
            P(None, "wide", "narrow"),
            P(None, "wide", "narrow"),
            P("wide", "narrow"),
            P("wide", "narrow"),
            P(None, "wide", "narrow"),
            P("narrow", "wide"),
            P(None, "wide", "narrow"),
            P(None, "wide", "narrow"),
            P(None, "wide", "narrow"),
            P("wide", "narrow"),
            P("wide", "narrow"),
            P(None, "wide", "narrow"),
            P("narrow", "wide"),
            P(None, "wide", "narrow"),
            P(None, "wide", "narrow"),
            P(None, "wide", "narrow"),
            P("wide", "narrow"),
            P("wide", "narrow"),
            P(None, "wide", "narrow"),
            P("narrow", "wide"),
            P(),
            P(),
        ),
        check_vma=False,
    )
```

profile of v0, /device:TPU:0, one launch (start us, length us, event | category | flops | bytes accessed | tf_op | source)
XLA Modules:
  0.0 3085.0 jit_solution(4479656606659378455)
XLA Ops:
  11.7 13.4 all-gather
  27.1 24.9 all_gather.48
  65.7 36.3 %all_gather.52 = bf16[2,72,3456]{1,0,2:T(2,128)(2,1)S(1)} all-gather(bf16[2,72,1728]{1,0,2:T(2,128)(2,1)S(1)} %copy.605), channel_id=1, replica_groups=mesh['wide'=16,'narrow'=2] {'narrow'}, dimensions={2}, use_global_device_ids=true | all-gather | bytes 1492992 | tf_op jit(solution)/shard_map/all_gather | solution.py:116
  113.7 22.3 all-gather.2
  140.7 22.3 all_gather.45
  171.4 22.3 all-gather.11.cloned.1.call-done
  208.4 108.1 %all-gather.17.cloned.1.call-done = bf16[1152,6912]{1,0:T(8,128)(2,1)} async-done(((bf16[72,6912]{1,0:T(8,128)(2,1)}), bf16[1152,6912]{1,0:T(8,128)(2,1)}) %all-gather.17.cloned.1.call-update) | async-done | bytes 15925264 | tf_op jit(solution)/shard_map/all_gather | solution.py:128
  316.5 20.7 copy.603
  337.2 89.5 %all-gather.15.cloned.1.call-done = bf16[8,1152,1152]{2,1,0:T(8,128)(2,1)} async-done(((bf16[8,72,1152]{2,1,0:T(8,128)(2,1)}), bf16[8,1152,1152]{2,1,0:T(8,128)(2,1)}) %all-gather.15.cloned.1.call-update) | async-done | bytes 21233680 | tf_op jit(solution)/shard_map/all_gather | solution.py:125
  453.0 97.9 %all-gather.19.cloned.1.call-done = bf16[2,1152,3456]{2,1,0:T(8,128)(2,1)} async-done(((bf16[2,72,3456]{2,1,0:T(8,128)(2,1)}), bf16[2,1152,3456]{2,1,0:T(8,128)(2,1)}) %all-gather.19.cloned.1.call-update) | async-done | bytes 15925264 | tf_op jit(solution)/shard_map/all_gather | solution.py:126
  1069.0 12.3 convolution_bitcast_fusion.4
  1081.3 12.4 convolution_bitcast_fusion.5
  1093.8 20.6 maximum_add_fusion.2
  1114.4 21.9 copy.695
  1136.4 12.8 convolution_bitcast_fusion.6
  1149.2 11.5 convolution_bitcast_fusion.8
  1177.9 32.3 %maximum_add_fusion.1 = f32[2,1152,3456]{2,1,0:T(8,128)} fusion(f32[1,1152,3456]{2,1,0:T(8,128)} %convolution_bitcast_fusion.8, f32[1,1152,3456]{2,1,0:T(8,128)} %convolution_bitcast_fusion.9, f32[1,1152,3456]{2,1,0:T(8,128)} %convolution_bitcast_fusion.6, f32[1,1152,3456]{2,1,0:T(8,128)} %convolution_bitcast_fusion.7), kind=kLoop, calls=%fused_computation.7 | loop fusion | flops 23887872 | bytes 95551488 | tf_op jit(solution)/shard_map/add | solution.py:454
  1211.1 11.2 multiply_add_fusion
  1275.9 42.7 %add.668 = f32[8,1152,1152]{2,1,0:T(8,128)} add(f32[8,1152,1152]{2,1,0:T(8,128)} %fusion.11, f32[8,1152,1152]{2,1,0:T(8,128)} %fusion.6) | non-fusion elementwise | flops 10616832 | bytes 127401984 | tf_op jit(solution)/shard_map/add | solution.py:454
  1320.0 12.1 convolution_bitcast_fusion.1
  1350.5 12.4 convolution_bitcast_fusion.2
  1362.9 50.1 %maximum_add_fusion = f32[2,1152,4608]{2,1,0:T(8,128)} fusion(f32[1,1152,4608]{2,1,0:T(8,128)} %convolution_bitcast_fusion.2, f32[1,1152,4608]{2,1,0:T(8,128)} %convolution_bitcast_fusion.3, f32[1,1152,4608]{2,1,0:T(8,128)} %convolution_bitcast_fusion, f32[1,1152,4608]{2,1,0:T(8,128)} %convolution_bitcast_fusion.1), kind=kLoop, calls=%fused_computation.6 | loop fusion | flops 31850496 | bytes 127401984 | tf_op jit(solution)/shard_map/add | solution.py:454
  1419.7 245.3 %reduce-scatter.24.cloned.1.call-done = f32[2,72,3456]{2,1,0:T(8,128)} async-done(((f32[2,1152,3456]{2,1,0:T(8,128)}), f32[2,72,3456]{2,1,0:T(8,128)}) %reduce-scatter.24.cloned.1.call-update) | async-done | bytes 1990672 | tf_op jit(solution)/shard_map/reduce_scatter | solution.py:139
  1673.5 315.6 %reduce-scatter.30.cloned.1.call-done = f32[72,6912]{1,0:T(8,128)} async-done(((f32[1152,6912]{1,0:T(8,128)}), f32[72,6912]{1,0:T(8,128)}) %reduce-scatter.30.cloned.1.call-update) | async-done | bytes 1990672 | tf_op jit(solution)/shard_map/reduce_scatter | solution.py:141
  1989.1 408.3 %reduce-scatter.22.cloned.1.call-done = f32[8,72,1152]{2,1,0:T(8,128)} async-done(((f32[8,1152,1152]{2,1,0:T(8,128)}), f32[8,72,1152]{2,1,0:T(8,128)}) %reduce-scatter.22.cloned.1.call-update) | async-done | bytes 2654224 | tf_op jit(solution)/shard_map/reduce_scatter | solution.py:138
  2408.1 397.3 %reduce-scatter.26.cloned.1.call-done = f32[2,72,4608]{2,1,0:T(8,128)} async-done(((f32[2,1152,4608]{2,1,0:T(8,128)}), f32[2,72,4608]{2,1,0:T(8,128)}) %reduce-scatter.26.cloned.1.call-update) | async-done | bytes 2654224 | tf_op jit(solution)/shard_map/reduce_scatter | solution.py:140
  2809.2 59.6 %all-reduce.1 = f32[8,1152]{1,0:T(8,128)S(1)} all-reduce(f32[8,1152]{1,0:T(8,128)S(1)} %add.683), channel_id=14, replica_groups=mesh['wide'=16,'narrow'=2] {'wide'}, use_global_device_ids=true, to_apply=%region_78.79.clone | all-reduce | flops 9216 | bytes 73728
  2878.0 19.4 reduce-scatter.38.cloned.1.call-done
  2903.5 26.7 reduce-scatter.32.cloned.1.call-done
  2933.2 40.5 %reduce-scatter.36.cloned.1.call-done = f32[576,576]{1,0:T(8,128)} async-done(((f32[1152,576]{1,0:T(8,128)}), f32[576,576]{1,0:T(8,128)}) %reduce-scatter.36.cloned.1.call-update) | async-done | bytes 1327120
  2981.8 32.2 %reduce-scatter.28.cloned.1.call-done = f32[2,72,2304]{2,1,0:T(8,128)} async-done(((f32[2,72,4608]{2,1,0:T(8,128)}), f32[2,72,2304]{2,1,0:T(8,128)}) %reduce-scatter.28.cloned.1.call-update) | async-done | bytes 1327120 | tf_op jit(solution)/shard_map/reduce_scatter | solution.py:150
  3019.5 39.6 %all-reduce.3 = (f32[]{:T(128)}, f32[]{:T(128)}) all-reduce(f32[]{:T(128)S(6)} %add.684, f32[]{:T(128)S(6)} %add.720), channel_id=1, replica_groups=mesh['wide'=16,'narrow'=2] {'wide','narrow'}, use_global_device_ids=true, to_apply=%region_81.82 | all-reduce | flops 2 | bytes 16 | tf_op jit(solution)/shard_map/psum | solution.py:458
  (1001 shorter events, 761.3 us)
Async XLA Ops:
  7.2 52.9 %all-gather.13.cloned.1.call-start = ((), (), s32[]{:S(2)}) async-start(), calls=%async_computation.12 | async-start | bytes 3538944 | tf_op jit(solution)/shard_map/all_gather | solution.py:115
  10.5 94.8 %all-gather.21.cloned.1.call-start = ((), (), s32[]{:S(2)}) async-start(), calls=%async_computation.16 | async-start | bytes 1990656 | tf_op jit(solution)/shard_map/all_gather | solution.py:117
  11.5 182.1 %all-gather.11.cloned.1.call-start = ((), (), s32[]{:S(2)}) async-start(), calls=%async_computation.11 | async-start | bytes 10653696 | tf_op jit(solution)/shard_map/all_gather | solution.py:129
  27.0 289.6 %all-gather.17.cloned.1.call-start = ((), (), s32[]{:S(2)}) async-start(), calls=%async_computation.14 | async-start | bytes 16920576 | tf_op jit(solution)/shard_map/all_gather | solution.py:128
  52.0 374.7 %all-gather.15.cloned.1.call-start = ((), (), s32[]{:S(2)}) async-start(), calls=%async_computation.13 | async-start | bytes 22560768 | tf_op jit(solution)/shard_map/all_gather | solution.py:125
  64.1 486.8 %all-gather.19.cloned.1.call-start = ((), (), s32[]{:S(2)}) async-start(), calls=%async_computation.15 | async-start | bytes 16920576 | tf_op jit(solution)/shard_map/all_gather | solution.py:126
  105.2 555.5 %all-gather.23.cloned.1.call-start = ((), (), s32[]{:S(2)}) async-start(), calls=%async_computation.17 | async-start | bytes 22560768 | tf_op jit(solution)/shard_map/all_gather | solution.py:127
  106.0 1308.9 %all-reduce.6.cloned.1.call-start = ((), (), s32[]{:S(2)}) async-start(), calls=%async_computation.29 | async-start | bytes 294912
  169.7 459.1 %copy-start = (f32[256,1152]{1,0:T(8,128)}, f32[256,1152]{1,0:T(8,128)S(1)}, u32[]{:S(2)}) copy-start(f32[256,1152]{1,0:T(8,128)S(1)} %get-tuple-element.291) | copy-start | bytes 3538948
  1017.3 399.4 %reduce-scatter.40.cloned.1.call-start = ((), (), s32[]{:S(2)}) async-start(), calls=%async_computation.27 | async-start | bytes 21307392 | tf_op jit(solution)/shard_map/reduce_scatter | solution.py:142
  1136.3 528.7 %reduce-scatter.24.cloned.1.call-start = ((), (), s32[]{:S(2)}) async-start(), calls=%async_computation.19 | async-start | bytes 33841152 | tf_op jit(solution)/shard_map/reduce_scatter | solution.py:139
  1210.2 778.8 %reduce-scatter.30.cloned.1.call-start = ((), (), s32[]{:S(2)}) async-start(), calls=%async_computation.22 | async-start | bytes 33841152 | tf_op jit(solution)/shard_map/reduce_scatter | solution.py:141
  1222.3 1175.1 %reduce-scatter.22.cloned.1.call-start = ((), (), s32[]{:S(2)}) async-start(), calls=%async_computation.18 | async-start | bytes 45121536 | tf_op jit(solution)/shard_map/reduce_scatter | solution.py:138
  1318.8 1486.6 %reduce-scatter.26.cloned.1.call-start = ((), (), s32[]{:S(2)}) async-start(), calls=%async_computation.20 | async-start | bytes 45121536 | tf_op jit(solution)/shard_map/reduce_scatter | solution.py:140
  1413.0 1461.5 %reduce-scatter.34.cloned.1.call-start = ((), (), s32[]{:S(2)}) async-start(), calls=%async_computation.24 | async-start | bytes 24576 | tf_op jit(solution)/shard_map/reduce_scatter | solution.py:153
  1416.3 1459.4 %reduce-scatter.42.cloned.1.call-start = ((), (), s32[]{:S(2)}) async-start(), calls=%async_computation.28 | async-start | bytes 2654208
  1419.7 1477.7 %reduce-scatter.38.cloned.1.call-start = ((), (), s32[]{:S(2)}) async-start(), calls=%async_computation.26 | async-start | bytes 5308416
  1673.4 1256.8 %reduce-scatter.32.cloned.1.call-start = ((), (), s32[]{:S(2)}) async-start(), calls=%async_computation.23 | async-start | bytes 2985984 | tf_op jit(solution)/shard_map/reduce_scatter | solution.py:151
  1989.1 984.6 %reduce-scatter.36.cloned.1.call-start = ((), (), s32[]{:S(2)}) async-start(), calls=%async_computation.25 | async-start | bytes 4423680
  2407.9 399.6 %copy-start.201 = (f32[1152]{0:T(1024)S(1)}, f32[1152]{0:T(1024)}, u32[]{:S(2)}) copy-start(f32[1152]{0:T(1024)} %get-tuple-element.262) | copy-start | bytes 13828
  2407.9 399.6 %copy-start.246 = (f32[1152]{0:T(1024)S(1)}, f32[1152]{0:T(1024)}, u32[]{:S(2)}) copy-start(f32[1152]{0:T(1024)} %get-tuple-element.165) | copy-start | bytes 13828
  2407.9 399.6 %copy-start.207 = (f32[1152]{0:T(1024)S(1)}, f32[1152]{0:T(1024)}, u32[]{:S(2)}) copy-start(f32[1152]{0:T(1024)} %get-tuple-element.176) | copy-start | bytes 13828
  2407.9 399.6 %copy-start.205 = (f32[1152]{0:T(1024)S(1)}, f32[1152]{0:T(1024)}, u32[]{:S(2)}) copy-start(f32[1152]{0:T(1024)} %get-tuple-element.168) | copy-start | bytes 13828
  2408.0 399.6 %copy-start.219 = (f32[1152]{0:T(1024)S(1)}, f32[1152]{0:T(1024)}, u32[]{:S(2)}) copy-start(f32[1152]{0:T(1024)} %copy-done.218) | copy-start | bytes 13828
  2408.0 399.6 %copy-start.257 = (f32[1152]{0:T(1024)S(1)}, f32[1152]{0:T(1024)}, u32[]{:S(2)}) copy-start(f32[1152]{0:T(1024)} %get-tuple-element.174) | copy-start | bytes 13828
  2408.0 399.6 %copy-start.255 = (f32[1152]{0:T(1024)S(1)}, f32[1152]{0:T(1024)}, u32[]{:S(2)}) copy-start(f32[1152]{0:T(1024)} %get-tuple-element.164) | copy-start | bytes 13828
  2408.0 399.7 %copy-start.203 = (f32[1152]{0:T(1024)S(1)}, f32[1152]{0:T(1024)}, u32[]{:S(2)}) copy-start(f32[1152]{0:T(1024)} %get-tuple-element.264) | copy-start | bytes 13828
  2408.0 399.7 %copy-start.251 = (f32[1152]{0:T(1024)S(1)}, f32[1152]{0:T(1024)}, u32[]{:S(2)}) copy-start(f32[1152]{0:T(1024)} %get-tuple-element.177) | copy-start | bytes 13828
  2408.0 399.7 %copy-start.249 = (f32[1152]{0:T(1024)S(1)}, f32[1152]{0:T(1024)}, u32[]{:S(2)}) copy-start(f32[1152]{0:T(1024)} %get-tuple-element.169) | copy-start | bytes 13828
  2408.0 399.7 %copy-start.211 = (f32[1152]{0:T(1024)S(1)}, f32[1152]{0:T(1024)}, u32[]{:S(2)}) copy-start(f32[1152]{0:T(1024)} %get-tuple-element.178) | copy-start | bytes 13828
  2408.0 399.7 %copy-start.209 = (f32[1152]{0:T(1024)S(1)}, f32[1152]{0:T(1024)}, u32[]{:S(2)}) copy-start(f32[1152]{0:T(1024)} %get-tuple-element.172) | copy-start | bytes 13828
  2408.0 605.9 %reduce-scatter.28.cloned.1.call-start = ((), (), s32[]{:S(2)}) async-start(), calls=%async_computation.21 | async-start | bytes 3981312 | tf_op jit(solution)/shard_map/reduce_scatter | solution.py:150
  (277 other events, 5366.5 us)
Sparse Core Ops, SparseCore 0:
  10.6 49.4 all-gather.12
  62.2 39.3 all-gather.20
  104.4 89.1 all-gather.10
  195.6 120.8 all-gather.16
  318.5 108.1 all-gather.14
  429.4 121.5 all-gather.18
  552.5 108.1 all-gather.22
  1017.4 87.7 all-reduce.5
  1136.4 204.1 reduce-scatter.39
  1345.3 319.7 reduce-scatter.23
  1669.9 319.1 reduce-scatter.29
  1993.8 403.6 reduce-scatter.21
  2401.7 403.6 reduce-scatter.25
  2808.1 8.8 reduce-scatter.33
  2819.2 28.2 reduce-scatter.41
  2849.6 47.7 reduce-scatter.37
  2899.6 30.6 reduce-scatter.31
  2932.5 41.2 reduce-scatter.35
  2976.0 37.9 reduce-scatter.27
where the time goes:
time: 3100 us; the launch traced here: 3080 us
  waiting for transfers between devices  1820 us (59%)
  matrix products  524 us (17%)
  local copies, waits for them, and re-layouts  254 us (8%)
  blocking collectives  232 us (7%)
  other arithmetic  227 us (7%)
    reduce_scatter x1, waiting for transfers between devices, reduce_all(): lax.psum_scatter(proj_grad, 'wide', scatter_dimension=1, tiled=True)  408 us
    reduce_scatter x1, waiting for transfers between devices, reduce_all(): lax.psum_scatter(mlp_grad, 'wide', scatter_dimension=1, tiled=True)  397 us
    reduce_scatter x1, waiting for transfers between devices, reduce_all(): lax.psum_scatter(ada_grad, 'wide', scatter_dimension=0, tiled=True)  316 us
    reduce_scatter x1, waiting for transfers between devices, reduce_all(): lax.psum_scatter(qkv_grad, 'wide', scatter_dimension=1, tiled=True)  245 us
    add x7, other arithmetic, body(): left_part + right_part  158 us
    dot_general x26, matrix products, matmul_tn(): lax.dot_general(operand, matrix, (((0,), (0,)), ((), ())), preferred_elem...  149 us
    dot_general x30, matrix products, matmul(): return jnp.dot(operand, matrix, preferred_element_type=jnp.float32)  131 us
    dot_general x26, matrix products, matmul_nt(): lax.dot_general(operand, matrix, (((1,), (1,)), ((), ())), preferred_elem...  126 us
  transfers between devices with their start and end apart: 19, of which 14 were waited for; matrix products, arithmetic and copies ran while one was open for 20% of the time, Pallas kernels for 0%

commit v1 on v0

v1 whole, which is shorter than its diff:
```python
import math

import jax
import jax.numpy as jnp
from jax import lax
from jax.experimental import pallas as pl
from jax.experimental.pallas import tpu as pltpu
from jax.sharding import PartitionSpec as P

D = 1152
HEADS = 16
HEAD_DIM = 72
CAP = 4096
FREQ = 256
F = 16
S = 16
LCAP = 120


LEARNING_RATE = 0.04


def rounded(values):
    return values.astype(jnp.bfloat16)


def matmul(operand, matrix):
    return jnp.dot(operand, matrix, preferred_element_type=jnp.float32)


def matmul_tn(operand, matrix):
    return lax.dot_general(
        operand, matrix, (((0,), (0,)), ((), ())), preferred_element_type=jnp.float32
    )


def matmul_nt(operand, matrix):
    return lax.dot_general(
        operand, matrix, (((1,), (1,)), ((), ())), preferred_element_type=jnp.float32
    )


def sinusoid(places, feature):
    half_width = feature // 2
    freqs_row = jnp.exp(-math.log(10000.0) * jnp.arange(half_width, dtype=jnp.float32) / half_width)
    angles = places[:, None] * freqs_row[None, :]
    return jnp.concatenate([jnp.cos(angles), jnp.sin(angles)], axis=1)


def layer_norm(values):
    centred = values - jnp.mean(values, axis=-1, keepdims=True)
    return centred * lax.rsqrt(jnp.mean(centred * centred, axis=-1, keepdims=True) + 1e-06)


def modulate(values, shift_row, scale_row):
    return layer_norm(values) * (1.0 + scale_row) + shift_row


def head_window(head):
    first = HEAD_DIM * head
    low_lane = first // 128 * 128
    high_lane = -(-(first + HEAD_DIM) // 128) * 128
    return (first - low_lane, low_lane, high_lane)


def lanes_of_head(rows, head):
    offset, low_lane, high_lane = head_window(head)
    lane = lax.broadcasted_iota(jnp.int32, (rows, high_lane - low_lane), 1)
    return (lane >= offset) & (lane < offset + HEAD_DIM)


def dot_f32(left, right, contract):
    return lax.dot_general(
        left, right, ((contract[:1], contract[1:]), ((), ())), preferred_element_type=jnp.float32
    )


def softmax_rows(scores, allowed):
    scores = jnp.where(allowed, scores * HEAD_DIM ** (-0.5), -1000000000.0)
    powers = jnp.exp(scores - jnp.max(scores, axis=-1, keepdims=True))
    return powers * (1.0 / jnp.sum(powers, axis=-1, keepdims=True))


def put_head(ref, base, head, window, values):
    _, low_lane, high_lane = window
    spot = (slice(None), slice(base + low_lane, base + high_lane))
    kept = ref[spot]
    mine = lanes_of_head(kept.shape[0], head)
    ref[spot] = jnp.where(mine, values, kept.astype(jnp.float32)).astype(ref.dtype)


def attend_heads(query_ref, key_ref, key_base, value_ref, value_base, out_ref, allowed):
    rows = query_ref.shape[0]
    for head in range(HEADS):
        window = head_window(head)
        _, low_lane, high_lane = window
        query = query_ref[:, low_lane:high_lane]
        query = jnp.where(lanes_of_head(rows, head), query, jnp.zeros_like(query))
        key = key_ref[:, key_base + low_lane : key_base + high_lane]
        weights = softmax_rows(dot_f32(query, key, (1, 1)), allowed)
        value = value_ref[:, value_base + low_lane : value_base + high_lane]
        put_head(out_ref, 0, head, window, dot_f32(rounded(weights), value, (1, 0)))


def attend_heads_back(
    query_ref, key_ref, key_base, value_ref, value_base, grad_ref,
    grad_query_ref, grad_key_ref, grad_value_ref, allowed,
):
    rows = query_ref.shape[0]
    for head in range(HEADS):
        window = head_window(head)
        _, low_lane, high_lane = window
        mine = lanes_of_head(rows, head)
        query = query_ref[:, low_lane:high_lane]
        zero = jnp.zeros_like(query)
        key = key_ref[:, key_base + low_lane : key_base + high_lane]
        value = value_ref[:, value_base + low_lane : value_base + high_lane]
        grad = grad_ref[:, low_lane:high_lane]
        weights = softmax_rows(dot_f32(jnp.where(mine, query, zero), key, (1, 1)), allowed)
        grad_weights = dot_f32(jnp.where(mine, grad, zero), value, (1, 1))
        put_head(grad_value_ref, value_base, head, window, dot_f32(rounded(weights), grad, (0, 0)))
        grad_scores = weights * (
            grad_weights - jnp.sum(grad_weights * weights, axis=-1, keepdims=True)
        )
        grad_low = rounded(grad_scores * HEAD_DIM ** (-0.5))
        put_head(grad_query_ref, 0, head, window, dot_f32(grad_low, key, (1, 0)))
        put_head(grad_key_ref, key_base, head, window, dot_f32(grad_low, query, (0, 0)))


def same_group(rows, spatial):
    row = lax.broadcasted_iota(jnp.int32, (rows, rows), 0)
    column = lax.broadcasted_iota(jnp.int32, (rows, rows), 1)
    if spatial:
        return row // S == column // S
    return row % S == column % S


VMEM_LIMIT = pltpu.CompilerParams(vmem_limit_bytes=48 * 1024 * 1024)


def self_attend(qkv, spatial):
    rows = F * S

    def kernel(qkv_ref, out_ref):
        out_ref[...] = jnp.zeros_like(out_ref)
        attend_heads(qkv_ref, qkv_ref, D, qkv_ref, 2 * D, out_ref, same_group(rows, spatial))

    return pl.pallas_call(
        kernel,
        grid=(qkv.shape[0] // rows,),
        in_specs=[pl.BlockSpec((rows, 3 * D), lambda i: (i, 0))],
        out_specs=pl.BlockSpec((rows, D), lambda i: (i, 0)),
        out_shape=jax.ShapeDtypeStruct((qkv.shape[0], D), jnp.bfloat16),
        compiler_params=VMEM_LIMIT,
        name="self_attend",
    )(qkv)


def self_attend_back(qkv, grad_mix, spatial):
    rows = F * S

    def kernel(qkv_ref, grad_ref, out_ref):
        out_ref[...] = jnp.zeros_like(out_ref)
        attend_heads_back(
            qkv_ref, qkv_ref, D, qkv_ref, 2 * D, grad_ref,
            out_ref, out_ref, out_ref, same_group(rows, spatial),
        )

    return pl.pallas_call(
        kernel,
        grid=(qkv.shape[0] // rows,),
        in_specs=[
            pl.BlockSpec((rows, 3 * D), lambda i: (i, 0)),
            pl.BlockSpec((rows, D), lambda i: (i, 0)),
        ],
        out_specs=pl.BlockSpec((rows, 3 * D), lambda i: (i, 0)),
        out_shape=jax.ShapeDtypeStruct(qkv.shape, jnp.bfloat16),
        compiler_params=VMEM_LIMIT,
        name="self_attend_back",
    )(qkv, grad_mix)


def caption_mask(length):
    return lax.broadcasted_iota(jnp.int32, (F * S, LCAP), 1) < length


def cross_attend(query, pairs, lengths):
    clips = pairs.shape[0]

    def kernel(length_ref, query_ref, pair_ref, out_ref):
        out_ref[...] = jnp.zeros_like(out_ref)
        allowed = caption_mask(length_ref[pl.program_id(0)])
        attend_heads(query_ref, pair_ref.at[0], 0, pair_ref.at[0], D, out_ref, allowed)

    return pl.pallas_call(
        kernel,
        grid_spec=pltpu.PrefetchScalarGridSpec(
            num_scalar_prefetch=1,
            grid=(clips,),
            in_specs=[
                pl.BlockSpec((F * S, D), lambda i, lens: (i, 0)),
                pl.BlockSpec((1, LCAP, 2 * D), lambda i, lens: (i, 0, 0)),
            ],
            out_specs=pl.BlockSpec((F * S, D), lambda i, lens: (i, 0)),
        ),
        out_shape=jax.ShapeDtypeStruct(query.shape, jnp.bfloat16),
        compiler_params=VMEM_LIMIT,
        name="cross_attend",
    )(lengths, query, pairs)


def cross_attend_back(query, pairs, grad_mix, lengths):
    clips = pairs.shape[0]

    def kernel(length_ref, query_ref, pair_ref, grad_ref, grad_query_ref, grad_pair_ref):
        grad_query_ref[...] = jnp.zeros_like(grad_query_ref)
        grad_pair_ref[...] = jnp.zeros_like(grad_pair_ref)
        allowed = caption_mask(length_ref[pl.program_id(0)])
        attend_heads_back(
            query_ref, pair_ref.at[0], 0, pair_ref.at[0], D, grad_ref,
            grad_query_ref, grad_pair_ref.at[0], grad_pair_ref.at[0], allowed,
        )

    return pl.pallas_call(
        kernel,
        grid_spec=pltpu.PrefetchScalarGridSpec(
            num_scalar_prefetch=1,
            grid=(clips,),
            in_specs=[
                pl.BlockSpec((F * S, D), lambda i, lens: (i, 0)),
                pl.BlockSpec((1, LCAP, 2 * D), lambda i, lens: (i, 0, 0)),
                pl.BlockSpec((F * S, D), lambda i, lens: (i, 0)),
            ],
            out_specs=[
                pl.BlockSpec((F * S, D), lambda i, lens: (i, 0)),
                pl.BlockSpec((1, LCAP, 2 * D), lambda i, lens: (i, 0, 0)),
            ],
        ),
        out_shape=[
            jax.ShapeDtypeStruct(query.shape, jnp.bfloat16),
            jax.ShapeDtypeStruct(pairs.shape, jnp.bfloat16),
        ],
        compiler_params=VMEM_LIMIT,
        name="cross_attend_back",
    )(lengths, query, pairs, grad_mix)


class Place:
    def __init__(self):
        self.wide = lax.axis_size("wide")
        self.narrow = lax.axis_size("narrow")
        self.depth = self.wide // 4
        self.half = self.depth // 2
        self.at = lax.axis_index("wide")
        self.core = self.at & 1
        self.x = (self.at >> 1) & 1
        self.z = self.at >> 2
        self.y = lax.axis_index("narrow")

    def over_wide(self, values, bit):
        return lax.ppermute(values, "wide", [(i, i ^ bit) for i in range(self.wide)])

    def over_core(self, values):
        return self.over_wide(values, 1)

    def over_x(self, values):
        return self.over_wide(values, 2)

    def over_z(self, values, bit):
        return self.over_wide(values, 4 * bit)

    def to_owner(self, values):
        pairs = [
            (i, i ^ 4 * self.half)
            for i in range(self.wide)
            if (i >> 2) // self.half != i & 1
        ]
        return lax.ppermute(values, "wide", pairs)

    def from_owner(self, values):
        pairs = [(i, i ^ 1) for i in range(self.wide) if (i >> 2) // self.half == i & 1]
        return lax.ppermute(values, "wide", pairs)

    def over_y(self, values, bit):
        return lax.ppermute(values, "narrow", [(i, i ^ bit) for i in range(self.narrow)])


def pair_up(bit, own, other):
    first = bit == 0
    return jnp.where(first, own, other), jnp.where(first, other, own)


def bits_of(size):
    return [1 << at for at in range(size.bit_length() - 1)]


def hold(values, others):
    if not others:
        return values
    kept, _ = lax.optimization_barrier((values, others))
    return kept


class Ticks:
    def __init__(self, joint):
        self.joint = joint
        self.ended = {True: [], False: []}
        self.sent = []

    def run(self, jobs, others=()):
        self.before = self.ended[True]
        ended = {True: [], False: []}
        before = dict(self.ended)
        if self.joint:
            before = {kind: list(before.values()) for kind in before}
            self.ended = {True: [], False: []}
        self.sent = []
        results = []
        for kind in (True, False):
            mine = [job for job in jobs if job.planar == kind]
            if not mine:
                continue
            values = [[value for value, _ in job.sends] for job in mine]
            values = hold(values, [before[kind], list(others)])
            self.sent.append(values)
            for job, held in zip(mine, values):
                result = [exchange(value) for value, (_, exchange) in zip(held, job.sends)]
                ended[kind].append(result)
                results.append((job, result))
            self.ended[kind] = ended[kind]
        for job, result in results:
            job.take(result)

    def during(self, values):
        return hold(values, [self.sent, self.before])

    def after(self, values):
        return hold(values, self.ended[True])


class Job:
    planar = False

    def __init__(self, transfers):
        self.transfers = transfers
        self.sends = next(transfers)

    def take(self, results):
        try:
            self.sends = self.transfers.send(results)
        except StopIteration:
            self.sends = None


def spread_y(place, values):
    pieces = [values]
    for bit in bits_of(place.narrow):
        pieces = pieces + [place.over_y(piece, bit) for piece in pieces]
    return pieces[1:]


class Gather(Job):
    def __init__(self, place, own):
        self.place = place
        super().__init__(self.plan(own[None]))

    def plan(self, block):
        place = self.place
        half = place.half
        for bit in bits_of(half):
            [other] = yield [(block, lambda values, bit=bit: place.over_z(values, bit))]
            block = jnp.concatenate(pair_up(place.z & bit, block, other))
        quarter = half // 2
        low, high = block[:quarter], block[quarter:]
        [low_away] = yield [(low, lambda values: place.over_z(values, half))]
        [high_away] = yield [(high, lambda values: place.over_z(values, half))]
        low = pair_up(place.z & half, low, low_away)
        high = pair_up(place.z & half, high, high_away)
        block = jnp.concatenate([low[0], high[0], low[1], high[1]])
        self.planar = True
        by_x, by_y = yield [(block, place.over_x), (block, lambda values: spread_y(place, values))]
        far_xy, near_xy = yield [
            (jnp.stack([piece[half:] for piece in by_y]), place.over_x),
            (by_x[:half], lambda values: spread_y(place, values)),
        ]
        columns = block.shape[-1] * place.narrow
        mine = unwritten((place.depth, 2, block.shape[1], columns))
        parts = (
            (0, 0, self.lanes([block] + list(by_y))),
            (0, 1, self.lanes([by_x[:half]] + list(near_xy))),
            (half, 1, self.lanes([by_x[half:]] + [far_xy[at] for at in range(place.narrow - 1)])),
        )
        for first_z, apart, part in parts:
            mine = lax.dynamic_update_slice(
                mine, part[:, None], (first_z, place.x ^ apart, 0, 0)
            )
        self.mine = mine
        self.planar = False
        [self.other] = yield [(mine, place.over_core)]

    def lanes(self, pieces):
        place = self.place
        if place.narrow == 1:
            return pieces[0]
        if place.narrow == 2:
            return jnp.concatenate(pair_up(place.y, pieces[0], pieces[1]), axis=-1)
        return jnp.concatenate(
            [lax.select_n(place.y ^ spot, *pieces) for spot in range(place.narrow)], axis=-1
        )

    def whole(self, first_row, rows):
        place = self.place
        span = slice(first_row, first_row + rows)
        columns = self.mine.shape[-1]
        whole = unwritten((place.depth, 2, 2, rows, columns))
        for part, core in ((self.mine, place.core), (self.other, 1 - place.core)):
            whole = lax.dynamic_update_slice(
                whole, part[:, :, None, span], (0, 0, core, 0, 0)
            )
        return whole.reshape(place.wide * rows, columns)


def unwritten(shape):
    return pl.pallas_call(
        lambda out_ref: None,
        out_specs=pl.BlockSpec(memory_space=pl.ANY),
        out_shape=jax.ShapeDtypeStruct(shape, jnp.bfloat16),
        name="unwritten",
    )()


def side(values, bit, axis):
    return lax.dynamic_index_in_dim(values, bit, axis, keepdims=False)


def columns_at(values, index, count):
    width = values.shape[-1] // count
    if count == 1:
        return values
    if count == 2:
        return jnp.where(index == 0, values[..., :width], values[..., width:])
    return lax.dynamic_slice_in_dim(values, index * width, width, axis=values.ndim - 1)


def wide_float(values):
    return values.astype(jnp.float32)


def reduce_y(place, values):
    for bit in reversed(bits_of(place.narrow)):
        upper = ((place.y & bit) != 0).astype(jnp.int32)
        away = place.over_y(rounded(columns_at(values, 1 - upper, 2)), bit)
        values = columns_at(values, upper, 2) + wide_float(away)
    return values


class Scatter(Job):
    def __init__(self, place, products):
        self.place = place
        super().__init__(self.plan(products))

    def plan(self, products):
        place = self.place
        spread = place.half
        quarter = spread // 2
        sends = []
        for operand, grad, *known in products:
            sends.append((columns_at(operand, 1 - place.core, 2), place.over_core))
            if not known:
                sends.append((grad, place.over_core))
        away = iter((yield sends))
        sums = []
        for operand, grad, *known in products:
            kept = rounded(matmul_tn(columns_at(operand, place.core, 2), grad))
            operand_away = next(away)
            grad_away = known[0] if known else next(away)
            total = matmul_tn(operand_away, grad_away) + wide_float(kept)
            sums.append(rounded(total).reshape(spread, 2, -1, grad.shape[1]))
        rows = sums[0].shape[2] // 2

        def summed(span, x_bit=None):
            mine = [view[span] for view in sums]
            if x_bit is not None:
                mine = [side(view, x_bit, 1) for view in mine]
            return jnp.stack(mine)

        near_span, far_span = slice(0, quarter), slice(quarter, None)
        self.planar = True
        if place.narrow == 2:
            near_away, far_away = yield [
                (summed(near_span, 1 - place.x), place.over_x),
                (
                    jnp.stack([columns_at(view[far_span], 1 - place.y, 2) for view in sums]),
                    lambda values: place.over_y(values, 1),
                ),
            ]

            def near(y_bit):
                mine = [columns_at(side(view[near_span], place.x, 1), y_bit, 2) for view in sums]
                return wide_float(jnp.stack(mine)) + wide_float(columns_at(near_away, y_bit, 2))

            def far(x_bit):
                mine = [columns_at(side(view[far_span], x_bit, 1), place.y, 2) for view in sums]
                return wide_float(jnp.stack(mine)) + wide_float(side(far_away, x_bit, 2))

            near_back, far_back = yield [
                (rounded(near(1 - place.y)), lambda values: place.over_y(values, 1)),
                (rounded(far(1 - place.x)), place.over_x),
            ]
            near = near(place.y) + wide_float(near_back)
            far = far(place.x) + wide_float(far_back)
        else:
            near_away, far = yield [
                (summed(near_span, 1 - place.x), place.over_x),
                (wide_float(summed(far_span)), lambda values: reduce_y(place, values)),
            ]
            near = wide_float(summed(near_span, place.x)) + wide_float(near_away)
            near, far_back = yield [
                (near, lambda values: reduce_y(place, values)),
                (rounded(side(far, 1 - place.x, 2)), place.over_x),
            ]
            far = side(far, place.x, 2) + wide_float(far_back)
        self.planar = False
        total, sent = pair_up(place.z & quarter, near, far)
        [away] = yield [(rounded(sent), lambda values: place.over_z(values, quarter))]
        total = total + wide_float(away)
        for bit in reversed(bits_of(quarter)):
            total = total.reshape((total.shape[0], 2, total.shape[1] // 2) + total.shape[2:])
            upper = ((place.z & bit) != 0).astype(jnp.int32)
            [away] = yield [
                (
                    rounded(side(total, 1 - upper, 1)),
                    lambda values, bit=bit: place.over_z(values, bit),
                )
            ]
            total = side(total, upper, 1) + wide_float(away)
        total = total[:, 0]
        [away] = yield [(rounded(total), place.to_owner)]
        total = total + wide_float(away)
        total = total.reshape(total.shape[0], 2, rows, -1)
        [away] = yield [(side(total, 1 - place.core, 1), place.from_owner)]
        owner = place.z // spread == place.core
        self.total = jnp.where(owner, side(total, place.core, 1), away)


class Reducer:
    def __init__(self, place):
        self.place = place
        self.ticks = Ticks(False)
        self.jobs = []

    def add(self, *products):
        job = Scatter(self.place, products)
        self.jobs.append(job)
        return job

    def run(self, *waiting):
        due = [job for job in self.jobs if job.sends is not None and job not in waiting]
        if due:
            self.ticks.run(due)
        return bool(due)


def all_bits(place):
    pairs = [
        (place.y & bit, lambda values, bit=bit: place.over_y(values, bit))
        for bit in bits_of(place.narrow)
    ]
    return pairs + wide_bits(place)


def wide_bits(place):
    return [
        (place.at & bit, lambda values, bit=bit: place.over_wide(values, bit))
        for bit in bits_of(place.wide)
    ]


def sum_everywhere(place, values):
    for _, exchange in all_bits(place):
        values = values + exchange(values)
    return values


def adam_update(master, first_moment, second_moment, gradient, step_value):
    first_new = 0.9 * first_moment + 0.1 * gradient
    second_new = 0.999 * second_moment + 0.001 * gradient * gradient
    first_hat = first_new / (1.0 - 0.9**step_value)
    second_hat = second_new / (1.0 - 0.999**step_value)
    master_new = master - LEARNING_RATE * (
        first_hat / (jnp.sqrt(second_hat) + 1e-08) + 0.01 * master
    )
    return (master_new, first_new, second_new)


def body(
    projections,
    qkv_weights,
    mlp_weights,
    ada_weights,
    entry_weights,
    patch_weights,
    shift_tables,
    first_projections,
    first_qkv_weights,
    first_mlp_weights,
    first_ada_weights,
    first_entry_weights,
    first_patch_weights,
    first_shift_tables,
    second_projections,
    second_qkv_weights,
    second_mlp_weights,
    second_ada_weights,
    second_entry_weights,
    second_patch_weights,
    second_shift_tables,
    latents,
    noise,
    captions,
    cap_len,
    timesteps,
    step_count,
):
    shards = (
        projections,
        qkv_weights,
        mlp_weights,
        ada_weights,
        entry_weights,
        patch_weights,
        shift_tables,
    )
    firsts = (
        first_projections,
        first_qkv_weights,
        first_mlp_weights,
        first_ada_weights,
        first_entry_weights,
        first_patch_weights,
        first_shift_tables,
    )
    seconds = (
        second_projections,
        second_qkv_weights,
        second_mlp_weights,
        second_ada_weights,
        second_entry_weights,
        second_patch_weights,
        second_shift_tables,
    )
    place = Place()
    clips = latents.shape[0]
    tokens = F * S
    video_count = clips * place.wide * place.narrow
    rows = projections.shape[1]
    entry_rows = entry_weights.shape[0]

    def by_clip(values):
        return values.reshape(clips, tokens, values.shape[-1])

    def flat(values):
        return values.reshape(clips * tokens, values.shape[-1])

    devices = place.wide * place.narrow
    all_clips = clips * devices

    def to_all(values):
        return lax.all_to_all(values, ("wide", "narrow"), split_axis=0, concat_axis=0, tiled=True)

    def columns_to_all(values):
        pieces = values.reshape(values.shape[0], place.narrow, -1).transpose(1, 0, 2)
        pieces = jnp.broadcast_to(pieces[None], (place.wide,) + pieces.shape)
        return to_all(pieces.reshape((devices,) + pieces.shape[2:]))

    proj_low, qkv_low, mlp_low, ada_low, entry_low, patch_low, table_low = (
        rounded(shard) for shard in shards
    )
    width = projections.shape[2]
    small = jnp.concatenate([patch_low.reshape(-1), table_low.reshape(-1)])
    small_rows = -(-small.shape[0] // (8 * width)) * 8
    small = jnp.pad(small, (0, small_rows * width - small.shape[0])).reshape(small_rows, width)
    ticks = Ticks(True)
    gathers = [
        Gather(place, own)
        for own in (
            jnp.concatenate([proj_low[:2].reshape(2 * rows, width), small]),
            entry_low,
            qkv_low.reshape(2 * rows, -1),
            proj_low[2:].reshape(6 * rows, width),
            mlp_low[0],
            mlp_low[1],
        )
    ]
    early, entry_gather, qkv_gather, late, mlp_in_gather, mlp_out_gather = gathers
    rounds = iter(range(2 * len(gathers) + len(bits_of(place.depth)) + 4))

    def gather_on(*others):
        now = next(rounds)
        due = [job for at, job in enumerate(gathers) if job.sends is not None and now >= 2 * at]
        if due:
            ticks.run(due, others)

    while entry_gather.sends is not None:
        gather_on()
    gather_on()
    entry_gather.other = ticks.during(entry_gather.other)
    small_all = early.whole(2 * rows, small_rows)
    proj_all = [early.whole(0, rows), early.whole(rows, rows)]
    entry_all = entry_gather.whole(0, entry_rows)
    small_all = small_all.reshape(place.wide, small_rows, place.narrow, width).transpose(0, 2, 1, 3)
    small_all = small_all.reshape(place.wide, place.narrow, small_rows * width)
    patch_count = patch_low.size
    patch_all = small_all[:, :, :patch_count].reshape(
        (place.wide, place.narrow) + patch_low.shape
    )
    patch_all = patch_all.transpose(2, 0, 3, 1, 4).reshape(2, D, -1)
    table_all = small_all[:, :, patch_count : patch_count + table_low.size].reshape(
        (place.wide, place.narrow) + table_low.shape
    )
    table_all = table_all.transpose(1, 2, 0, 3).reshape(8, D).astype(jnp.float32)

    time_value = timesteps.astype(jnp.float32)
    signal = jnp.cos((time_value / 1000.0 + 0.008) / 1.008 * (math.pi / 2)) ** 2
    noise_rows = flat(noise.astype(jnp.float32))
    noised_low = rounded(
        flat(
            jnp.sqrt(signal)[:, None, None] * latents.astype(jnp.float32)
            + jnp.sqrt(1.0 - signal)[:, None, None] * noise.astype(jnp.float32)
        )
    )
    spatial_pos = jnp.tile(sinusoid(jnp.arange(S, dtype=jnp.float32), D), (clips * F, 1))
    frame_pos = jnp.tile(jnp.repeat(sinusoid(jnp.arange(F, dtype=jnp.float32), D), S, 0), (clips, 1))
    embed_low = rounded(sinusoid(time_value, FREQ))
    time_inner = matmul(embed_low, entry_all[CAP:])
    inner_low = rounded(jax.nn.silu(time_inner))
    time_embed = matmul(inner_low, proj_all[0])
    embed_act = rounded(jax.nn.silu(time_embed))

    def by_rows(values):
        return values.reshape(clips, place.wide, rows).transpose(1, 0, 2)

    sent = jnp.concatenate(
        [
            by_rows(embed_act),
            by_rows(inner_low),
            jnp.broadcast_to(embed_low[None], (place.wide,) + embed_low.shape),
        ],
        axis=-1,
    )
    sent = jnp.broadcast_to(sent[:, None], (place.wide, place.narrow) + sent.shape[1:])
    sent = to_all(sent.reshape((devices,) + sent.shape[2:])).reshape(all_clips, -1)
    my_embed_act, my_inner, embed_all = sent[:, :rows], sent[:, rows : 2 * rows], sent[:, 2 * rows :]
    part = to_all(matmul(my_embed_act, ada_low).reshape(devices, clips, -1))
    part = part.reshape(place.wide, place.narrow, clips, -1)
    modulations = jnp.sum(part, axis=0).transpose(1, 0, 2).reshape(clips, 6, D) + table_all[:6]
    shift_a, scale_a, gate_a, shift_m, scale_m, gate_m = (
        modulations[:, at : at + 1] for at in range(6)
    )
    final_shift = (time_embed + table_all[6])[:, None]
    final_scale = (time_embed + table_all[7])[:, None]

    gather_on(entry_all)
    caption_rows = captions.reshape(clips * LCAP, CAP)
    caption_inner = matmul(caption_rows, entry_all[:CAP])
    caption_act = rounded(jax.nn.gelu(caption_inner))
    context_low = rounded(matmul(caption_act, proj_all[1]))
    gather_on(context_low, part)
    qkv_gather.other = ticks.during(qkv_gather.other)
    qkv_all = [qkv_gather.whole(0, rows), qkv_gather.whole(rows, rows)]
    gather_on(*qkv_all)

    hidden = matmul_nt(noised_low, patch_all[0]) + spatial_pos
    normed_spatial = rounded(flat(modulate(by_clip(hidden), shift_a, scale_a)))
    spatial_qkv = rounded(matmul(normed_spatial, qkv_all[0]))
    spatial_mix = self_attend(spatial_qkv, True)
    gather_on(spatial_mix)
    late.other = ticks.during(late.other)
    proj_all = proj_all + [late.whole(at * rows, rows) for at in range(6)]
    pair_weight = jnp.concatenate([proj_all[5], proj_all[6]], axis=1)
    gather_on(*proj_all)
    cross_pairs = rounded(matmul(ticks.during(context_low), pair_weight))
    spatial_out = matmul(spatial_mix, proj_all[2])
    hidden_one = hidden + flat(gate_a * by_clip(spatial_out))
    temporal_in = rounded(hidden_one + frame_pos)
    temporal_qkv = rounded(matmul(temporal_in, qkv_all[1]))
    temporal_mix = self_attend(temporal_qkv, False)
    gather_on(cross_pairs, temporal_mix)
    mlp_in_gather.other = ticks.during(mlp_in_gather.other)
    mlp_in = mlp_in_gather.whole(0, rows)
    temporal_out = matmul(temporal_mix, proj_all[3])
    hidden_two = hidden_one + flat(gate_a * by_clip(temporal_out))
    hidden_two_low = rounded(hidden_two)
    cross_query = rounded(matmul(hidden_two_low, proj_all[4]))
    while mlp_out_gather.sends is not None:
        gather_on(cross_query, mlp_in)
    mlp_out = mlp_out_gather.whole(0, rows)
    cross_mix = cross_attend(cross_query, cross_pairs.reshape(clips, LCAP, 2 * D), cap_len)
    hidden_three = hidden_two + matmul(cross_mix, proj_all[7])
    normed_mlp = rounded(flat(modulate(by_clip(hidden_three), shift_m, scale_m)))
    expand = matmul(normed_mlp, mlp_in)
    expand_act = rounded(jax.nn.gelu(expand))
    expand_act_away = place.over_core(expand_act)
    contract = matmul_nt(expand_act, mlp_out)
    hidden_four = hidden_three + flat(gate_m * by_clip(contract))
    final_low = rounded(flat(modulate(by_clip(hidden_four), final_shift, final_scale)))
    misfit = matmul(final_low, patch_all[1]) - noise_rows
    entries = tokens * latents.shape[2]
    loss_value = jnp.sum(misfit * misfit) / (entries * video_count)

    grad_pred = rounded(2.0 * misfit / (entries * video_count))
    grad_patch_out = matmul_tn(final_low, grad_pred)
    _, pull_final = jax.vjp(modulate, by_clip(hidden_four), final_shift, final_scale)
    grad_four, grad_fshift, grad_fscale = pull_final(by_clip(matmul_nt(grad_pred, patch_all[1])))
    grad_contract = rounded(flat(grad_four * gate_m))
    grad_gate_mlp = jnp.sum(grad_four * by_clip(contract), axis=1)
    reducer = Reducer(place)
    during, after = reducer.ticks.during, reducer.ticks.after
    mlp_out_scatter = reducer.add((grad_contract, expand_act, expand_act_away))
    reducer.run()
    reducer.run()
    _, pull_gelu = jax.vjp(jax.nn.gelu, expand)
    grad_expand = rounded(pull_gelu(matmul(during(grad_contract), mlp_out))[0])
    grad_expand = after(grad_expand)
    mlp_in_scatter = reducer.add((normed_mlp, grad_expand))
    reducer.run()
    _, pull_mlp_norm = jax.vjp(modulate, by_clip(hidden_three), shift_m, scale_m)
    grad_three_part, grad_shift_mlp, grad_scale_mlp = pull_mlp_norm(
        by_clip(matmul_nt(during(grad_expand), mlp_in))
    )
    grad_three = flat(grad_four + grad_three_part)
    grad_cross_out = after(rounded(grad_three))
    grad_cross_mix = rounded(matmul_nt(during(grad_cross_out), proj_all[7]))
    grad_cross_mix = after(grad_cross_mix)
    reducer.run()
    grad_query_low, grad_pairs_low = cross_attend_back(
        cross_query, cross_pairs.reshape(clips, LCAP, 2 * D), during(grad_cross_mix), cap_len
    )
    grad_query_low, grad_pairs_low = after((grad_query_low, grad_pairs_low))
    grad_pairs_low = grad_pairs_low.reshape(clips * LCAP, 2 * D)
    reducer.run()
    grad_two = grad_three + matmul_nt(during(grad_query_low), proj_all[4])
    grad_temporal_out = rounded(flat(by_clip(grad_two) * gate_a))
    grad_gate_attn = jnp.sum(by_clip(grad_two * temporal_out), axis=1)
    grad_temporal_mix = rounded(matmul_nt(grad_temporal_out, proj_all[3]))
    grad_temporal_qkv = self_attend_back(temporal_qkv, grad_temporal_mix, False)
    grad_temporal_qkv = after(grad_temporal_qkv)
    qkv_one_scatter = reducer.add((temporal_in, grad_temporal_qkv))
    reducer.run()
    grad_one = grad_two + matmul_nt(grad_temporal_qkv, qkv_all[1])
    grad_spatial_out = rounded(flat(by_clip(grad_one) * gate_a))
    grad_gate_attn = grad_gate_attn + jnp.sum(by_clip(grad_one * spatial_out), axis=1)
    grad_spatial_mix = rounded(matmul_nt(grad_spatial_out, proj_all[2]))
    reducer.run()
    grad_spatial_qkv = self_attend_back(spatial_qkv, during(grad_spatial_mix), True)
    grad_spatial_qkv = after(grad_spatial_qkv)
    qkv_zero_scatter = reducer.add((normed_spatial, grad_spatial_qkv))
    reducer.run()
    grad_normed_spatial = after(matmul_nt(during(grad_spatial_qkv), qkv_all[0]))
    reducer.run()
    qkv_zero_started = reducer.ticks.sent
    grad_context = rounded(matmul_nt(during(grad_pairs_low), pair_weight))
    square_scatter = reducer.add(
        (spatial_mix, grad_spatial_out),
        (temporal_mix, grad_temporal_out),
        (hidden_two_low, grad_query_low),
        (cross_mix, grad_cross_out),
    )
    reducer.run()
    reducer.run()
    _, pull_caption = jax.vjp(jax.nn.gelu, caption_inner)
    grad_caption_inner = rounded(pull_caption(matmul_nt(during(grad_context), proj_all[1]))[0])
    caption_wide = jnp.pad(caption_rows, ((0, 0), (0, place.wide * entry_rows - CAP)))
    entry_scatter = reducer.add((caption_wide, grad_caption_inner))
    reducer.run()
    reducer.run()
    caption_scatter = reducer.add(
        (caption_act, grad_context),
        (context_low, grad_pairs_low[:, :D]),
        (context_low, grad_pairs_low[:, D:]),
    )
    while reducer.run():
        pass
    sum_mlp_in, sum_mlp_out = mlp_in_scatter.total[0], mlp_out_scatter.total[0]
    sum_qkv_one = qkv_one_scatter.total[0]
    sum_qkv_zero = qkv_zero_scatter.total[0]
    sum_two, sum_three, sum_four, sum_seven = square_scatter.total
    sum_one, sum_five, sum_six = caption_scatter.total
    sum_entry = entry_scatter.total[0]
    _, pull_spatial_norm = jax.vjp(modulate, by_clip(hidden), shift_a, scale_a)
    grad_hidden_part, grad_shift_attn, grad_scale_attn = pull_spatial_norm(
        by_clip(grad_normed_spatial)
    )
    grad_hidden = rounded(grad_one + flat(grad_hidden_part))
    grad_patch_in = matmul_tn(grad_hidden, noised_low)
    grad_modulations = jnp.stack(
        [
            grad_shift_attn[:, 0],
            grad_scale_attn[:, 0],
            grad_gate_attn,
            grad_shift_mlp[:, 0],
            grad_scale_mlp[:, 0],
            grad_gate_mlp,
        ],
        axis=1,
    )

    grad_ada_out = hold(rounded(grad_modulations.reshape(clips, 6 * D)), qkv_zero_started)
    grad_ada_mine = columns_to_all(grad_ada_out).reshape(all_clips, -1)
    grad_ada = matmul_tn(my_embed_act, grad_ada_mine)
    act_part = to_all(matmul_nt(grad_ada_mine, ada_low).reshape(devices, clips, rows))
    act_part = jnp.sum(act_part.reshape(place.wide, place.narrow, clips, rows), axis=1)
    grad_embed_act = act_part.transpose(1, 0, 2).reshape(clips, D)
    _, pull_embed = jax.vjp(jax.nn.silu, time_embed)
    grad_time_embed = rounded(
        pull_embed(grad_embed_act)[0] + (grad_fshift + grad_fscale)[:, 0]
    )
    _, pull_inner = jax.vjp(jax.nn.silu, time_inner)
    grad_time_inner = rounded(pull_inner(matmul_nt(grad_time_embed, proj_all[0]))[0])
    time_rows = columns_to_all(jnp.concatenate([grad_time_embed, grad_time_inner]))
    grad_embed_mine = time_rows[:, :clips].reshape(all_clips, width)
    grad_inner_mine = time_rows[:, clips:].reshape(all_clips, width)
    grad_proj_zero = matmul_tn(my_inner, grad_embed_mine)
    grad_time_rows = matmul_tn(embed_all, grad_inner_mine)
    spot = jnp.clip((place.at + 1) * entry_rows - CAP, 0, FREQ + entry_rows)
    padded_rows = jnp.pad(grad_time_rows, ((entry_rows, entry_rows), (0, 0)))
    grad_entry_time = lax.dynamic_slice_in_dim(padded_rows, spot, entry_rows, axis=0)

    grad_tables = jnp.concatenate(
        [
            jnp.sum(grad_modulations, axis=0),
            jnp.sum(grad_fshift, axis=0),
            jnp.sum(grad_fscale, axis=0),
        ]
    )
    grad_patches = jnp.stack([grad_patch_in, grad_patch_out]).reshape(
        2, place.wide, rows, place.narrow, -1
    )
    grad_tables = grad_tables.reshape(place.narrow, -1, place.wide, rows)
    small_grads = jnp.concatenate(
        [
            grad_patches.transpose(1, 3, 0, 2, 4).reshape(devices, -1),
            grad_tables.transpose(2, 0, 1, 3).reshape(devices, -1),
        ],
        axis=1,
    )
    small_grads = jnp.sum(to_all(small_grads), axis=0)
    sum_patch = small_grads[: patch_weights.size].reshape(patch_weights.shape)
    sum_tables = small_grads[patch_weights.size :].reshape(shift_tables.shape)

    sum_projections = jnp.stack(
        [
            grad_proj_zero,
            sum_one,
            sum_two,
            sum_three,
            sum_four,
            sum_five,
            sum_six,
            sum_seven,
        ]
    )
    summed = (
        sum_projections,
        jnp.stack([sum_qkv_zero, sum_qkv_one]),
        jnp.stack([sum_mlp_in, sum_mlp_out]),
        grad_ada,
        sum_entry + grad_entry_time,
        sum_patch,
        sum_tables,
    )
    square_part = sum((jnp.sum(piece * piece) for piece in summed))
    both = jnp.stack([loss_value, square_part])[:, None] * jnp.ones((1, 128), jnp.float32)
    both = sum_everywhere(place, both)
    loss_total, square_total = both[0, 0], both[1, 0]
    grad_norm = jnp.sqrt(square_total)
    threshold = (video_count * latents.shape[1]) ** (-0.5)
    factor = threshold / jnp.maximum(grad_norm, threshold)
    step_value = step_count[0].astype(jnp.float32)
    updated = [
        adam_update(master, first_moment, second_moment, gradient * factor, step_value)
        for master, first_moment, second_moment, gradient in zip(shards, firsts, seconds, summed)
    ]
    return (
        updated[0][0],
        updated[1][0],
        updated[2][0],
        updated[3][0],
        updated[4][0],
        updated[5][0],
        updated[6][0],
        updated[0][1],
        updated[1][1],
        updated[2][1],
        updated[3][1],
        updated[4][1],
        updated[5][1],
        updated[6][1],
        updated[0][2],
        updated[1][2],
        updated[2][2],
        updated[3][2],
        updated[4][2],
        updated[5][2],
        updated[6][2],
        loss_total,
        grad_norm,
    )


def solution(mesh):
    return jax.shard_map(
        body,
        mesh=mesh,
        in_specs=(
            P(None, "wide", "narrow"),
            P(None, "wide", "narrow"),
            P(None, "wide", "narrow"),
            P("wide", "narrow"),
            P("wide", "narrow"),
            P(None, "wide", "narrow"),
            P("narrow", "wide"),
            P(None, "wide", "narrow"),
            P(None, "wide", "narrow"),
            P(None, "wide", "narrow"),
            P("wide", "narrow"),
            P("wide", "narrow"),
            P(None, "wide", "narrow"),
            P("narrow", "wide"),
            P(None, "wide", "narrow"),
            P(None, "wide", "narrow"),
            P(None, "wide", "narrow"),
            P("wide", "narrow"),
            P("wide", "narrow"),
            P(None, "wide", "narrow"),
            P("narrow", "wide"),
            P(("wide", "narrow"), None, None),
            P(("wide", "narrow"), None, None),
            P(("wide", "narrow"), None, None),
            P(("wide", "narrow")),
            P(("wide", "narrow")),
            P(),
        ),
        out_specs=(
            P(None, "wide", "narrow"),
            P(None, "wide", "narrow"),
            P(None, "wide", "narrow"),
            P("wide", "narrow"),
            P("wide", "narrow"),
            P(None, "wide", "narrow"),
            P("narrow", "wide"),
            P(None, "wide", "narrow"),
            P(None, "wide", "narrow"),
            P(None, "wide", "narrow"),
            P("wide", "narrow"),
            P("wide", "narrow"),
            P(None, "wide", "narrow"),
            P("narrow", "wide"),
            P(None, "wide", "narrow"),
            P(None, "wide", "narrow"),
            P(None, "wide", "narrow"),
            P("wide", "narrow"),
            P("wide", "narrow"),
            P(None, "wide", "narrow"),
            P("narrow", "wide"),
            P(),
            P(),
        ),
        check_vma=False,
    )
```

time: 3100 us -> 1320 us (0.43)
  waiting for transfers between devices: 1820 us -> 455 us
  matrix products: 524 us -> 218 us
  blocking collectives: 232 us -> 0 us
  starting transfers between devices: 1.86 us -> 148 us
  Pallas kernels: 0 us -> 67.9 us
  local copies, waits for them, and re-layouts: 254 us -> 200 us
    reduce_scatter x8 -> x0, waiting for transfers between devices: 1430 us -> none  [the longest x1 408 us: reduce_all(): lax.psum_scatter(proj_grad, 'wide', scatter_dimension=1, tiled=True)]
    ppermute x0 -> x126, waiting for transfers between devices: none -> 446 us  [the longest x85 267 us: over_wide(): lax.ppermute(values, 'wide', [(i, i ^ bit) for i in range(self.wide)])]
    all_gather x7 -> x0, waiting for transfers between devices: 331 us -> none  [the longest x1 108 us: gather_all(): lax.all_gather(ada_cols, 'wide', axis=0, tiled=True)]
    add x17 -> x16, other arithmetic: 160 us -> 2.29 us  [the longest x7 2.09 us: plan(): total = total + wide_float(away)]
    all_gather x7 -> x0, blocking collectives: 128 us -> none  [the longest x1 36.3 us: gather_all(): lax.all_gather(qkv_low, 'narrow', axis=2, tiled=True)]
    ppermute x0 -> x126, starting transfers between devices: none -> 125 us  [the longest x85 73.3 us: over_wide(): lax.ppermute(values, 'wide', [(i, i ^ bit) for i in range(self.wide)])]
    dot_general x36 -> x0, matrix products: 118 us -> none  [the longest x6 34.4 us: attend_backward(): jnp.einsum('bhnm,bmhd->bnhd', grad_low, key_heads, preferred_element_type...]
    dot_general x26 -> x29, matrix products: 149 us -> 79.9 us  [matmul_tn(): lax.dot_general(operand, matrix, (((0,), (0,)), ((), ())), preferred_elem...]
  transfers between devices with their start and end apart: 19 -> 132, of which waited for: 14 -> 53; matrix products, arithmetic and copies ran while one was open for 20% -> 40% of each run, Pallas kernels for 0% -> 5%
where the time goes in v1:
time: 1320 us; the launch traced here: 1310 us
  waiting for transfers between devices  455 us (34%)
  matrix products  218 us (17%)
  other arithmetic  208 us (16%)
  local copies, waits for them, and re-layouts  200 us (15%)
  starting transfers between devices  148 us (11%)
  Pallas kernels  67.9 us (5%)
  between operations  13.3 us (1%)
    ppermute x85, waiting for transfers between devices, over_wide(): lax.ppermute(values, 'wide', [(i, i ^ bit) for i in range(self.wide)])  267 us
    ppermute x27, waiting for transfers between devices, over_y(): lax.ppermute(values, 'narrow', [(i, i ^ bit) for i in range(self.narrow)])  129 us
    dot_general x29, matrix products, matmul_tn(): lax.dot_general(operand, matrix, (((0,), (0,)), ((), ())), preferred_elem...  79.9 us
    dot_general x15, matrix products, matmul(): return jnp.dot(operand, matrix, preferred_element_type=jnp.float32)  77.9 us
    ppermute x85, starting transfers between devices, over_wide(): lax.ppermute(values, 'wide', [(i, i ^ bit) for i in range(self.wide)])  73.3 us
    convert_element_type x39, other arithmetic, rounded(): return values.astype(jnp.bfloat16)  64 us
    dot_general x14, matrix products, matmul_nt(): lax.dot_general(operand, matrix, (((1,), (1,)), ((), ())), preferred_elem...  60.5 us
    ppermute x7, waiting for transfers between devices, to_owner(): return lax.ppermute(values, 'wide', pairs)  50.4 us
  transfers between devices with their start and end apart: 132, of which 53 were waited for; matrix products, arithmetic and copies ran while one was open for 40% of the time, Pallas kernels for 5%

profile of v1, /device:TPU:0, one launch (start us, length us, event | category | flops | bytes accessed | tf_op | source)
XLA Modules:
  0.0 1311.0 jit_solution(935797109441319728)
XLA Ops:
  13.6 8.3 collective-permute-done.1
  45.2 10.0 collective-permute-done.5
  72.0 9.2 collective-permute-done.10
  97.1 22.2 %collective-permute-done.12 = bf16[4,272,576]{2,1,0:T(8,128)(2,1)} collective-permute-done((bf16[4,272,576]{2,1,0:T(8,128)(2,1)}, bf16[4,272,576]{2,1,0:T(8,128)(2,1)}, u32[]{:S(2)}, u32[]{:S(2)}) %collective-permute-start.12) | collective-permute-done | bytes 1253408 | tf_op jit(solution)/shard_map/ppermute | solution.py:261
  132.6 9.4 collective-permute-done.17
  172.0 34.4 %collective-permute-done.21 = bf16[4,144,1728]{2,1,0:T(8,128)(2,1)} collective-permute-done((bf16[4,144,1728]{2,1,0:T(8,128)(2,1)}, bf16[4,144,1728]{2,1,0:T(8,128)(2,1)}, u32[]{:S(2)}, u32[]{:S(2)}) %collective-permute-start.21) | collective-permute-done | bytes 1990688 | tf_op jit(solution)/shard_map/ppermute | solution.py:261
  221.7 11.5 collective-permute-done.25
  271.0 8.2 multiply_convert_fusion.2
  305.5 36.3 %collective-permute-done.28 = bf16[4,432,576]{2,1,0:T(8,128)(2,1)} collective-permute-done((bf16[4,432,576]{2,1,0:T(8,128)(2,1)}, bf16[4,432,576]{2,1,0:T(8,128)(2,1)}, u32[]{:S(2)}, u32[]{:S(2)}) %collective-permute-start.28) | collective-permute-done | bytes 1990688 | tf_op jit(solution)/shard_map/ppermute | solution.py:285
  397.7 9.1 convolution_convert_fusion.6.qkv_ref
  419.9 14.0 %collective-permute-done.38 = bf16[1,72,2304]{2,1,0:T(8,128)(2,1)S(1)} collective-permute-done((bf16[1,72,2304]{2,1,0:T(8,128)(2,1)S(1)}, bf16[1,72,2304]{2,1,0:T(8,128)(2,1)S(1)}, u32[]{:S(2)}, u32[]{:S(2)}) %collective-permute-start.38) | collective-permute-done | bytes 331808 | tf_op jit(solution)/shard_map/ppermute | solution.py:261
  434.9 11.8 collective-permute-done.37
  492.8 28.0 %collective-permute-done.44 = bf16[4,72,2304]{2,1,0:T(8,128)(2,1)S(1)} collective-permute-done((bf16[4,72,2304]{2,1,0:T(8,128)(2,1)}, bf16[4,72,2304]{2,1,0:T(8,128)(2,1)S(1)}, u32[]{:S(2)}, u32[]{:S(2)}) %collective-permute-start.44) | collective-permute-done | bytes 1327136 | tf_op jit(solution)/shard_map/ppermute | solution.py:261
  531.1 12.3 collective-permute-done.45
  565.8 14.5 %multiply_convert_fusion = (bf16[512,4608]{1,0:T(8,128)(2,1)}, f32[512,4608]{1,0:T(8,128)}) fusion(bf16[512,1152]{1,0:T(8,128)(2,1)S(1)} %fusion.45, bf16[1152,4608]{1,0:T(8,128)(2,1)} %bitcast.1074), kind=kOutput, calls=%fused_computation.17 | convolution fusion | flops 5457051648 | bytes 25952256 | tf_op jit(solution)/shard_map/dot_general | solution.py:28
  591.1 12.8 broadcast_multiply_fusion
  651.2 14.3 %fusion.8 = bf16[512,4608]{1,0:T(8,128)(2,1)} fusion(f32[512,4608]{1,0:T(8,128)} %get-tuple-element.739, bf16[512,1152]{1,0:T(8,128)(2,1)S(1)} %bitcast.1091, bf16[1152,4608]{1,0:T(8,128)(2,1)S(1)} %bitcast.1071), kind=kOutput, calls=%fused_computation.14 | convolution fusion | flops 5483003904 | bytes 25952256 | tf_op jit(solution)/shard_map/dot_general | solution.py:28
  667.2 12.4 collective-permute-done.50
  690.5 11.4 multiply_reduce_fusion.3
  734.9 16.3 %cross_attend_back.1 = (bf16[512,1152]{1,0:T(8,128)(2,1)S(1)}, bf16[2,120,2304]{2,1,0:T(8,128)(2,1)S(1)}) custom-call(s32[2]{0:T(128)S(1)} %copy-done.11, bf16[512,1152]{1,0:T(8,128)(2,1)S(1)} %convolution_convert_fusion.18.query_ref, bf16[2,120,2304]{2,1,0:T(8,128)(2,1)S(1)} %bitcast.1035, bf16[512,1152]{1,0:T(8,128)(2,1)S(1)} %convolution_convert_fusion.17.grad_ref), custom_call_target="tpu_custom_call" | custom-call | tf_op jit(solution)/shard_map/cross_attend_back/pallas_call | solution.py:224
  776.6 18.5 %self_attend_back.2 = bf16[512,3456]{1,0:T(8,128)(2,1)S(1)} custom-call(bf16[512,3456]{1,0:T(8,128)(2,1)} %copy-done.5, bf16[512,1152]{1,0:T(8,128)(2,1)S(1)} %convolution_convert_fusion.16.grad_ref), custom_call_target="tpu_custom_call" | custom-call | tf_op jit(solution)/shard_map/self_attend_back/pallas_call | solution.py:169
  848.3 18.3 %self_attend_back.3 = bf16[512,3456]{1,0:T(8,128)(2,1)S(1)} custom-call(bf16[512,3456]{1,0:T(8,128)(2,1)} %copy-done.4, bf16[512,1152]{1,0:T(8,128)(2,1)S(1)} %copy-done.10), custom_call_target="tpu_custom_call" | custom-call | tf_op jit(solution)/shard_map/self_attend_back/pallas_call | solution.py:169
  1010.6 11.2 collective-permute-done.91
  1056.2 9.7 collective-permute-done.92
  1072.2 13.6 %collective-permute-done.94 = bf16[1,144,1728]{2,1,0:T(8,128)(2,1)S(1)} collective-permute-done((bf16[1,144,1728]{2,1,0:T(8,128)(2,1)S(1)}, bf16[1,144,1728]{2,1,0:T(8,128)(2,1)S(1)}, u32[]{:S(2)}, u32[]{:S(2)}) %collective-permute-start.94) | collective-permute-done | bytes 497696 | tf_op jit(solution)/shard_map/ppermute | solution.py:278
  1090.5 11.2 collective-permute-done.89
  1105.9 13.5 %collective-permute-done.97 = bf16[4,1,144,576]{3,2,0,1:T(8,128)(2,1)S(1)} collective-permute-done((bf16[4,1,144,576]{3,2,0,1:T(8,128)(2,1)S(1)}, bf16[4,1,144,576]{3,2,0,1:T(8,128)(2,1)S(1)}, u32[]{:S(2)}, u32[]{:S(2)}) %collective-permute-start.97) | collective-permute-done | bytes 663584 | tf_op jit(solution)/shard_map/ppermute | solution.py:261
  1133.2 21.4 %collective-permute-done.106 = bf16[1,1,2,544,576]{4,3,2,1,0:T(8,128)(2,1)S(1)} collective-permute-done((bf16[1,1,2,544,576]{4,3,2,1,0:T(8,128)(2,1)S(1)}, bf16[1,1,2,544,576]{4,3,2,1,0:T(8,128)(2,1)S(1)}, u32[]{:S(2)}, u32[]{:S(2)}) %collective-permute-start.106) | collective-permute-done | bytes 1253408 | tf_op jit(solution)/shard_map/ppermute | solution.py:285
  1159.4 13.7 %collective-permute-done.107 = bf16[1,1,544,576]{3,2,1,0:T(8,128)(2,1)S(1)} collective-permute-done((bf16[1,1,544,576]{3,2,1,0:T(8,128)(2,1)S(1)}, bf16[1,1,544,576]{3,2,1,0:T(8,128)(2,1)S(1)}, u32[]{:S(2)}, u32[]{:S(2)}) %collective-permute-start.107) | collective-permute-done | bytes 626720 | tf_op jit(solution)/shard_map/ppermute | solution.py:285
  1182.0 9.9 collective-permute-done.114
  1205.4 9.7 collective-permute-done.116
  1230.8 16.0 %collective-permute-done.119 = bf16[3,144,576]{2,1,0:T(8,128)(2,1)S(1)} collective-permute-done((bf16[3,144,576]{2,1,0:T(8,128)(2,1)S(1)}, bf16[3,144,576]{2,1,0:T(8,128)(2,1)S(1)}, u32[]{:S(2)}, u32[]{:S(2)}) %collective-permute-start.119) | collective-permute-done | bytes 497696 | tf_op jit(solution)/shard_map/ppermute | solution.py:278
  (1301 shorter events, 824.7 us)
Async XLA Ops:
  82.2 39.4 %collective-permute-start.13 = (bf16[4,2,152,1152]{3,2,1,0:T(8,128)(2,1)S(1)}, bf16[4,2,152,1152]{3,2,1,0:T(8,128)(2,1)}, u32[]{:S(2)}, u32[]{:S(2)}) collective-permute-start(bf16[4,2,152,1152]{3,2,1,0:T(8,128)(2,1)S(1)} %fusion.118), channel_id=1, source_target_pairs={{0,2},{2,0},{4,6},{6,4},{8,10},{10,8},{12,14},{14,12},{16,18},{18,... | collective-permute-start | bytes 8405000 | tf_op jit(solution)/shard_map/ppermute | solution.py:261
  85.4 35.1 %collective-permute-start.11 = (bf16[4,272,576]{2,1,0:T(8,128)(2,1)}, bf16[4,272,576]{2,1,0:T(8,128)(2,1)}, u32[]{:S(2)}, u32[]{:S(2)}) collective-permute-start(bf16[4,272,576]{2,1,0:T(8,128)(2,1)} %pad_maximum_fusion.8), channel_id=1, source_target_pairs={{0,1},{1,0},{2,3},{3,2},{4,5},{5,4},{6,7},{7,6},{8,9},{9,8},{10,11... | collective-permute-start | bytes 3760136 | tf_op jit(solution)/shard_map/ppermute | solution.py:285
  154.2 60.1 %collective-permute-start.19 = (bf16[4,2,272,1152]{3,2,1,0:T(8,128)(2,1)}, bf16[4,2,272,1152]{3,2,1,0:T(8,128)(2,1)}, u32[]{:S(2)}, u32[]{:S(2)}) collective-permute-start(bf16[4,2,272,1152]{3,2,1,0:T(8,128)(2,1)} %fusion.86), channel_id=1, source_target_pairs={{0,2},{2,0},{4,6},{6,4},{8,10},{10,8},{12,14},{14,12},{16,18},{18,... | collective-permute-start | bytes 15040520 | tf_op jit(solution)/shard_map/ppermute | solution.py:261
  157.5 50.2 %collective-permute-start.20 = (bf16[4,144,1728]{2,1,0:T(8,128)(2,1)}, bf16[4,144,1728]{2,1,0:T(8,128)(2,1)}, u32[]{:S(2)}, u32[]{:S(2)}) collective-permute-start(bf16[4,144,1728]{2,1,0:T(8,128)(2,1)} %pad_maximum_fusion.6), channel_id=1, source_target_pairs={{0,1},{1,0},{2,3},{3,2},{4,5},{5,4},{6,7},{7,6},{8,9},{9,8},{10,11... | collective-permute-start | bytes 5971976 | tf_op jit(solution)/shard_map/ppermute | solution.py:285
  159.0 47.4 %collective-permute-start.21 = (bf16[4,144,1728]{2,1,0:T(8,128)(2,1)}, bf16[4,144,1728]{2,1,0:T(8,128)(2,1)}, u32[]{:S(2)}, u32[]{:S(2)}) collective-permute-start(bf16[4,144,1728]{2,1,0:T(8,128)(2,1)} %pad_maximum_fusion.6), channel_id=1, source_target_pairs={{0,4},{2,6},{4,0},{6,2},{8,12},{10,14},{12,8},{14,10},{16,20},{18,... | collective-permute-start | bytes 5971976 | tf_op jit(solution)/shard_map/ppermute | solution.py:261
  166.9 47.4 %collective-permute-start.22 = (bf16[1,432,576]{2,1,0:T(8,128)(2,1)S(1)}, bf16[1,432,576]{2,1,0:T(8,128)(2,1)S(1)}, u32[]{:S(2)}, u32[]{:S(2)}) collective-permute-start(bf16[1,432,576]{2,1,0:T(8,128)(2,1)S(1)} %copy-done.173), channel_id=1, source_target_pairs={{0,16},{2,18},{4,20},{6,22},{8,24},{10,26},{12,28},{14,30},{16,0},... | collective-permute-start | bytes 1493000 | tf_op jit(solution)/shard_map/ppermute | solution.py:261
  246.6 112.3 %collective-permute-start.27 = (bf16[4,2,144,3456]{3,2,1,0:T(8,128)(2,1)}, bf16[4,2,144,3456]{3,2,1,0:T(8,128)(2,1)}, u32[]{:S(2)}, u32[]{:S(2)}) collective-permute-start(bf16[4,2,144,3456]{3,2,1,0:T(8,128)(2,1)} %fusion.48), channel_id=1, source_target_pairs={{0,2},{2,0},{4,6},{6,4},{8,10},{10,8},{12,14},{14,12},{16,18},{18,... | collective-permute-start | bytes 23887880 | tf_op jit(solution)/shard_map/ppermute | solution.py:261
  282.6 59.2 %collective-permute-start.28 = (bf16[4,432,576]{2,1,0:T(8,128)(2,1)}, bf16[4,432,576]{2,1,0:T(8,128)(2,1)}, u32[]{:S(2)}, u32[]{:S(2)}) collective-permute-start(bf16[4,432,576]{2,1,0:T(8,128)(2,1)} %pad_maximum_fusion.5), channel_id=1, source_target_pairs={{0,1},{1,0},{2,3},{3,2},{4,5},{5,4},{6,7},{7,6},{8,9},{9,8},{10,11... | collective-permute-start | bytes 5971976 | tf_op jit(solution)/shard_map/ppermute | solution.py:285
  290.7 68.2 %all-to-all-start.1 = ((f32[32,2,3456]{2,1,0:T(2,128)}), f32[32,2,3456]{2,1,0:T(2,128)S(1)}, u32[]{:S(2)}, u32[]{:S(2)}) async-start(f32[32,2,3456]{2,1,0:T(2,128)} %reshape.1705), calls=%async_computation.1 | async-start | bytes 1769472 | tf_op jit(solution)/shard_map/all_to_all | solution.py:669
  295.7 59.7 %collective-permute-start.29 = (bf16[4,432,576]{2,1,0:T(8,128)(2,1)}, bf16[4,432,576]{2,1,0:T(8,128)(2,1)S(1)}, u32[]{:S(2)}, u32[]{:S(2)}) collective-permute-start(bf16[4,432,576]{2,1,0:T(8,128)(2,1)} %pad_maximum_fusion.5), channel_id=1, source_target_pairs={{0,4},{2,6},{4,0},{6,2},{8,12},{10,14},{12,8},{14,10},{16,20},{18,... | collective-permute-start | bytes 5971976 | tf_op jit(solution)/shard_map/ppermute | solution.py:261
  297.7 61.2 %collective-permute-start.30 = (bf16[1,72,2304]{2,1,0:T(8,128)(2,1)}, bf16[1,72,2304]{2,1,0:T(8,128)(2,1)}, u32[]{:S(2)}, u32[]{:S(2)}) collective-permute-start(bf16[1,72,2304]{2,1,0:T(8,128)(2,1)} %get-tuple-element.196), channel_id=1, source_target_pairs={{0,16},{2,18},{4,20},{6,22},{8,24},{10,26},{12,28},{14,30},{16,0},... | collective-permute-start | bytes 995336 | tf_op jit(solution)/shard_map/ppermute | solution.py:261
  358.9 34.1 %collective-permute-start.34 = (bf16[1,72,2304]{2,1,0:T(8,128)(2,1)}, bf16[1,72,2304]{2,1,0:T(8,128)(2,1)}, u32[]{:S(2)}, u32[]{:S(2)}) collective-permute-start(bf16[1,72,2304]{2,1,0:T(8,128)(2,1)} %get-tuple-element.199), channel_id=1, source_target_pairs={{0,16},{2,18},{4,20},{6,22},{8,24},{10,26},{12,28},{14,30},{16,0},... | collective-permute-start | bytes 995336 | tf_op jit(solution)/shard_map/ppermute | solution.py:261
  393.0 56.3 %collective-permute-start.35 = (bf16[4,2,432,1152]{3,2,1,0:T(8,128)(2,1)}, bf16[4,2,432,1152]{3,2,1,0:T(8,128)(2,1)}, u32[]{:S(2)}, u32[]{:S(2)}) collective-permute-start(bf16[4,2,432,1152]{3,2,1,0:T(8,128)(2,1)} %fusion.50), channel_id=1, source_target_pairs={{0,2},{2,0},{4,6},{6,4},{8,10},{10,8},{12,14},{14,12},{16,18},{18,... | collective-permute-start | bytes 23887880 | tf_op jit(solution)/shard_map/ppermute | solution.py:261
  450.6 34.7 %collective-permute-start.39 = (bf16[1,72,2304]{2,1,0:T(8,128)(2,1)}, bf16[1,72,2304]{2,1,0:T(8,128)(2,1)}, u32[]{:S(2)}, u32[]{:S(2)}) collective-permute-start(bf16[1,72,2304]{2,1,0:T(8,128)(2,1)} %get-tuple-element.208), channel_id=1, source_target_pairs={{0,16},{2,18},{4,20},{6,22},{8,24},{10,26},{12,28},{14,30},{16,0},... | collective-permute-start | bytes 995336 | tf_op jit(solution)/shard_map/ppermute | solution.py:261
  485.3 41.2 %collective-permute-start.42 = (bf16[4,2,72,4608]{3,2,1,0:T(8,128)(2,1)S(1)}, bf16[4,2,72,4608]{3,2,1,0:T(8,128)(2,1)}, u32[]{:S(2)}, u32[]{:S(2)}) collective-permute-start(bf16[4,2,72,4608]{3,2,1,0:T(8,128)(2,1)S(1)} %fusion.74), channel_id=1, source_target_pairs={{0,2},{2,0},{4,6},{6,4},{8,10},{10,8},{12,14},{14,12},{16,18},{18,... | collective-permute-start | bytes 15925256 | tf_op jit(solution)/shard_map/ppermute | solution.py:261
  546.1 37.9 %collective-permute-start.47 = (bf16[4,2,72,4608]{3,2,1,0:T(8,128)(2,1)}, bf16[4,2,72,4608]{3,2,1,0:T(8,128)(2,1)}, u32[]{:S(2)}, u32[]{:S(2)}) collective-permute-start(bf16[4,2,72,4608]{3,2,1,0:T(8,128)(2,1)} %fusion.76), channel_id=1, source_target_pairs={{0,2},{2,0},{4,6},{6,4},{8,10},{10,8},{12,14},{14,12},{16,18},{18,... | collective-permute-start | bytes 15925256 | tf_op jit(solution)/shard_map/ppermute | solution.py:261
  580.3 60.3 %collective-permute-start.49 = (bf16[512,4608]{1,0:T(8,128)(2,1)}, bf16[512,4608]{1,0:T(8,128)(2,1)}, u32[]{:S(2)}, u32[]{:S(2)}) collective-permute-start(bf16[512,4608]{1,0:T(8,128)(2,1)} %get-tuple-element.738), channel_id=1, source_target_pairs={{0,2},{2,0},{4,6},{6,4},{8,10},{10,8},{12,14},{14,12},{16,18},{18,... | collective-permute-start | bytes 14155784 | tf_op jit(solution)/shard_map/ppermute | solution.py:261
  680.0 43.8 %collective-permute-start.55 = (bf16[512,4608]{1,0:T(8,128)(2,1)}, bf16[512,4608]{1,0:T(8,128)(2,1)}, u32[]{:S(2)}, u32[]{:S(2)}) collective-permute-start(bf16[512,4608]{1,0:T(8,128)(2,1)} %fusion.8), channel_id=1, source_target_pairs={{0,2},{2,0},{4,6},{6,4},{8,10},{10,8},{12,14},{14,12},{16,18},{18,... | collective-permute-start | bytes 14155784 | tf_op jit(solution)/shard_map/ppermute | solution.py:261
  682.1 41.7 %collective-permute-start.54 = (bf16[512,576]{0,1:T(8,128)(2,1)}, bf16[512,576]{0,1:T(8,128)(2,1)}, u32[]{:S(2)}, u32[]{:S(2)}) collective-permute-start(bf16[512,576]{0,1:T(8,128)(2,1)} %copy.554), channel_id=1, source_target_pairs={{0,2},{2,0},{4,6},{6,4},{8,10},{10,8},{12,14},{14,12},{16,18},{18,... | collective-permute-start | bytes 1769480 | tf_op jit(solution)/shard_map/ppermute | solution.py:261
  756.9 43.6 %collective-permute-start.61 = (bf16[1,144,2304]{2,1,0:T(8,128)(2,1)}, bf16[1,144,2304]{2,1,0:T(8,128)(2,1)}, u32[]{:S(2)}, u32[]{:S(2)}) collective-permute-start(bf16[1,144,2304]{2,1,0:T(8,128)(2,1)} %get-tuple-element.239), channel_id=1, source_target_pairs={{2,18},{6,22},{10,26},{14,30},{16,0},{20,4},{24,8},{28,12},{3,19},... | collective-permute-start | bytes 1990664 | tf_op jit(solution)/shard_map/ppermute | solution.py:278
  769.3 35.8 %collective-permute-start.59 = (bf16[1,1,144,2304]{3,2,1,0:T(8,128)(2,1)}, bf16[1,1,144,2304]{3,2,1,0:T(8,128)(2,1)S(1)}, u32[]{:S(2)}, u32[]{:S(2)}) collective-permute-start(bf16[1,1,144,2304]{3,2,1,0:T(8,128)(2,1)} %fusion.80), channel_id=1, source_target_pairs={{0,1},{1,0},{2,3},{3,2},{4,5},{5,4},{6,7},{7,6},{8,9},{9,8},{10,11... | collective-permute-start | bytes 1990664 | tf_op jit(solution)/shard_map/ppermute | solution.py:285
  769.7 36.1 %collective-permute-start.60 = (bf16[1,1,144,2304]{3,2,1,0:T(8,128)(2,1)}, bf16[1,1,144,2304]{3,2,1,0:T(8,128)(2,1)S(1)}, u32[]{:S(2)}, u32[]{:S(2)}) collective-permute-start(bf16[1,1,144,2304]{3,2,1,0:T(8,128)(2,1)} %fusion.79), channel_id=1, source_target_pairs={{0,4},{2,6},{4,0},{6,2},{8,12},{10,14},{12,8},{14,10},{16,20},{18,... | collective-permute-start | bytes 1990664 | tf_op jit(solution)/shard_map/ppermute | solution.py:261
  876.8 66.8 %collective-permute-start.72 = (bf16[512,3456]{1,0:T(8,128)(2,1)S(1)}, bf16[512,3456]{1,0:T(8,128)(2,1)}, u32[]{:S(2)}, u32[]{:S(2)}) collective-permute-start(bf16[512,3456]{1,0:T(8,128)(2,1)S(1)} %self_attend_back.3), channel_id=1, source_target_pairs={{0,2},{2,0},{4,6},{6,4},{8,10},{10,8},{12,14},{14,12},{16,18},{18,... | collective-permute-start | bytes 10616840 | tf_op jit(solution)/shard_map/ppermute | solution.py:261
  878.9 58.5 %collective-permute-start.73 = (f32[1,72,2304]{2,1,0:T(8,128)}, f32[1,72,2304]{2,1,0:T(8,128)}, u32[]{:S(2)}, u32[]{:S(2)}) collective-permute-start(f32[1,72,2304]{2,1,0:T(8,128)} %dynamic-slice_bitcast_fusion.17), channel_id=1, source_target_pairs={{0,2},{4,6},{8,10},{12,14},{18,16},{22,20},{26,24},{30,28},{1,3},{... | collective-permute-start | bytes 1990664 | tf_op jit(solution)/shard_map/ppermute | solution.py:282
  889.9 53.7 %collective-permute-start.71 = (bf16[512,576]{0,1:T(8,128)(2,1)}, bf16[512,576]{0,1:T(8,128)(2,1)}, u32[]{:S(2)}, u32[]{:S(2)}) collective-permute-start(bf16[512,576]{0,1:T(8,128)(2,1)} %copy.556), channel_id=1, source_target_pairs={{0,2},{2,0},{4,6},{6,4},{8,10},{10,8},{12,14},{14,12},{16,18},{18,... | collective-permute-start | bytes 1769480 | tf_op jit(solution)/shard_map/ppermute | solution.py:261
  953.5 50.1 %collective-permute-start.84 = (bf16[1,1,2,144,1728]{4,3,2,1,0:T(8,128)(2,1)}, bf16[1,1,2,144,1728]{4,3,2,1,0:T(8,128)(2,1)}, u32[]{:S(2)}, u32[]{:S(2)}) collective-permute-start(bf16[1,1,2,144,1728]{4,3,2,1,0:T(8,128)(2,1)} %fusion.101), channel_id=1, source_target_pairs={{0,1},{1,0},{2,3},{3,2},{4,5},{5,4},{6,7},{7,6},{8,9},{9,8},{10,11... | collective-permute-start | bytes 2985992 | tf_op jit(solution)/shard_map/ppermute | solution.py:285
  955.0 52.6 %collective-permute-start.83 = (bf16[1,1,144,3456]{3,2,1,0:T(8,128)(2,1)}, bf16[1,1,144,3456]{3,2,1,0:T(8,128)(2,1)S(1)}, u32[]{:S(2)}, u32[]{:S(2)}) collective-permute-start(bf16[1,1,144,3456]{3,2,1,0:T(8,128)(2,1)} %get-tuple-element.258), channel_id=1, source_target_pairs={{0,4},{2,6},{4,0},{6,2},{8,12},{10,14},{12,8},{14,10},{16,20},{18,... | collective-permute-start | bytes 2985992 | tf_op jit(solution)/shard_map/ppermute | solution.py:261
  973.7 61.7 %collective-permute-start.75 = (bf16[512,576]{0,1:T(8,128)(2,1)}, bf16[512,576]{0,1:T(8,128)(2,1)}, u32[]{:S(2)}, u32[]{:S(2)}) collective-permute-start(bf16[512,576]{0,1:T(8,128)(2,1)} %copy.562), channel_id=1, source_target_pairs={{0,2},{2,0},{4,6},{6,4},{8,10},{10,8},{12,14},{14,12},{16,18},{18,... | collective-permute-start | bytes 1769480 | tf_op jit(solution)/shard_map/ppermute | solution.py:261
  973.9 61.6 %collective-permute-start.76 = (bf16[512,1152]{1,0:T(8,128)(2,1)}, bf16[512,1152]{1,0:T(8,128)(2,1)}, u32[]{:S(2)}, u32[]{:S(2)}) collective-permute-start(bf16[512,1152]{1,0:T(8,128)(2,1)} %copy-done.104), channel_id=1, source_target_pairs={{0,2},{2,0},{4,6},{6,4},{8,10},{10,8},{12,14},{14,12},{16,18},{18,... | collective-permute-start | bytes 3538952 | tf_op jit(solution)/shard_map/ppermute | solution.py:261
  976.3 62.2 %collective-permute-start.77 = (bf16[512,576]{0,1:T(8,128)(2,1)}, bf16[512,576]{0,1:T(8,128)(2,1)}, u32[]{:S(2)}, u32[]{:S(2)}) collective-permute-start(bf16[512,576]{0,1:T(8,128)(2,1)} %copy.563), channel_id=1, source_target_pairs={{0,2},{2,0},{4,6},{6,4},{8,10},{10,8},{12,14},{14,12},{16,18},{18,... | collective-permute-start | bytes 1769480 | tf_op jit(solution)/shard_map/ppermute | solution.py:261
  1048.9 37.0 %collective-permute-start.88 = (bf16[4,1,2,144,576]{4,3,2,1,0:T(8,128)(2,1)S(1)}, bf16[4,1,2,144,576]{4,3,2,1,0:T(8,128)(2,1)S(1)}, u32[]{:S(2)}, u32[]{:S(2)}) collective-permute-start(bf16[4,1,2,144,576]{4,3,2,1,0:T(8,128)(2,1)S(1)} %pad_maximum_fusion.7), channel_id=1, source_target_pairs={{0,1},{1,0},{2,3},{3,2},{4,5},{5,4},{6,7},{7,6},{8,9},{9,8},{10,11... | collective-permute-start | bytes 3981320 | tf_op jit(solution)/shard_map/ppermute | solution.py:285
  1051.0 35.1 %collective-permute-start.87 = (bf16[4,1,144,1152]{3,2,0,1:T(8,128)(2,1)S(1)}, bf16[4,1,144,1152]{3,2,0,1:T(8,128)(2,1)S(1)}, u32[]{:S(2)}, u32[]{:S(2)}) collective-permute-start(bf16[4,1,144,1152]{3,2,0,1:T(8,128)(2,1)S(1)} %pad_maximum_fusion.11), channel_id=1, source_target_pairs={{0,4},{2,6},{4,0},{6,2},{8,12},{10,14},{12,8},{14,10},{16,20},{18,... | collective-permute-start | bytes 3981320 | tf_op jit(solution)/shard_map/ppermute | solution.py:261
  (391 other events, 4968.9 us)

commit v2 on v1

--- a/solution.py
+++ b/solution.py
@@ -81,50 +81,63 @@
     return powers * (1.0 / jnp.sum(powers, axis=-1, keepdims=True))
 
 
-def put_head(ref, base, head, window, values):
-    _, low_lane, high_lane = window
-    spot = (slice(None), slice(base + low_lane, base + high_lane))
-    kept = ref[spot]
-    mine = lanes_of_head(kept.shape[0], head)
-    ref[spot] = jnp.where(mine, values, kept.astype(jnp.float32)).astype(ref.dtype)
+class HeadSums:
+    def __init__(self, ref, base):
+        self.ref = ref
+        self.base = base
+        self.tiles = {}
+
+    def add(self, head, values):
+        _, low_lane, high_lane = head_window(head)
+        for tile in range(low_lane // 128, high_lane // 128):
+            start = 128 * tile - low_lane
+            share = values[:, start : start + 128]
+            self.tiles[tile] = self.tiles[tile] + share if tile in self.tiles else share
+        done = D // 128 if head == HEADS - 1 else HEAD_DIM * (head + 1) // 128
+        for tile in [at for at in self.tiles if at < done]:
+            start = self.base + 128 * tile
+            self.ref[:, start : start + 128] = self.tiles.pop(tile).astype(self.ref.dtype)
+
+
+def head_lanes(ref, base, head):
+    _, low_lane, high_lane = head_window(head)
+    values = ref[:, base + low_lane : base + high_lane]
+    return jnp.where(lanes_of_head(values.shape[0], head), values, jnp.zeros_like(values))
 
 
 def attend_heads(query_ref, key_ref, key_base, value_ref, value_base, out_ref, allowed):
-    rows = query_ref.shape[0]
+    sums = HeadSums(out_ref, 0)
     for head in range(HEADS):
-        window = head_window(head)
-        _, low_lane, high_lane = window
-        query = query_ref[:, low_lane:high_lane]
-        query = jnp.where(lanes_of_head(rows, head), query, jnp.zeros_like(query))
+        _, low_lane, high_lane = head_window(head)
+        query = head_lanes(query_ref, 0, head)
         key = key_ref[:, key_base + low_lane : key_base + high_lane]
         weights = softmax_rows(dot_f32(query, key, (1, 1)), allowed)
-        value = value_ref[:, value_base + low_lane : value_base + high_lane]
-        put_head(out_ref, 0, head, window, dot_f32(rounded(weights), value, (1, 0)))
+        value = head_lanes(value_ref, value_base, head)
+        sums.add(head, dot_f32(rounded(weights), value, (1, 0)))
 
 
 def attend_heads_back(
     query_ref, key_ref, key_base, value_ref, value_base, grad_ref,
     grad_query_ref, grad_key_ref, grad_value_ref, allowed,
 ):
-    rows = query_ref.shape[0]
+    query_sums = HeadSums(grad_query_ref, 0)
+    key_sums = HeadSums(grad_key_ref, key_base)
+    value_sums = HeadSums(grad_value_ref, value_base)
     for head in range(HEADS):
-        window = head_window(head)
-        _, low_lane, high_lane = window
-        mine = lanes_of_head(rows, head)
-        query = query_ref[:, low_lane:high_lane]
-        zero = jnp.zeros_like(query)
-        key = key_ref[:, key_base + low_lane : key_base + high_lane]
+        _, low_lane, high_lane = head_window(head)
+        query = head_lanes(query_ref, 0, head)
+        key = head_lanes(key_ref, key_base, head)
         value = value_ref[:, value_base + low_lane : value_base + high_lane]
-        grad = grad_ref[:, low_lane:high_lane]
-        weights = softmax_rows(dot_f32(jnp.where(mine, query, zero), key, (1, 1)), allowed)
-        grad_weights = dot_f32(jnp.where(mine, grad, zero), value, (1, 1))
-        put_head(grad_value_ref, value_base, head, window, dot_f32(rounded(weights), grad, (0, 0)))
+        grad = head_lanes(grad_ref, 0, head)
+        weights = softmax_rows(dot_f32(query, key, (1, 1)), allowed)
+        grad_weights = dot_f32(grad, value, (1, 1))
+        value_sums.add(head, dot_f32(rounded(weights), grad, (0, 0)))
         grad_scores = weights * (
             grad_weights - jnp.sum(grad_weights * weights, axis=-1, keepdims=True)
         )
         grad_low = rounded(grad_scores * HEAD_DIM ** (-0.5))
-        put_head(grad_query_ref, 0, head, window, dot_f32(grad_low, key, (1, 0)))
-        put_head(grad_key_ref, key_base, head, window, dot_f32(grad_low, query, (0, 0)))
+        query_sums.add(head, dot_f32(grad_low, key, (1, 0)))
+        key_sums.add(head, dot_f32(grad_low, query, (0, 0)))
 
 
 def same_group(rows, spatial):
@@ -142,7 +155,6 @@
     rows = F * S
 
     def kernel(qkv_ref, out_ref):
-        out_ref[...] = jnp.zeros_like(out_ref)
         attend_heads(qkv_ref, qkv_ref, D, qkv_ref, 2 * D, out_ref, same_group(rows, spatial))
 
     return pl.pallas_call(
@@ -160,7 +172,6 @@
     rows = F * S
 
     def kernel(qkv_ref, grad_ref, out_ref):
-        out_ref[...] = jnp.zeros_like(out_ref)
         attend_heads_back(
             qkv_ref, qkv_ref, D, qkv_ref, 2 * D, grad_ref,
             out_ref, out_ref, out_ref, same_group(rows, spatial),
@@ -188,7 +199,6 @@
     clips = pairs.shape[0]
 
     def kernel(length_ref, query_ref, pair_ref, out_ref):
-        out_ref[...] = jnp.zeros_like(out_ref)
         allowed = caption_mask(length_ref[pl.program_id(0)])
         attend_heads(query_ref, pair_ref.at[0], 0, pair_ref.at[0], D, out_ref, allowed)
 
@@ -213,8 +223,6 @@
     clips = pairs.shape[0]
 
     def kernel(length_ref, query_ref, pair_ref, grad_ref, grad_query_ref, grad_pair_ref):
-        grad_query_ref[...] = jnp.zeros_like(grad_query_ref)
-        grad_pair_ref[...] = jnp.zeros_like(grad_pair_ref)
         allowed = caption_mask(length_ref[pl.program_id(0)])
         attend_heads_back(
             query_ref, pair_ref.at[0], 0, pair_ref.at[0], D, grad_ref,
@@ -463,26 +471,24 @@
         place = self.place
         spread = place.half
         quarter = spread // 2
-        sends = []
-        for operand, grad, *known in products:
-            sends.append((columns_at(operand, 1 - place.core, 2), place.over_core))
-            if not known:
-                sends.append((grad, place.over_core))
-        away = iter((yield sends))
-        sums = []
-        for operand, grad, *known in products:
-            kept = rounded(matmul_tn(columns_at(operand, place.core, 2), grad))
-            operand_away = next(away)
+        sends = [(grad, place.over_core) for _, _, grad, *known in products if len(known) == 1]
+        away = iter((yield sends) if sends else ())
+        views = []
+        for operand, operand_away, grad, parts, *known in products:
             grad_away = known[0] if known else next(away)
-            total = matmul_tn(operand_away, grad_away) + wide_float(kept)
-            sums.append(rounded(total).reshape(spread, 2, -1, grad.shape[1]))
-        rows = sums[0].shape[2] // 2
+            kept = matmul_tn(columns_at(operand, place.core, 2), grad)
+            total = matmul_tn(columns_at(operand_away, place.core, 2), grad_away)
+            total = rounded(total + wide_float(rounded(kept)))
+            width = grad.shape[1] // parts
+            for part in range(parts):
+                view = total[:, part * width : (part + 1) * width]
+                views.append(view.reshape(spread, 2, -1, width))
 
         def summed(span, x_bit=None):
-            mine = [view[span] for view in sums]
+            mine = [view[span] for view in views]
             if x_bit is not None:
                 mine = [side(view, x_bit, 1) for view in mine]
-            return jnp.stack(mine)
+            return jnp.concatenate(mine, axis=-2) if len(mine) > 1 else mine[0]
 
         near_span, far_span = slice(0, quarter), slice(quarter, None)
         self.planar = True
@@ -490,18 +496,18 @@
             near_away, far_away = yield [
                 (summed(near_span, 1 - place.x), place.over_x),
                 (
-                    jnp.stack([columns_at(view[far_span], 1 - place.y, 2) for view in sums]),
+                    columns_at(summed(far_span), 1 - place.y, 2),
                     lambda values: place.over_y(values, 1),
                 ),
             ]
 
             def near(y_bit):
-                mine = [columns_at(side(view[near_span], place.x, 1), y_bit, 2) for view in sums]
-                return wide_float(jnp.stack(mine)) + wide_float(columns_at(near_away, y_bit, 2))
+                mine = columns_at(summed(near_span, place.x), y_bit, 2)
+                return wide_float(mine) + wide_float(columns_at(near_away, y_bit, 2))
 
             def far(x_bit):
-                mine = [columns_at(side(view[far_span], x_bit, 1), place.y, 2) for view in sums]
-                return wide_float(jnp.stack(mine)) + wide_float(side(far_away, x_bit, 2))
+                mine = columns_at(summed(far_span, x_bit), place.y, 2)
+                return wide_float(mine) + wide_float(side(far_away, x_bit, 1))
 
             near_back, far_back = yield [
                 (rounded(near(1 - place.y)), lambda values: place.over_y(values, 1)),
@@ -517,30 +523,41 @@
             near = wide_float(summed(near_span, place.x)) + wide_float(near_away)
             near, far_back = yield [
                 (near, lambda values: reduce_y(place, values)),
-                (rounded(side(far, 1 - place.x, 2)), place.over_x),
+                (rounded(side(far, 1 - place.x, 1)), place.over_x),
             ]
-            far = side(far, place.x, 2) + wide_float(far_back)
+            far = side(far, place.x, 1) + wide_float(far_back)
         self.planar = False
         total, sent = pair_up(place.z & quarter, near, far)
         [away] = yield [(rounded(sent), lambda values: place.over_z(values, quarter))]
         total = total + wide_float(away)
         for bit in reversed(bits_of(quarter)):
-            total = total.reshape((total.shape[0], 2, total.shape[1] // 2) + total.shape[2:])
+            total = total.reshape((2, total.shape[0] // 2) + total.shape[1:])
             upper = ((place.z & bit) != 0).astype(jnp.int32)
             [away] = yield [
                 (
-                    rounded(side(total, 1 - upper, 1)),
+                    rounded(side(total, 1 - upper, 0)),
                     lambda values, bit=bit: place.over_z(values, bit),
                 )
             ]
-            total = side(total, upper, 1) + wide_float(away)
-        total = total[:, 0]
+            total = side(total, upper, 0) + wide_float(away)
+        total = total[0]
         [away] = yield [(rounded(total), place.to_owner)]
         total = total + wide_float(away)
-        total = total.reshape(total.shape[0], 2, rows, -1)
-        [away] = yield [(side(total, 1 - place.core, 1), place.from_owner)]
+        pieces, first = [], 0
+        for view in views:
+            rows = view.shape[2]
+            pieces.append(total[first : first + rows].reshape(2, rows // 2, -1))
+            first += rows
+        sent = [side(piece, 1 - place.core, 0) for piece in pieces]
+        sent = jnp.concatenate(sent) if len(sent) > 1 else sent[0]
+        [away] = yield [(sent, place.from_owner)]
         owner = place.z // spread == place.core
-        self.total = jnp.where(owner, side(total, place.core, 1), away)
+        self.total, first = [], 0
+        for piece in pieces:
+            rows = piece.shape[1]
+            theirs = away[first : first + rows]
+            self.total.append(jnp.where(owner, side(piece, place.core, 0), theirs))
+            first += rows
 
 
 class Reducer:
@@ -554,32 +571,11 @@
         self.jobs.append(job)
         return job
 
-    def run(self, *waiting):
-        due = [job for job in self.jobs if job.sends is not None and job not in waiting]
+    def run(self, *others, wait=()):
+        due = [job for job in self.jobs if job.sends is not None and job not in wait]
         if due:
-            self.ticks.run(due)
+            self.ticks.run(due, others)
         return bool(due)
-
-
-def all_bits(place):
-    pairs = [
-        (place.y & bit, lambda values, bit=bit: place.over_y(values, bit))
-        for bit in bits_of(place.narrow)
-    ]
-    return pairs + wide_bits(place)
-
-
-def wide_bits(place):
-    return [
-        (place.at & bit, lambda values, bit=bit: place.over_wide(values, bit))
-        for bit in bits_of(place.wide)
-    ]
-
-
-def sum_everywhere(place, values):
-    for _, exchange in all_bits(place):
-        values = values + exchange(values)
-    return values
 
 
 def adam_update(master, first_moment, second_moment, gradient, step_value):
@@ -701,13 +697,10 @@
         if due:
             ticks.run(due, others)
 
-    while entry_gather.sends is not None:
+    while early.sends is not None:
         gather_on()
-    gather_on()
-    entry_gather.other = ticks.during(entry_gather.other)
     small_all = early.whole(2 * rows, small_rows)
     proj_all = [early.whole(0, rows), early.whole(rows, rows)]
-    entry_all = entry_gather.whole(0, entry_rows)
     small_all = small_all.reshape(place.wide, small_rows, place.narrow, width).transpose(0, 2, 1, 3)
     small_all = small_all.reshape(place.wide, place.narrow, small_rows * width)
     patch_count = patch_low.size
@@ -732,6 +725,11 @@
     spatial_pos = jnp.tile(sinusoid(jnp.arange(S, dtype=jnp.float32), D), (clips * F, 1))
     frame_pos = jnp.tile(jnp.repeat(sinusoid(jnp.arange(F, dtype=jnp.float32), D), S, 0), (clips, 1))
     embed_low = rounded(sinusoid(time_value, FREQ))
+    while entry_gather.sends is not None:
+        gather_on(patch_all, table_all)
+    gather_on()
+    entry_gather.other = ticks.during(entry_gather.other)
+    entry_all = entry_gather.whole(0, entry_rows)
     time_inner = matmul(embed_low, entry_all[CAP:])
     inner_low = rounded(jax.nn.silu(time_inner))
     time_embed = matmul(inner_low, proj_all[0])
@@ -749,55 +747,70 @@
         axis=-1,
     )
     sent = jnp.broadcast_to(sent[:, None], (place.wide, place.narrow) + sent.shape[1:])
+    gather_on(sent, entry_all)
+    sent = ticks.during(sent)
     sent = to_all(sent.reshape((devices,) + sent.shape[2:])).reshape(all_clips, -1)
     my_embed_act, my_inner, embed_all = sent[:, :rows], sent[:, rows : 2 * rows], sent[:, 2 * rows :]
-    part = to_all(matmul(my_embed_act, ada_low).reshape(devices, clips, -1))
-    part = part.reshape(place.wide, place.narrow, clips, -1)
-    modulations = jnp.sum(part, axis=0).transpose(1, 0, 2).reshape(clips, 6, D) + table_all[:6]
-    shift_a, scale_a, gate_a, shift_m, scale_m, gate_m = (
-        modulations[:, at : at + 1] for at in range(6)
-    )
-    final_shift = (time_embed + table_all[6])[:, None]
-    final_scale = (time_embed + table_all[7])[:, None]
-
-    gather_on(entry_all)
+    part = matmul(my_embed_act, ada_low).reshape(devices, clips, -1)
+
     caption_rows = captions.reshape(clips * LCAP, CAP)
-    caption_inner = matmul(caption_rows, entry_all[:CAP])
+    caption_wide = jnp.pad(caption_rows, ((0, 0), (0, place.wide * entry_rows - CAP)))
+    caption_inner = matmul(ticks.during(caption_rows), entry_all[:CAP])
     caption_act = rounded(jax.nn.gelu(caption_inner))
     context_low = rounded(matmul(caption_act, proj_all[1]))
     gather_on(context_low, part)
+    part = to_all(ticks.during(part))
     qkv_gather.other = ticks.during(qkv_gather.other)
     qkv_all = [qkv_gather.whole(0, rows), qkv_gather.whole(rows, rows)]
-    gather_on(*qkv_all)
+    part = part.reshape(place.wide, place.narrow, clips, -1)
+    modulations = jnp.sum(part, axis=0).transpose(1, 0, 2).reshape(clips, 6, D) + table_all[:6]
+    caption_wide_away = place.over_core(caption_wide)
+    caption_act_away = place.over_core(caption_act)
+    context_low_away = place.over_core(context_low)
+    gather_on(modulations, caption_wide_away, caption_act_away, context_low_away, *qkv_all)
+    modulations = ticks.during(modulations)
+    shift_a, scale_a, gate_a, shift_m, scale_m, gate_m = (
+        modulations[:, at : at + 1] for at in range(6)
+    )
+    final_shift = (time_embed + table_all[6])[:, None]
+    final_scale = (time_embed + table_all[7])[:, None]
 
     hidden = matmul_nt(noised_low, patch_all[0]) + spatial_pos
     normed_spatial = rounded(flat(modulate(by_clip(hidden), shift_a, scale_a)))
     spatial_qkv = rounded(matmul(normed_spatial, qkv_all[0]))
-    spatial_mix = self_attend(spatial_qkv, True)
-    gather_on(spatial_mix)
+    normed_spatial_away = place.over_core(normed_spatial)
+    gather_on(spatial_qkv, normed_spatial_away)
     late.other = ticks.during(late.other)
     proj_all = proj_all + [late.whole(at * rows, rows) for at in range(6)]
     pair_weight = jnp.concatenate([proj_all[5], proj_all[6]], axis=1)
-    gather_on(*proj_all)
-    cross_pairs = rounded(matmul(ticks.during(context_low), pair_weight))
+    spatial_mix = self_attend(ticks.during(spatial_qkv), True)
+    gather_on(spatial_mix, pair_weight, *proj_all)
+    spatial_mix, context_low = ticks.during((spatial_mix, context_low))
+    cross_pairs = rounded(matmul(context_low, pair_weight))
     spatial_out = matmul(spatial_mix, proj_all[2])
     hidden_one = hidden + flat(gate_a * by_clip(spatial_out))
     temporal_in = rounded(hidden_one + frame_pos)
     temporal_qkv = rounded(matmul(temporal_in, qkv_all[1]))
-    temporal_mix = self_attend(temporal_qkv, False)
-    gather_on(cross_pairs, temporal_mix)
+    spatial_mix_away = place.over_core(spatial_mix)
+    temporal_in_away = place.over_core(temporal_in)
+    gather_on(cross_pairs, temporal_qkv, spatial_mix_away, temporal_in_away)
+    temporal_mix = self_attend(ticks.during(temporal_qkv), False)
     mlp_in_gather.other = ticks.during(mlp_in_gather.other)
     mlp_in = mlp_in_gather.whole(0, rows)
     temporal_out = matmul(temporal_mix, proj_all[3])
     hidden_two = hidden_one + flat(gate_a * by_clip(temporal_out))
     hidden_two_low = rounded(hidden_two)
+    temporal_mix_away = place.over_core(temporal_mix)
+    hidden_two_low_away = place.over_core(hidden_two_low)
     cross_query = rounded(matmul(hidden_two_low, proj_all[4]))
     while mlp_out_gather.sends is not None:
         gather_on(cross_query, mlp_in)
     mlp_out = mlp_out_gather.whole(0, rows)
     cross_mix = cross_attend(cross_query, cross_pairs.reshape(clips, LCAP, 2 * D), cap_len)
+    cross_mix_away = place.over_core(cross_mix)
     hidden_three = hidden_two + matmul(cross_mix, proj_all[7])
     normed_mlp = rounded(flat(modulate(by_clip(hidden_three), shift_m, scale_m)))
+    normed_mlp_away = place.over_core(normed_mlp)
     expand = matmul(normed_mlp, mlp_in)
     expand_act = rounded(jax.nn.gelu(expand))
     expand_act_away = place.over_core(expand_act)
@@ -816,69 +829,68 @@
     grad_gate_mlp = jnp.sum(grad_four * by_clip(contract), axis=1)
     reducer = Reducer(place)
     during, after = reducer.ticks.during, reducer.ticks.after
-    mlp_out_scatter = reducer.add((grad_contract, expand_act, expand_act_away))
-    reducer.run()
+    grad_contract_away = place.over_core(grad_contract)
+    mlp_out_scatter = reducer.add(
+        (grad_contract, grad_contract_away, expand_act, 1, expand_act_away)
+    )
     reducer.run()
     _, pull_gelu = jax.vjp(jax.nn.gelu, expand)
     grad_expand = rounded(pull_gelu(matmul(during(grad_contract), mlp_out))[0])
-    grad_expand = after(grad_expand)
-    mlp_in_scatter = reducer.add((normed_mlp, grad_expand))
+    mlp_in_scatter = reducer.add((normed_mlp, normed_mlp_away, grad_expand, 1))
     reducer.run()
     _, pull_mlp_norm = jax.vjp(modulate, by_clip(hidden_three), shift_m, scale_m)
     grad_three_part, grad_shift_mlp, grad_scale_mlp = pull_mlp_norm(
         by_clip(matmul_nt(during(grad_expand), mlp_in))
     )
     grad_three = flat(grad_four + grad_three_part)
-    grad_cross_out = after(rounded(grad_three))
+    grad_cross_out = rounded(grad_three)
+    reducer.run(grad_cross_out)
     grad_cross_mix = rounded(matmul_nt(during(grad_cross_out), proj_all[7]))
-    grad_cross_mix = after(grad_cross_mix)
-    reducer.run()
     grad_query_low, grad_pairs_low = cross_attend_back(
-        cross_query, cross_pairs.reshape(clips, LCAP, 2 * D), during(grad_cross_mix), cap_len
-    )
-    grad_query_low, grad_pairs_low = after((grad_query_low, grad_pairs_low))
+        cross_query, cross_pairs.reshape(clips, LCAP, 2 * D), grad_cross_mix, cap_len
+    )
     grad_pairs_low = grad_pairs_low.reshape(clips * LCAP, 2 * D)
-    reducer.run()
-    grad_two = grad_three + matmul_nt(during(grad_query_low), proj_all[4])
+    grad_context = rounded(matmul_nt(grad_pairs_low, pair_weight))
+    caption_scatter = reducer.add(
+        (caption_act, caption_act_away, grad_context, 1),
+        (context_low, context_low_away, grad_pairs_low, 2),
+    )
+    reducer.run(grad_query_low)
+    _, pull_caption = jax.vjp(jax.nn.gelu, caption_inner)
+    grad_context, grad_query_low = during((grad_context, grad_query_low))
+    grad_caption_inner = rounded(pull_caption(matmul_nt(grad_context, proj_all[1]))[0])
+    grad_two = grad_three + matmul_nt(grad_query_low, proj_all[4])
     grad_temporal_out = rounded(flat(by_clip(grad_two) * gate_a))
     grad_gate_attn = jnp.sum(by_clip(grad_two * temporal_out), axis=1)
     grad_temporal_mix = rounded(matmul_nt(grad_temporal_out, proj_all[3]))
-    grad_temporal_qkv = self_attend_back(temporal_qkv, grad_temporal_mix, False)
-    grad_temporal_qkv = after(grad_temporal_qkv)
-    qkv_one_scatter = reducer.add((temporal_in, grad_temporal_qkv))
+    reducer.run(grad_temporal_mix, grad_caption_inner)
+    grad_temporal_qkv = self_attend_back(temporal_qkv, during(grad_temporal_mix), False)
+    entry_scatter = reducer.add((caption_wide, caption_wide_away, grad_caption_inner, 1))
+    qkv_one_scatter = reducer.add((temporal_in, temporal_in_away, grad_temporal_qkv, 1))
     reducer.run()
-    grad_one = grad_two + matmul_nt(grad_temporal_qkv, qkv_all[1])
+    grad_one = grad_two + matmul_nt(during(grad_temporal_qkv), qkv_all[1])
     grad_spatial_out = rounded(flat(by_clip(grad_one) * gate_a))
     grad_gate_attn = grad_gate_attn + jnp.sum(by_clip(grad_one * spatial_out), axis=1)
     grad_spatial_mix = rounded(matmul_nt(grad_spatial_out, proj_all[2]))
+    reducer.run(grad_spatial_mix, wait=(qkv_one_scatter,))
+    grad_spatial_qkv = self_attend_back(spatial_qkv, during(grad_spatial_mix), True)
+    qkv_zero_scatter = reducer.add((normed_spatial, normed_spatial_away, grad_spatial_qkv, 1))
+    reducer.run(wait=(qkv_one_scatter,))
+    grad_normed_spatial = matmul_nt(during(grad_spatial_qkv), qkv_all[0])
+    square_scatter = reducer.add(
+        (spatial_mix, spatial_mix_away, grad_spatial_out, 1),
+        (temporal_mix, temporal_mix_away, grad_temporal_out, 1),
+        (hidden_two_low, hidden_two_low_away, grad_query_low, 1),
+        (cross_mix, cross_mix_away, grad_cross_out, 1),
+    )
+    reducer.run(grad_normed_spatial, wait=(qkv_zero_scatter,))
+    grad_normed_spatial = during(grad_normed_spatial)
+    reducer.run(wait=(qkv_zero_scatter, square_scatter))
+    reducer.run(wait=(square_scatter,))
+    qkv_zero_started = reducer.ticks.sent
+    reducer.run(wait=(square_scatter,))
     reducer.run()
-    grad_spatial_qkv = self_attend_back(spatial_qkv, during(grad_spatial_mix), True)
-    grad_spatial_qkv = after(grad_spatial_qkv)
-    qkv_zero_scatter = reducer.add((normed_spatial, grad_spatial_qkv))
-    reducer.run()
-    grad_normed_spatial = after(matmul_nt(during(grad_spatial_qkv), qkv_all[0]))
-    reducer.run()
-    qkv_zero_started = reducer.ticks.sent
-    grad_context = rounded(matmul_nt(during(grad_pairs_low), pair_weight))
-    square_scatter = reducer.add(
-        (spatial_mix, grad_spatial_out),
-        (temporal_mix, grad_temporal_out),
-        (hidden_two_low, grad_query_low),
-        (cross_mix, grad_cross_out),
-    )
-    reducer.run()
-    reducer.run()
-    _, pull_caption = jax.vjp(jax.nn.gelu, caption_inner)
-    grad_caption_inner = rounded(pull_caption(matmul_nt(during(grad_context), proj_all[1]))[0])
-    caption_wide = jnp.pad(caption_rows, ((0, 0), (0, place.wide * entry_rows - CAP)))
-    entry_scatter = reducer.add((caption_wide, grad_caption_inner))
-    reducer.run()
-    reducer.run()
-    caption_scatter = reducer.add(
-        (caption_act, grad_context),
-        (context_low, grad_pairs_low[:, :D]),
-        (context_low, grad_pairs_low[:, D:]),
-    )
+    middle = reducer.ticks.sent
     while reducer.run():
         pass
     sum_mlp_in, sum_mlp_out = mlp_in_scatter.total[0], mlp_out_scatter.total[0]
@@ -908,6 +920,7 @@
     grad_ada_out = hold(rounded(grad_modulations.reshape(clips, 6 * D)), qkv_zero_started)
     grad_ada_mine = columns_to_all(grad_ada_out).reshape(all_clips, -1)
     grad_ada = matmul_tn(my_embed_act, grad_ada_mine)
+    grad_ada_mine = hold(grad_ada_mine, middle)
     act_part = to_all(matmul_nt(grad_ada_mine, ada_low).reshape(devices, clips, rows))
     act_part = jnp.sum(act_part.reshape(place.wide, place.narrow, clips, rows), axis=1)
     grad_embed_act = act_part.transpose(1, 0, 2).reshape(clips, D)
@@ -944,7 +957,7 @@
         ],
         axis=1,
     )
-    small_grads = jnp.sum(to_all(small_grads), axis=0)
+    small_grads = jnp.sum(to_all(hold(small_grads, middle)), axis=0)
     sum_patch = small_grads[: patch_weights.size].reshape(patch_weights.shape)
     sum_tables = small_grads[patch_weights.size :].reshape(shift_tables.shape)
 
@@ -970,9 +983,8 @@
         sum_tables,
     )
     square_part = sum((jnp.sum(piece * piece) for piece in summed))
-    both = jnp.stack([loss_value, square_part])[:, None] * jnp.ones((1, 128), jnp.float32)
-    both = sum_everywhere(place, both)
-    loss_total, square_total = both[0, 0], both[1, 0]
+    both = jnp.broadcast_to(jnp.stack([loss_value, square_part]), (devices, 2))
+    loss_total, square_total = jnp.sum(to_all(both), axis=0)
     grad_norm = jnp.sqrt(square_total)
     threshold = (video_count * latents.shape[1]) ** (-0.5)
     factor = threshold / jnp.maximum(grad_norm, threshold)

time: 1320 us -> 1250 us (0.947)
  waiting for transfers between devices: 455 us -> 369 us
  other arithmetic: 208 us -> 235 us
  local copies, waits for them, and re-layouts: 200 us -> 175 us
    ppermute x27 -> x26, waiting for transfers between devices: 129 us -> 61.7 us  [over_y(): lax.ppermute(values, 'narrow', [(i, i ^ bit) for i in range(self.narrow)])]
    ppermute x85 -> x79, waiting for transfers between devices: 267 us -> 226 us  [over_wide(): lax.ppermute(values, 'wide', [(i, i ^ bit) for i in range(self.wide)])]
    convert_element_type x39, other arithmetic: 64 us -> 88.2 us  [rounded(): return values.astype(jnp.bfloat16)]
    all_to_all x6 -> x7, waiting for transfers between devices: 8.5 us -> 32.5 us  [to_all(): lax.all_to_all(values, ('wide', 'narrow'), split_axis=0, concat_axis=0, t...]
    optimization_barrier x8 -> x0, local copies, waits for them, and re-layouts: 17 us -> none  [hold(): kept, _ = lax.optimization_barrier((values, others))]
    select_n x30, other arithmetic: 29.5 us -> 44.9 us  [pair_up(): return (jnp.where(first, own, other), jnp.where(first, other, own))]
    dot_general x29 -> x27, matrix products: 79.9 us -> 93.8 us  [matmul_tn(): lax.dot_general(operand, matrix, (((0,), (0,)), ((), ())), preferred_elem...]
    ppermute x85 -> x79, starting transfers between devices: 73.3 us -> 80.1 us  [over_wide(): lax.ppermute(values, 'wide', [(i, i ^ bit) for i in range(self.wide)])]
  transfers between devices with their start and end apart: 132 -> 126, of which waited for: 53 -> 45; matrix products, arithmetic and copies ran while one was open for 40% -> 45% of each run, Pallas kernels for 5% -> 5%
where the time goes in v2:
time: 1250 us; the launch traced here: 1240 us
  waiting for transfers between devices  369 us (30%)
  other arithmetic  235 us (19%)
  matrix products  230 us (18%)
  local copies, waits for them, and re-layouts  175 us (14%)
  starting transfers between devices  157 us (13%)
  Pallas kernels  64.6 us (5%)
  between operations  12.7 us (1%)
    ppermute x79, waiting for transfers between devices, over_wide(): lax.ppermute(values, 'wide', [(i, i ^ bit) for i in range(self.wide)])  226 us
    dot_general x27, matrix products, matmul_tn(): lax.dot_general(operand, matrix, (((0,), (0,)), ((), ())), preferred_elem...  93.8 us
    convert_element_type x39, other arithmetic, rounded(): return values.astype(jnp.bfloat16)  88.2 us
    ppermute x79, starting transfers between devices, over_wide(): lax.ppermute(values, 'wide', [(i, i ^ bit) for i in range(self.wide)])  80.1 us
    dot_general x15, matrix products, matmul(): return jnp.dot(operand, matrix, preferred_element_type=jnp.float32)  73.2 us
    dot_general x14, matrix products, matmul_nt(): lax.dot_general(operand, matrix, (((1,), (1,)), ((), ())), preferred_elem...  63.1 us
    ppermute x26, waiting for transfers between devices, over_y(): lax.ppermute(values, 'narrow', [(i, i ^ bit) for i in range(self.narrow)])  61.7 us
    unnamed x577, local copies, waits for them, and re-layouts  51.2 us
  transfers between devices with their start and end apart: 126, of which 45 were waited for; matrix products, arithmetic and copies ran while one was open for 45% of the time, Pallas kernels for 5%

profile of v2, /device:TPU:0, one launch (start us, length us, event | category | flops | bytes accessed | tf_op | source)
XLA Modules:
  0.0 1242.7 jit_solution(11337334534552331478)
XLA Ops:
  14.9 8.3 collective-permute-done.1
  27.2 8.3 collective-permute-done.3
  45.5 13.8 %collective-permute-done.4 = bf16[1,272,576]{2,1,0:T(8,128)(2,1)S(1)} collective-permute-done((bf16[1,272,576]{2,1,0:T(8,128)(2,1)}, bf16[1,272,576]{2,1,0:T(8,128)(2,1)S(1)}, u32[]{:S(2)}, u32[]{:S(2)}) %collective-permute-start.4) | collective-permute-done | bytes 313376 | tf_op jit(solution)/shard_map/ppermute | solution.py:269
  72.5 10.0 collective-permute-done.10
  97.5 23.1 %collective-permute-done.12 = bf16[4,272,576]{2,1,0:T(8,128)(2,1)} collective-permute-done((bf16[4,272,576]{2,1,0:T(8,128)(2,1)}, bf16[4,272,576]{2,1,0:T(8,128)(2,1)}, u32[]{:S(2)}, u32[]{:S(2)}) %collective-permute-start.12) | collective-permute-done | bytes 1253408 | tf_op jit(solution)/shard_map/ppermute | solution.py:269
  142.1 10.8 collective-permute-done.17
  172.9 40.4 %collective-permute-done.21 = bf16[4,144,1728]{2,1,0:T(8,128)(2,1)S(1)} collective-permute-done((bf16[4,144,1728]{2,1,0:T(8,128)(2,1)S(1)}, bf16[4,144,1728]{2,1,0:T(8,128)(2,1)S(1)}, u32[]{:S(2)}, u32[]{:S(2)}) %collective-permute-start.21) | collective-permute-done | bytes 1990688 | tf_op jit(solution)/shard_map/ppermute | solution.py:269
  215.0 10.3 broadcast_select_fusion.3
  285.3 7.6 multiply_convert_fusion.2
  295.5 27.6 %all-to-all-done = bf16[32,2,400]{2,1,0:T(2,128)(2,1)} async-done(((bf16[32,2,400]{2,1,0:T(2,128)(2,1)}), bf16[32,2,400]{2,1,0:T(2,128)(2,1)}, u32[]{:S(2)}, u32[]{:S(2)}) %all-to-all-start) | async-done | bytes 51232 | tf_op jit(solution)/shard_map/all_to_all | solution.py:665
  357.0 16.4 %collective-permute-done.32 = bf16[1,2,432,576]{3,2,1,0:T(8,128)(2,1)} collective-permute-done((bf16[1,2,432,576]{3,2,1,0:T(8,128)(2,1)}, bf16[1,2,432,576]{3,2,1,0:T(8,128)(2,1)}, u32[]{:S(2)}, u32[]{:S(2)}) %collective-permute-start.32) | collective-permute-done | bytes 995360 | tf_op jit(solution)/shard_map/ppermute | solution.py:269
  382.9 7.8 collective-permute-done.31
  409.6 10.8 collective-permute-done.41
  420.5 12.2 collective-permute-done.39
  479.6 10.8 collective-permute-done.47
  531.6 14.7 %multiply_convert_fusion = (bf16[512,4608]{1,0:T(8,128)(2,1)}, f32[512,4608]{1,0:T(8,128)}) fusion(bf16[512,1152]{1,0:T(8,128)(2,1)S(1)} %fusion.36, bf16[1152,4608]{1,0:T(8,128)(2,1)} %bitcast.917), kind=kOutput, calls=%fused_computation.17 | convolution fusion | flops 5457051648 | bytes 25952256 | tf_op jit(solution)/shard_map/dot_general | solution.py:28
  556.7 12.7 %broadcast_multiply_fusion = (f32[2,256,1152]{2,1,0:T(8,128)S(1)}, f32[2,256,1152]{2,1,0:T(8,128)}) fusion(f32[2,1152]{1,0:T(2,128)S(1)} %copy-done.233, bf16[2,256,4608]{2,1,0:T(8,128)(2,1)} %bitcast.129, bf16[1152,4608,1]{1,0,2:T(8,128)(2,1)} %bitcast.919), kind=kOutput, calls=%fused_computation.267 | convolution fusion | flops 5436407808 | bytes 20063232 | tf_op jit(solution)/shard_map/dot_general | solution.py:38
  617.6 14.6 %fusion.8 = bf16[512,4608]{1,0:T(8,128)(2,1)} fusion(f32[512,4608]{1,0:T(8,128)} %get-tuple-element.739, bf16[512,1152]{1,0:T(8,128)(2,1)} %bitcast.146, bf16[1152,4608]{1,0:T(8,128)(2,1)S(1)} %bitcast.922), kind=kOutput, calls=%fused_computation.14 | convolution fusion | flops 5483003904 | bytes 25952256 | tf_op jit(solution)/shard_map/dot_general | solution.py:28
  633.9 7.8 convolution_convert_fusion.1
  648.4 11.4 multiply_reduce_fusion.3
  688.2 15.5 %cross_attend_back.1 = (bf16[512,1152]{1,0:T(8,128)(2,1)S(1)}, bf16[2,120,2304]{2,1,0:T(8,128)(2,1)S(1)}) custom-call(s32[2]{0:T(128)S(1)} %copy-done.6, bf16[512,1152]{1,0:T(8,128)(2,1)S(1)} %convolution_convert_fusion.17.query_ref, bf16[2,120,2304]{2,1,0:T(8,128)(2,1)S(1)} %bitcast.885, bf16[512,1152]{1,0:T(8,128)(2,1)S(1)} %convolution_convert_fusion.16.grad_ref), custom_call_target="tpu_custom_call" | custom-call | tf_op jit(solution)/shard_map/cross_attend_back/pallas_call | solution.py:232
  765.2 17.2 %self_attend_back.2 = bf16[512,3456]{1,0:T(8,128)(2,1)S(1)} custom-call(bf16[512,3456]{1,0:T(8,128)(2,1)} %copy-done.1, bf16[512,1152]{1,0:T(8,128)(2,1)S(1)} %convolution_convert_fusion.15.grad_ref), custom_call_target="tpu_custom_call" | custom-call | tf_op jit(solution)/shard_map/self_attend_back/pallas_call | solution.py:180
  806.3 7.9 fusion.33
  839.7 24.7 %collective-permute-done.80 = bf16[1,2,544,576]{3,2,1,0:T(8,128)(2,1)S(1)} collective-permute-done((bf16[1,2,544,576]{3,2,1,0:T(8,128)(2,1)S(1)}, bf16[1,2,544,576]{3,2,1,0:T(8,128)(2,1)S(1)}, u32[]{:S(2)}, u32[]{:S(2)}) %collective-permute-start.80) | collective-permute-done | bytes 1253408 | tf_op jit(solution)/shard_map/ppermute | solution.py:293
  872.7 9.0 collective-permute-done.83
  895.2 17.2 %self_attend_back.3 = bf16[512,3456]{1,0:T(8,128)(2,1)S(1)} custom-call(bf16[512,3456]{1,0:T(8,128)(2,1)} %copy-done, bf16[512,1152]{1,0:T(8,128)(2,1)S(1)} %convolution_convert_fusion.14.grad_ref), custom_call_target="tpu_custom_call" | custom-call | tf_op jit(solution)/shard_map/self_attend_back/pallas_call | solution.py:180
  924.0 7.6 fusion.234
  938.7 17.9 %collective-permute-done.88 = bf16[1,2,144,1728]{3,2,1,0:T(8,128)(2,1)S(1)} collective-permute-done((bf16[1,2,144,1728]{3,2,1,0:T(8,128)(2,1)S(1)}, bf16[1,2,144,1728]{3,2,1,0:T(8,128)(2,1)S(1)}, u32[]{:S(2)}, u32[]{:S(2)}) %collective-permute-start.88) | collective-permute-done | bytes 995360 | tf_op jit(solution)/shard_map/ppermute | solution.py:293
  961.0 9.3 collective-permute-done.89
  1041.8 12.6 %collective-permute-done.97 = bf16[544,576]{1,0:T(8,128)(2,1)S(1)} collective-permute-done((bf16[544,576]{1,0:T(8,128)(2,1)S(1)}, bf16[544,576]{1,0:T(8,128)(2,1)S(1)}, u32[]{:S(2)}, u32[]{:S(2)}) %collective-permute-start.97) | collective-permute-done | bytes 626720 | tf_op jit(solution)/shard_map/ppermute | solution.py:286
  1134.8 7.9 collective-permute-done.114
  1172.8 16.2 %collective-permute-done.117 = bf16[576,576]{1,0:T(8,128)(2,1)S(1)} collective-permute-done((bf16[576,576]{1,0:T(8,128)(2,1)}, bf16[576,576]{1,0:T(8,128)(2,1)S(1)}, u32[]{:S(2)}, u32[]{:S(2)}) %collective-permute-start.117) | collective-permute-done | bytes 663584 | tf_op jit(solution)/shard_map/ppermute | solution.py:286
  (1227 shorter events, 787.8 us)
Async XLA Ops:
  83.6 41.1 %collective-permute-start.13 = (bf16[4,2,152,1152]{3,2,1,0:T(8,128)(2,1)S(1)}, bf16[4,2,152,1152]{3,2,1,0:T(8,128)(2,1)}, u32[]{:S(2)}, u32[]{:S(2)}) collective-permute-start(bf16[4,2,152,1152]{3,2,1,0:T(8,128)(2,1)S(1)} %fusion.95), channel_id=1, source_target_pairs={{0,2},{2,0},{4,6},{6,4},{8,10},{10,8},{12,14},{14,12},{16,18},{18,... | collective-permute-start | bytes 8405000 | tf_op jit(solution)/shard_map/ppermute | solution.py:269
  93.8 35.5 %collective-permute-start.14 = (bf16[1,144,1728]{2,1,0:T(8,128)(2,1)}, bf16[1,144,1728]{2,1,0:T(8,128)(2,1)}, u32[]{:S(2)}, u32[]{:S(2)}) collective-permute-start(bf16[1,144,1728]{2,1,0:T(8,128)(2,1)} %get-tuple-element.168), channel_id=1, source_target_pairs={{0,16},{2,18},{4,20},{6,22},{8,24},{10,26},{12,28},{14,30},{16,0},... | collective-permute-start | bytes 1493000 | tf_op jit(solution)/shard_map/ppermute | solution.py:269
  164.0 65.3 %collective-permute-start.19 = (bf16[4,2,272,1152]{3,2,1,0:T(8,128)(2,1)S(1)}, bf16[4,2,272,1152]{3,2,1,0:T(8,128)(2,1)}, u32[]{:S(2)}, u32[]{:S(2)}) collective-permute-start(bf16[4,2,272,1152]{3,2,1,0:T(8,128)(2,1)S(1)} %fusion.68), channel_id=1, source_target_pairs={{0,2},{2,0},{4,6},{6,4},{8,10},{10,8},{12,14},{14,12},{16,18},{18,... | collective-permute-start | bytes 15040520 | tf_op jit(solution)/shard_map/ppermute | solution.py:269
  165.7 49.3 %collective-permute-start.20 = (bf16[4,144,1728]{2,1,0:T(8,128)(2,1)S(1)}, bf16[4,144,1728]{2,1,0:T(8,128)(2,1)S(1)}, u32[]{:S(2)}, u32[]{:S(2)}) collective-permute-start(bf16[4,144,1728]{2,1,0:T(8,128)(2,1)S(1)} %pad_maximum_fusion.3), channel_id=1, source_target_pairs={{0,1},{1,0},{2,3},{3,2},{4,5},{5,4},{6,7},{7,6},{8,9},{9,8},{10,11... | collective-permute-start | bytes 5971976 | tf_op jit(solution)/shard_map/ppermute | solution.py:293
  166.3 47.1 %collective-permute-start.21 = (bf16[4,144,1728]{2,1,0:T(8,128)(2,1)S(1)}, bf16[4,144,1728]{2,1,0:T(8,128)(2,1)S(1)}, u32[]{:S(2)}, u32[]{:S(2)}) collective-permute-start(bf16[4,144,1728]{2,1,0:T(8,128)(2,1)S(1)} %pad_maximum_fusion.3), channel_id=1, source_target_pairs={{0,4},{2,6},{4,0},{6,2},{8,12},{10,14},{12,8},{14,10},{16,20},{18,... | collective-permute-start | bytes 5971976 | tf_op jit(solution)/shard_map/ppermute | solution.py:269
  172.1 57.2 %collective-permute-start.22 = (bf16[1,432,576]{2,1,0:T(8,128)(2,1)}, bf16[1,432,576]{2,1,0:T(8,128)(2,1)}, u32[]{:S(2)}, u32[]{:S(2)}) collective-permute-start(bf16[1,432,576]{2,1,0:T(8,128)(2,1)} %get-tuple-element.176), channel_id=1, source_target_pairs={{0,16},{2,18},{4,20},{6,22},{8,24},{10,26},{12,28},{14,30},{16,0},... | collective-permute-start | bytes 1493000 | tf_op jit(solution)/shard_map/ppermute | solution.py:269
  260.1 78.7 %collective-permute-start.29 = (bf16[4,2,144,3456]{3,2,1,0:T(8,128)(2,1)}, bf16[4,2,144,3456]{3,2,1,0:T(8,128)(2,1)}, u32[]{:S(2)}, u32[]{:S(2)}) collective-permute-start(bf16[4,2,144,3456]{3,2,1,0:T(8,128)(2,1)} %fusion.39), channel_id=1, source_target_pairs={{0,2},{2,0},{4,6},{6,4},{8,10},{10,8},{12,14},{14,12},{16,18},{18,... | collective-permute-start | bytes 23887880 | tf_op jit(solution)/shard_map/ppermute | solution.py:269
  261.6 121.3 %collective-permute-start.35 = (bf16[240,4352]{1,0:T(8,128)(2,1)}, bf16[240,4352]{1,0:T(8,128)(2,1)}, u32[]{:S(2)}, u32[]{:S(2)}) collective-permute-start(bf16[240,4352]{1,0:T(8,128)(2,1)} %pad.13), channel_id=1, source_target_pairs={{0,2},{2,0},{4,6},{6,4},{8,10},{10,8},{12,14},{14,12},{16,18},{18,... | collective-permute-start | bytes 6266888 | tf_op jit(solution)/shard_map/ppermute | solution.py:269
  270.8 57.7 %collective-permute-start.27 = (bf16[4,432,576]{2,1,0:T(8,128)(2,1)}, bf16[4,432,576]{2,1,0:T(8,128)(2,1)}, u32[]{:S(2)}, u32[]{:S(2)}) collective-permute-start(bf16[4,432,576]{2,1,0:T(8,128)(2,1)} %pad_maximum_fusion.2), channel_id=1, source_target_pairs={{0,1},{1,0},{2,3},{3,2},{4,5},{5,4},{6,7},{7,6},{8,9},{9,8},{10,11... | collective-permute-start | bytes 5971976 | tf_op jit(solution)/shard_map/ppermute | solution.py:293
  272.4 61.8 %collective-permute-start.28 = (bf16[4,432,576]{2,1,0:T(8,128)(2,1)}, bf16[4,432,576]{2,1,0:T(8,128)(2,1)}, u32[]{:S(2)}, u32[]{:S(2)}) collective-permute-start(bf16[4,432,576]{2,1,0:T(8,128)(2,1)} %pad_maximum_fusion.2), channel_id=1, source_target_pairs={{0,4},{2,6},{4,0},{6,2},{8,12},{10,14},{12,8},{14,10},{16,20},{18,... | collective-permute-start | bytes 5971976 | tf_op jit(solution)/shard_map/ppermute | solution.py:269
  273.8 65.0 %collective-permute-start.30 = (bf16[1,72,2304]{2,1,0:T(8,128)(2,1)}, bf16[1,72,2304]{2,1,0:T(8,128)(2,1)}, u32[]{:S(2)}, u32[]{:S(2)}) collective-permute-start(bf16[1,72,2304]{2,1,0:T(8,128)(2,1)} %get-tuple-element.185), channel_id=1, source_target_pairs={{0,16},{2,18},{4,20},{6,22},{8,24},{10,26},{12,28},{14,30},{16,0},... | collective-permute-start | bytes 995336 | tf_op jit(solution)/shard_map/ppermute | solution.py:269
  276.4 46.8 %all-to-all-start = ((bf16[32,2,400]{2,1,0:T(2,128)(2,1)}), bf16[32,2,400]{2,1,0:T(2,128)(2,1)}, u32[]{:S(2)}, u32[]{:S(2)}) async-start(bf16[32,2,400]{2,1,0:T(2,128)(2,1)} %bitcast.46), calls=%async_computation | async-start | bytes 131072 | tf_op jit(solution)/shard_map/all_to_all | solution.py:665
  328.5 54.3 %collective-permute-start.36 = (bf16[240,1152]{1,0:T(8,128)(2,1)}, bf16[240,1152]{1,0:T(8,128)(2,1)}, u32[]{:S(2)}, u32[]{:S(2)}) collective-permute-start(bf16[240,1152]{1,0:T(8,128)(2,1)} %copy-done.212), channel_id=1, source_target_pairs={{0,2},{2,0},{4,6},{6,4},{8,10},{10,8},{12,14},{14,12},{16,18},{18,... | collective-permute-start | bytes 1658888 | tf_op jit(solution)/shard_map/ppermute | solution.py:269
  340.3 35.8 %collective-permute-start.33 = (bf16[2,432,576]{2,1,0:T(8,128)(2,1)}, bf16[2,432,576]{2,1,0:T(8,128)(2,1)}, u32[]{:S(2)}, u32[]{:S(2)}) collective-permute-start(bf16[2,432,576]{2,1,0:T(8,128)(2,1)} %slice.1091), channel_id=1, source_target_pairs={{0,1},{1,0},{2,3},{3,2},{4,5},{5,4},{6,7},{7,6},{8,9},{9,8},{10,11... | collective-permute-start | bytes 2985992 | tf_op jit(solution)/shard_map/ppermute | solution.py:293
  344.3 38.2 %all-to-all-start.1 = ((f32[32,2,3456]{2,1,0:T(2,128)}), f32[32,2,3456]{2,1,0:T(2,128)S(1)}, u32[]{:S(2)}, u32[]{:S(2)}) async-start(f32[32,2,3456]{2,1,0:T(2,128)} %reshape.822), calls=%async_computation.1 | async-start | bytes 1769472 | tf_op jit(solution)/shard_map/all_to_all | solution.py:665
  390.7 45.8 %collective-permute-start.40 = (bf16[4,2,432,1152]{3,2,1,0:T(8,128)(2,1)}, bf16[4,2,432,1152]{3,2,1,0:T(8,128)(2,1)S(1)}, u32[]{:S(2)}, u32[]{:S(2)}) collective-permute-start(bf16[4,2,432,1152]{3,2,1,0:T(8,128)(2,1)} %fusion.41), channel_id=1, source_target_pairs={{0,2},{2,0},{4,6},{6,4},{8,10},{10,8},{12,14},{14,12},{16,18},{18,... | collective-permute-start | bytes 23887880 | tf_op jit(solution)/shard_map/ppermute | solution.py:269
  460.6 35.4 %collective-permute-start.48 = (bf16[4,2,72,4608]{3,2,1,0:T(8,128)(2,1)}, bf16[4,2,72,4608]{3,2,1,0:T(8,128)(2,1)S(1)}, u32[]{:S(2)}, u32[]{:S(2)}) collective-permute-start(bf16[4,2,72,4608]{3,2,1,0:T(8,128)(2,1)} %fusion.60), channel_id=1, source_target_pairs={{0,2},{2,0},{4,6},{6,4},{8,10},{10,8},{12,14},{14,12},{16,18},{18,... | collective-permute-start | bytes 15925256 | tf_op jit(solution)/shard_map/ppermute | solution.py:269
  460.6 35.3 %collective-permute-start.49 = (bf16[512,1152]{1,0:T(8,128)(2,1)S(1)}, bf16[512,1152]{1,0:T(8,128)(2,1)}, u32[]{:S(2)}, u32[]{:S(2)}) collective-permute-start(bf16[512,1152]{1,0:T(8,128)(2,1)S(1)} %self_attend.2), channel_id=1, source_target_pairs={{0,2},{2,0},{4,6},{6,4},{8,10},{10,8},{12,14},{14,12},{16,18},{18,... | collective-permute-start | bytes 3538952 | tf_op jit(solution)/shard_map/ppermute | solution.py:269
  546.3 60.7 %collective-permute-start.55 = (bf16[512,4608]{1,0:T(8,128)(2,1)}, bf16[512,4608]{1,0:T(8,128)(2,1)}, u32[]{:S(2)}, u32[]{:S(2)}) collective-permute-start(bf16[512,4608]{1,0:T(8,128)(2,1)} %get-tuple-element.738), channel_id=1, source_target_pairs={{0,2},{2,0},{4,6},{6,4},{8,10},{10,8},{12,14},{14,12},{16,18},{18,... | collective-permute-start | bytes 14155784 | tf_op jit(solution)/shard_map/ppermute | solution.py:269
  596.4 78.3 %collective-permute-start.58 = (bf16[512,1152]{1,0:T(8,128)(2,1)}, bf16[512,1152]{1,0:T(8,128)(2,1)}, u32[]{:S(2)}, u32[]{:S(2)}) collective-permute-start(bf16[512,1152]{1,0:T(8,128)(2,1)} %copy-done.134), channel_id=1, source_target_pairs={{0,2},{2,0},{4,6},{6,4},{8,10},{10,8},{12,14},{14,12},{16,18},{18,... | collective-permute-start | bytes 3538952 | tf_op jit(solution)/shard_map/ppermute | solution.py:269
  596.4 419.7 %collective-permute-start.100 = (bf16[512,1152]{1,0:T(8,128)(2,1)}, bf16[512,1152]{1,0:T(8,128)(2,1)}, u32[]{:S(2)}, u32[]{:S(2)}) collective-permute-start(bf16[512,1152]{1,0:T(8,128)(2,1)} %cross_attend.1), channel_id=1, source_target_pairs={{0,2},{2,0},{4,6},{6,4},{8,10},{10,8},{12,14},{14,12},{16,18},{18,... | collective-permute-start | bytes 3538952 | tf_op jit(solution)/shard_map/ppermute | solution.py:269
  632.2 42.5 %collective-permute-start.59 = (bf16[512,4608]{1,0:T(8,128)(2,1)}, bf16[512,4608]{1,0:T(8,128)(2,1)}, u32[]{:S(2)}, u32[]{:S(2)}) collective-permute-start(bf16[512,4608]{1,0:T(8,128)(2,1)} %fusion.8), channel_id=1, source_target_pairs={{0,2},{2,0},{4,6},{6,4},{8,10},{10,8},{12,14},{14,12},{16,18},{18,... | collective-permute-start | bytes 14155784 | tf_op jit(solution)/shard_map/ppermute | solution.py:269
  683.4 35.1 %collective-permute-start.62 = (bf16[1,144,4608]{2,1,0:T(8,128)(2,1)}, bf16[1,144,4608]{2,1,0:T(8,128)(2,1)}, u32[]{:S(2)}, u32[]{:S(2)}) collective-permute-start(bf16[1,144,4608]{2,1,0:T(8,128)(2,1)} %get-tuple-element.220), channel_id=1, source_target_pairs={{0,4},{2,6},{4,0},{6,2},{8,12},{10,14},{12,8},{14,10},{16,20},{18,... | collective-permute-start | bytes 3981320 | tf_op jit(solution)/shard_map/ppermute | solution.py:269
  684.7 35.7 %collective-permute-start.63 = (bf16[1,2,144,2304]{3,2,1,0:T(8,128)(2,1)}, bf16[1,2,144,2304]{3,2,1,0:T(8,128)(2,1)}, u32[]{:S(2)}, u32[]{:S(2)}) collective-permute-start(bf16[1,2,144,2304]{3,2,1,0:T(8,128)(2,1)} %slice_select_fusion.2), channel_id=1, source_target_pairs={{0,1},{1,0},{2,3},{3,2},{4,5},{5,4},{6,7},{7,6},{8,9},{9,8},{10,11... | collective-permute-start | bytes 3981320 | tf_op jit(solution)/shard_map/ppermute | solution.py:293
  713.3 35.4 %collective-permute-start.66 = (bf16[240,2304]{1,0:T(8,128)(2,1)S(1)}, bf16[240,2304]{1,0:T(8,128)(2,1)S(1)}, u32[]{:S(2)}, u32[]{:S(2)}) collective-permute-start(bf16[240,2304]{1,0:T(8,128)(2,1)S(1)} %bitcast.888), channel_id=1, source_target_pairs={{0,2},{2,0},{4,6},{6,4},{8,10},{10,8},{12,14},{14,12},{16,18},{18,... | collective-permute-start | bytes 3317768 | tf_op jit(solution)/shard_map/ppermute | solution.py:269
  761.5 42.1 %collective-permute-start.71 = (bf16[1,2,432,576]{3,2,1,0:T(8,128)(2,1)}, bf16[1,2,432,576]{3,2,1,0:T(8,128)(2,1)}, u32[]{:S(2)}, u32[]{:S(2)}) collective-permute-start(bf16[1,2,432,576]{3,2,1,0:T(8,128)(2,1)} %slice_select_fusion.4), channel_id=1, source_target_pairs={{0,1},{1,0},{2,3},{3,2},{4,5},{5,4},{6,7},{7,6},{8,9},{9,8},{10,11... | collective-permute-start | bytes 2985992 | tf_op jit(solution)/shard_map/ppermute | solution.py:293
  792.2 45.7 %collective-permute-start.77 = (bf16[144,2304]{1,0:T(8,128)(2,1)}, bf16[144,2304]{1,0:T(8,128)(2,1)}, u32[]{:S(2)}, u32[]{:S(2)}) collective-permute-start(bf16[144,2304]{1,0:T(8,128)(2,1)} %get-tuple-element.240), channel_id=1, source_target_pairs={{2,18},{6,22},{10,26},{14,30},{16,0},{20,4},{24,8},{28,12},{3,19},... | collective-permute-start | bytes 1990664 | tf_op jit(solution)/shard_map/ppermute | solution.py:286
  793.8 91.9 %collective-permute-start.78 = (bf16[512,3456]{1,0:T(8,128)(2,1)S(1)}, bf16[512,3456]{1,0:T(8,128)(2,1)}, u32[]{:S(2)}, u32[]{:S(2)}) collective-permute-start(bf16[512,3456]{1,0:T(8,128)(2,1)S(1)} %self_attend_back.2), channel_id=1, source_target_pairs={{0,2},{2,0},{4,6},{6,4},{8,10},{10,8},{12,14},{14,12},{16,18},{18,... | collective-permute-start | bytes 10616840 | tf_op jit(solution)/shard_map/ppermute | solution.py:269
  921.5 51.6 %collective-permute-start.86 = (bf16[512,3456]{1,0:T(8,128)(2,1)S(1)}, bf16[512,3456]{1,0:T(8,128)(2,1)}, u32[]{:S(2)}, u32[]{:S(2)}) collective-permute-start(bf16[512,3456]{1,0:T(8,128)(2,1)S(1)} %self_attend_back.3), channel_id=1, source_target_pairs={{0,2},{2,0},{4,6},{6,4},{8,10},{10,8},{12,14},{14,12},{16,18},{18,... | collective-permute-start | bytes 10616840 | tf_op jit(solution)/shard_map/ppermute | solution.py:269
  938.6 82.6 %collective-permute-start.99 = (bf16[512,1152]{1,0:T(8,128)(2,1)}, bf16[512,1152]{1,0:T(8,128)(2,1)}, u32[]{:S(2)}, u32[]{:S(2)}) collective-permute-start(bf16[512,1152]{1,0:T(8,128)(2,1)} %get-tuple-element.501), channel_id=1, source_target_pairs={{0,2},{2,0},{4,6},{6,4},{8,10},{10,8},{12,14},{14,12},{16,18},{18,... | collective-permute-start | bytes 3538952 | tf_op jit(solution)/shard_map/ppermute | solution.py:269
  1040.4 44.4 %collective-permute-start.108 = (bf16[1,576,1152]{2,1,0:T(8,128)(2,1)}, bf16[1,576,1152]{2,1,0:T(8,128)(2,1)}, u32[]{:S(2)}, u32[]{:S(2)}) collective-permute-start(bf16[1,576,1152]{2,1,0:T(8,128)(2,1)} %pad_maximum_fusion.8), channel_id=1, source_target_pairs={{0,4},{2,6},{4,0},{6,2},{8,12},{10,14},{12,8},{14,10},{16,20},{18,... | collective-permute-start | bytes 3981320 | tf_op jit(solution)/shard_map/ppermute | solution.py:269
  1041.0 57.8 %collective-permute-start.109 = (bf16[1,2,576,576]{3,2,1,0:T(8,128)(2,1)}, bf16[1,2,576,576]{3,2,1,0:T(8,128)(2,1)}, u32[]{:S(2)}, u32[]{:S(2)}) collective-permute-start(bf16[1,2,576,576]{3,2,1,0:T(8,128)(2,1)} %slice_select_fusion), channel_id=1, source_target_pairs={{0,1},{1,0},{2,3},{3,2},{4,5},{5,4},{6,7},{7,6},{8,9},{9,8},{10,11... | collective-permute-start | bytes 3981320 | tf_op jit(solution)/shard_map/ppermute | solution.py:293
  (377 other events, 4908.4 us)

commit v3 on v2

--- a/solution.py
+++ b/solution.py
@@ -375,6 +375,10 @@
     def plan(self, block):
         place = self.place
         half = place.half
+        rows, width = block.shape[1:]
+        self.folded = place.narrow == 2 and width % 128 != 0 and rows % 16 == 0
+        if self.folded:
+            block = jnp.concatenate([block[:, : rows // 2], block[:, rows // 2 :]], axis=-1)
         for bit in bits_of(half):
             [other] = yield [(block, lambda values, bit=bit: place.over_z(values, bit))]
             block = jnp.concatenate(pair_up(place.z & bit, block, other))
@@ -391,8 +395,8 @@
             (jnp.stack([piece[half:] for piece in by_y]), place.over_x),
             (by_x[:half], lambda values: spread_y(place, values)),
         ]
-        columns = block.shape[-1] * place.narrow
-        mine = unwritten((place.depth, 2, block.shape[1], columns))
+        columns = width * place.narrow
+        mine = unwritten((place.depth, 2, rows, columns))
         parts = (
             (0, 0, self.lanes([block] + list(by_y))),
             (0, 1, self.lanes([by_x[:half]] + list(near_xy))),
@@ -410,6 +414,16 @@
         place = self.place
         if place.narrow == 1:
             return pieces[0]
+        if self.folded:
+            low, high = pair_up(place.y, pieces[0], pieces[1])
+            width = low.shape[-1] // 2
+            return jnp.concatenate(
+                [
+                    jnp.concatenate([low[..., :width], high[..., :width]], axis=-1),
+                    jnp.concatenate([low[..., width:], high[..., width:]], axis=-1),
+                ],
+                axis=-2,
+            )
         if place.narrow == 2:
             return jnp.concatenate(pair_up(place.y, pieces[0], pieces[1]), axis=-1)
         return jnp.concatenate(

time: 1250 us -> 1220 us (0.976)
  waiting for transfers between devices: 369 us -> 351 us
    ppermute x79, waiting for transfers between devices: 226 us -> 211 us  [over_wide(): lax.ppermute(values, 'wide', [(i, i ^ bit) for i in range(self.wide)])]
    select_n x30, other arithmetic: 44.9 us -> 29.5 us  [pair_up(): return (jnp.where(first, own, other), jnp.where(first, other, own))]
    unnamed x577 -> x601, local copies, waits for them, and re-layouts: 51.2 us -> 54.6 us
  transfers between devices with their start and end apart: 126 -> 126, of which waited for: 45 -> 49; matrix products, arithmetic and copies ran while one was open for 45% -> 46% of each run, Pallas kernels for 5% -> 5%
where the time goes in v3:
time: 1220 us; the launch traced here: 1210 us
  waiting for transfers between devices  351 us (29%)
  matrix products  231 us (19%)
  other arithmetic  223 us (18%)
  local copies, waits for them, and re-layouts  180 us (15%)
  starting transfers between devices  148 us (12%)
  Pallas kernels  64.7 us (5%)
  between operations  13.1 us (1%)
    ppermute x79, waiting for transfers between devices, over_wide(): lax.ppermute(values, 'wide', [(i, i ^ bit) for i in range(self.wide)])  211 us
    dot_general x27, matrix products, matmul_tn(): lax.dot_general(operand, matrix, (((0,), (0,)), ((), ())), preferred_elem...  93 us
    convert_element_type x39, other arithmetic, rounded(): return values.astype(jnp.bfloat16)  87.2 us
    dot_general x15, matrix products, matmul(): return jnp.dot(operand, matrix, preferred_element_type=jnp.float32)  75 us
    ppermute x79, starting transfers between devices, over_wide(): lax.ppermute(values, 'wide', [(i, i ^ bit) for i in range(self.wide)])  68.5 us
    ppermute x26, waiting for transfers between devices, over_y(): lax.ppermute(values, 'narrow', [(i, i ^ bit) for i in range(self.narrow)])  66.8 us
    dot_general x14, matrix products, matmul_nt(): lax.dot_general(operand, matrix, (((1,), (1,)), ((), ())), preferred_elem...  63.1 us
    unnamed x601, local copies, waits for them, and re-layouts  54.6 us
  transfers between devices with their start and end apart: 126, of which 49 were waited for; matrix products, arithmetic and copies ran while one was open for 46% of the time, Pallas kernels for 5%

profile of v3, /device:TPU:0, one launch (start us, length us, event | category | flops | bytes accessed | tf_op | source)
XLA Modules:
  0.0 1210.8 jit_solution(8076239941787140505)
XLA Ops:
  30.4 7.0 collective-permute-done.3
  46.2 9.6 collective-permute-done.4
  66.6 8.4 collective-permute-done.7
  86.3 17.3 %collective-permute-done.14 = bf16[1,72,3456]{2,1,0:T(8,128)(2,1)S(1)} collective-permute-done((bf16[1,72,3456]{2,1,0:T(8,128)(2,1)S(1)}, bf16[1,72,3456]{2,1,0:T(8,128)(2,1)S(1)}, u32[]{:S(2)}, u32[]{:S(2)}) %collective-permute-start.14) | collective-permute-done | bytes 497696 | tf_op jit(solution)/shard_map/ppermute | solution.py:269
  136.6 12.5 %collective-permute-done.18 = bf16[1,72,3456]{2,1,0:T(8,128)(2,1)S(1)} collective-permute-done((bf16[1,72,3456]{2,1,0:T(8,128)(2,1)}, bf16[1,72,3456]{2,1,0:T(8,128)(2,1)S(1)}, u32[]{:S(2)}, u32[]{:S(2)}) %collective-permute-start.18) | collective-permute-done | bytes 497696 | tf_op jit(solution)/shard_map/ppermute | solution.py:269
  164.6 34.8 %collective-permute-done.21 = bf16[4,72,3456]{2,1,0:T(8,128)(2,1)S(1)} collective-permute-done((bf16[4,72,3456]{2,1,0:T(8,128)(2,1)S(1)}, bf16[4,72,3456]{2,1,0:T(8,128)(2,1)S(1)}, u32[]{:S(2)}, u32[]{:S(2)}) %collective-permute-start.21) | collective-permute-done | bytes 1990688 | tf_op jit(solution)/shard_map/ppermute | solution.py:269
  251.9 8.1 multiply_convert_fusion.2
  267.9 23.5 %all-to-all-done = bf16[32,2,400]{2,1,0:T(2,128)(2,1)} async-done(((bf16[32,2,400]{2,1,0:T(2,128)(2,1)}), bf16[32,2,400]{2,1,0:T(2,128)(2,1)}, u32[]{:S(2)}, u32[]{:S(2)}) %all-to-all-start) | async-done | bytes 51232 | tf_op jit(solution)/shard_map/all_to_all | solution.py:679
  324.9 15.0 %collective-permute-done.32 = bf16[1,2,216,1152]{3,2,1,0:T(8,128)(2,1)} collective-permute-done((bf16[1,2,216,1152]{3,2,1,0:T(8,128)(2,1)}, bf16[1,2,216,1152]{3,2,1,0:T(8,128)(2,1)}, u32[]{:S(2)}, u32[]{:S(2)}) %collective-permute-start.32) | collective-permute-done | bytes 995360 | tf_op jit(solution)/shard_map/ppermute | solution.py:269
  349.9 7.2 collective-permute-done.31
  377.2 7.9 collective-permute-done.41
  385.1 13.0 %collective-permute-done.39 = bf16[4,72,2304]{2,1,0:T(8,128)(2,1)S(1)} collective-permute-done((bf16[4,72,2304]{2,1,0:T(8,128)(2,1)S(1)}, bf16[4,72,2304]{2,1,0:T(8,128)(2,1)S(1)}, u32[]{:S(2)}, u32[]{:S(2)}) %collective-permute-start.39) | collective-permute-done | bytes 1327136 | tf_op jit(solution)/shard_map/ppermute | solution.py:269
  447.1 11.0 collective-permute-done.47
  497.8 14.7 %multiply_convert_fusion = (bf16[512,4608]{1,0:T(8,128)(2,1)}, f32[512,4608]{1,0:T(8,128)}) fusion(bf16[512,1152]{1,0:T(8,128)(2,1)S(1)} %fusion.42, bf16[1152,4608]{1,0:T(8,128)(2,1)} %bitcast.911), kind=kOutput, calls=%fused_computation.17 | convolution fusion | flops 5457051648 | bytes 25952256 | tf_op jit(solution)/shard_map/dot_general | solution.py:28
  523.0 12.7 %broadcast_multiply_fusion = (f32[2,256,1152]{2,1,0:T(8,128)S(1)}, f32[2,256,1152]{2,1,0:T(8,128)}) fusion(f32[2,1152]{1,0:T(2,128)S(1)} %copy-done.239, bf16[2,256,4608]{2,1,0:T(8,128)(2,1)} %bitcast.129, bf16[1152,4608,1]{1,0,2:T(8,128)(2,1)} %bitcast.913), kind=kOutput, calls=%fused_computation.294 | convolution fusion | flops 5436407808 | bytes 20063232 | tf_op jit(solution)/shard_map/dot_general | solution.py:38
  583.8 14.7 %fusion.8 = bf16[512,4608]{1,0:T(8,128)(2,1)} fusion(f32[512,4608]{1,0:T(8,128)} %get-tuple-element.781, bf16[512,1152]{1,0:T(8,128)(2,1)} %bitcast.146, bf16[1152,4608]{1,0:T(8,128)(2,1)S(1)} %bitcast.916), kind=kOutput, calls=%fused_computation.14 | convolution fusion | flops 5483003904 | bytes 25952256 | tf_op jit(solution)/shard_map/dot_general | solution.py:28
  600.2 7.8 convolution_convert_fusion.1
  615.4 11.4 multiply_reduce_fusion.3
  654.3 15.5 %cross_attend_back.1 = (bf16[512,1152]{1,0:T(8,128)(2,1)S(1)}, bf16[2,120,2304]{2,1,0:T(8,128)(2,1)S(1)}) custom-call(s32[2]{0:T(128)S(1)} %copy-done.6, bf16[512,1152]{1,0:T(8,128)(2,1)S(1)} %convolution_convert_fusion.17.query_ref, bf16[2,120,2304]{2,1,0:T(8,128)(2,1)S(1)} %bitcast.877, bf16[512,1152]{1,0:T(8,128)(2,1)S(1)} %convolution_convert_fusion.16.grad_ref), custom_call_target="tpu_custom_call" | custom-call | tf_op jit(solution)/shard_map/cross_attend_back/pallas_call | solution.py:232
  708.3 6.6 fusion.1
  732.0 17.2 %self_attend_back.2 = bf16[512,3456]{1,0:T(8,128)(2,1)S(1)} custom-call(bf16[512,3456]{1,0:T(8,128)(2,1)} %copy-done.1, bf16[512,1152]{1,0:T(8,128)(2,1)S(1)} %convolution_convert_fusion.15.grad_ref), custom_call_target="tpu_custom_call" | custom-call | tf_op jit(solution)/shard_map/self_attend_back/pallas_call | solution.py:180
  773.2 7.9 fusion.39
  791.6 9.1 collective-permute-done.76
  806.6 25.4 %collective-permute-done.80 = bf16[1,2,544,576]{3,2,1,0:T(8,128)(2,1)S(1)} collective-permute-done((bf16[1,2,544,576]{3,2,1,0:T(8,128)(2,1)S(1)}, bf16[1,2,544,576]{3,2,1,0:T(8,128)(2,1)S(1)}, u32[]{:S(2)}, u32[]{:S(2)}) %collective-permute-start.80) | collective-permute-done | bytes 1253408 | tf_op jit(solution)/shard_map/ppermute | solution.py:293
  840.0 9.3 collective-permute-done.83
  862.1 17.2 %self_attend_back.3 = bf16[512,3456]{1,0:T(8,128)(2,1)S(1)} custom-call(bf16[512,3456]{1,0:T(8,128)(2,1)} %copy-done, bf16[512,1152]{1,0:T(8,128)(2,1)S(1)} %convolution_convert_fusion.14.grad_ref), custom_call_target="tpu_custom_call" | custom-call | tf_op jit(solution)/shard_map/self_attend_back/pallas_call | solution.py:180
  892.1 7.6 fusion.273
  906.2 18.9 %collective-permute-done.88 = bf16[1,2,144,1728]{3,2,1,0:T(8,128)(2,1)S(1)} collective-permute-done((bf16[1,2,144,1728]{3,2,1,0:T(8,128)(2,1)S(1)}, bf16[1,2,144,1728]{3,2,1,0:T(8,128)(2,1)S(1)}, u32[]{:S(2)}, u32[]{:S(2)}) %collective-permute-start.88) | collective-permute-done | bytes 995360 | tf_op jit(solution)/shard_map/ppermute | solution.py:293
  929.8 8.8 collective-permute-done.89
  1010.5 11.8 collective-permute-done.97
  1102.8 7.9 collective-permute-done.114
  1140.8 16.2 %collective-permute-done.117 = bf16[576,576]{1,0:T(8,128)(2,1)S(1)} collective-permute-done((bf16[576,576]{1,0:T(8,128)(2,1)}, bf16[576,576]{1,0:T(8,128)(2,1)S(1)}, u32[]{:S(2)}, u32[]{:S(2)}) %collective-permute-start.117) | collective-permute-done | bytes 663584 | tf_op jit(solution)/shard_map/ppermute | solution.py:286
  (1277 shorter events, 782.1 us)
Async XLA Ops:
  9.4 340.4 %collective-permute-start.35 = (bf16[240,4352]{1,0:T(8,128)(2,1)}, bf16[240,4352]{1,0:T(8,128)(2,1)}, u32[]{:S(2)}, u32[]{:S(2)}) collective-permute-start(bf16[240,4352]{1,0:T(8,128)(2,1)} %pad.13), channel_id=1, source_target_pairs={{0,2},{2,0},{4,6},{6,4},{8,10},{10,8},{12,14},{14,12},{16,18},{18,... | collective-permute-start | bytes 6266888 | tf_op jit(solution)/shard_map/ppermute | solution.py:269
  156.3 44.8 %collective-permute-start.20 = (bf16[4,72,3456]{2,1,0:T(8,128)(2,1)S(1)}, bf16[4,72,3456]{2,1,0:T(8,128)(2,1)S(1)}, u32[]{:S(2)}, u32[]{:S(2)}) collective-permute-start(bf16[4,72,3456]{2,1,0:T(8,128)(2,1)S(1)} %pad_maximum_fusion.16), channel_id=1, source_target_pairs={{0,1},{1,0},{2,3},{3,2},{4,5},{5,4},{6,7},{7,6},{8,9},{9,8},{10,11... | collective-permute-start | bytes 5971976 | tf_op jit(solution)/shard_map/ppermute | solution.py:293
  157.9 41.5 %collective-permute-start.21 = (bf16[4,72,3456]{2,1,0:T(8,128)(2,1)S(1)}, bf16[4,72,3456]{2,1,0:T(8,128)(2,1)S(1)}, u32[]{:S(2)}, u32[]{:S(2)}) collective-permute-start(bf16[4,72,3456]{2,1,0:T(8,128)(2,1)S(1)} %pad_maximum_fusion.16), channel_id=1, source_target_pairs={{0,4},{2,6},{4,0},{6,2},{8,12},{10,14},{12,8},{14,10},{16,20},{18,... | collective-permute-start | bytes 5971976 | tf_op jit(solution)/shard_map/ppermute | solution.py:269
  159.4 47.6 %collective-permute-start.19 = (bf16[4,2,272,1152]{3,2,1,0:T(8,128)(2,1)S(1)}, bf16[4,2,272,1152]{3,2,1,0:T(8,128)(2,1)}, u32[]{:S(2)}, u32[]{:S(2)}) collective-permute-start(bf16[4,2,272,1152]{3,2,1,0:T(8,128)(2,1)S(1)} %fusion.83), channel_id=1, source_target_pairs={{0,2},{2,0},{4,6},{6,4},{8,10},{10,8},{12,14},{14,12},{16,18},{18,... | collective-permute-start | bytes 15040520 | tf_op jit(solution)/shard_map/ppermute | solution.py:269
  163.0 43.9 %collective-permute-start.22 = (bf16[1,216,1152]{2,1,0:T(8,128)(2,1)}, bf16[1,216,1152]{2,1,0:T(8,128)(2,1)S(1)}, u32[]{:S(2)}, u32[]{:S(2)}) collective-permute-start(bf16[1,216,1152]{2,1,0:T(8,128)(2,1)} %get-tuple-element.176), channel_id=1, source_target_pairs={{0,16},{2,18},{4,20},{6,22},{8,24},{10,26},{12,28},{14,30},{16,0},... | collective-permute-start | bytes 1493000 | tf_op jit(solution)/shard_map/ppermute | solution.py:269
  236.1 71.5 %collective-permute-start.29 = (bf16[4,2,144,3456]{3,2,1,0:T(8,128)(2,1)}, bf16[4,2,144,3456]{3,2,1,0:T(8,128)(2,1)}, u32[]{:S(2)}, u32[]{:S(2)}) collective-permute-start(bf16[4,2,144,3456]{3,2,1,0:T(8,128)(2,1)} %fusion.52), channel_id=1, source_target_pairs={{0,2},{2,0},{4,6},{6,4},{8,10},{10,8},{12,14},{14,12},{16,18},{18,... | collective-permute-start | bytes 23887880 | tf_op jit(solution)/shard_map/ppermute | solution.py:269
  243.4 55.2 %collective-permute-start.27 = (bf16[4,216,1152]{2,1,0:T(8,128)(2,1)}, bf16[4,216,1152]{2,1,0:T(8,128)(2,1)}, u32[]{:S(2)}, u32[]{:S(2)}) collective-permute-start(bf16[4,216,1152]{2,1,0:T(8,128)(2,1)} %pad_maximum_fusion.17), channel_id=1, source_target_pairs={{0,1},{1,0},{2,3},{3,2},{4,5},{5,4},{6,7},{7,6},{8,9},{9,8},{10,11... | collective-permute-start | bytes 5971976 | tf_op jit(solution)/shard_map/ppermute | solution.py:293
  244.1 52.1 %collective-permute-start.28 = (bf16[4,216,1152]{2,1,0:T(8,128)(2,1)}, bf16[4,216,1152]{2,1,0:T(8,128)(2,1)}, u32[]{:S(2)}, u32[]{:S(2)}) collective-permute-start(bf16[4,216,1152]{2,1,0:T(8,128)(2,1)} %pad_maximum_fusion.17), channel_id=1, source_target_pairs={{0,4},{2,6},{4,0},{6,2},{8,12},{10,14},{12,8},{14,10},{16,20},{18,... | collective-permute-start | bytes 5971976 | tf_op jit(solution)/shard_map/ppermute | solution.py:269
  245.5 62.1 %collective-permute-start.30 = (bf16[1,72,2304]{2,1,0:T(8,128)(2,1)}, bf16[1,72,2304]{2,1,0:T(8,128)(2,1)}, u32[]{:S(2)}, u32[]{:S(2)}) collective-permute-start(bf16[1,72,2304]{2,1,0:T(8,128)(2,1)} %get-tuple-element.185), channel_id=1, source_target_pairs={{0,16},{2,18},{4,20},{6,22},{8,24},{10,26},{12,28},{14,30},{16,0},... | collective-permute-start | bytes 995336 | tf_op jit(solution)/shard_map/ppermute | solution.py:269
  246.3 45.0 %all-to-all-start = ((bf16[32,2,400]{2,1,0:T(2,128)(2,1)}), bf16[32,2,400]{2,1,0:T(2,128)(2,1)}, u32[]{:S(2)}, u32[]{:S(2)}) async-start(bf16[32,2,400]{2,1,0:T(2,128)(2,1)} %bitcast.46), calls=%async_computation | async-start | bytes 131072 | tf_op jit(solution)/shard_map/all_to_all | solution.py:679
  296.2 53.7 %collective-permute-start.36 = (bf16[240,1152]{1,0:T(8,128)(2,1)}, bf16[240,1152]{1,0:T(8,128)(2,1)}, u32[]{:S(2)}, u32[]{:S(2)}) collective-permute-start(bf16[240,1152]{1,0:T(8,128)(2,1)} %copy-done.219), channel_id=1, source_target_pairs={{0,2},{2,0},{4,6},{6,4},{8,10},{10,8},{12,14},{14,12},{16,18},{18,... | collective-permute-start | bytes 1658888 | tf_op jit(solution)/shard_map/ppermute | solution.py:269
  312.1 37.4 %all-to-all-start.1 = ((f32[32,2,3456]{2,1,0:T(2,128)}), f32[32,2,3456]{2,1,0:T(2,128)S(1)}, u32[]{:S(2)}, u32[]{:S(2)}) async-start(f32[32,2,3456]{2,1,0:T(2,128)} %reshape.822), calls=%async_computation.1 | async-start | bytes 1769472 | tf_op jit(solution)/shard_map/all_to_all | solution.py:679
  357.0 47.0 %collective-permute-start.40 = (bf16[4,2,432,1152]{3,2,1,0:T(8,128)(2,1)}, bf16[4,2,432,1152]{3,2,1,0:T(8,128)(2,1)S(1)}, u32[]{:S(2)}, u32[]{:S(2)}) collective-permute-start(bf16[4,2,432,1152]{3,2,1,0:T(8,128)(2,1)} %fusion.46), channel_id=1, source_target_pairs={{0,2},{2,0},{4,6},{6,4},{8,10},{10,8},{12,14},{14,12},{16,18},{18,... | collective-permute-start | bytes 23887880 | tf_op jit(solution)/shard_map/ppermute | solution.py:269
  425.8 33.5 %collective-permute-start.46 = (bf16[4,72,2304]{2,1,0:T(8,128)(2,1)}, bf16[4,72,2304]{2,1,0:T(8,128)(2,1)}, u32[]{:S(2)}, u32[]{:S(2)}) collective-permute-start(bf16[4,72,2304]{2,1,0:T(8,128)(2,1)} %pad_maximum_fusion.20), channel_id=1, source_target_pairs={{0,1},{1,0},{2,3},{3,2},{4,5},{5,4},{6,7},{7,6},{8,9},{9,8},{10,11... | collective-permute-start | bytes 3981320 | tf_op jit(solution)/shard_map/ppermute | solution.py:293
  428.2 35.6 %collective-permute-start.48 = (bf16[4,2,72,4608]{3,2,1,0:T(8,128)(2,1)}, bf16[4,2,72,4608]{3,2,1,0:T(8,128)(2,1)S(1)}, u32[]{:S(2)}, u32[]{:S(2)}) collective-permute-start(bf16[4,2,72,4608]{3,2,1,0:T(8,128)(2,1)} %fusion.74), channel_id=1, source_target_pairs={{0,2},{2,0},{4,6},{6,4},{8,10},{10,8},{12,14},{14,12},{16,18},{18,... | collective-permute-start | bytes 15925256 | tf_op jit(solution)/shard_map/ppermute | solution.py:269
  428.2 35.5 %collective-permute-start.49 = (bf16[512,1152]{1,0:T(8,128)(2,1)S(1)}, bf16[512,1152]{1,0:T(8,128)(2,1)}, u32[]{:S(2)}, u32[]{:S(2)}) collective-permute-start(bf16[512,1152]{1,0:T(8,128)(2,1)S(1)} %self_attend.2), channel_id=1, source_target_pairs={{0,2},{2,0},{4,6},{6,4},{8,10},{10,8},{12,14},{14,12},{16,18},{18,... | collective-permute-start | bytes 3538952 | tf_op jit(solution)/shard_map/ppermute | solution.py:269
  512.5 60.7 %collective-permute-start.55 = (bf16[512,4608]{1,0:T(8,128)(2,1)}, bf16[512,4608]{1,0:T(8,128)(2,1)}, u32[]{:S(2)}, u32[]{:S(2)}) collective-permute-start(bf16[512,4608]{1,0:T(8,128)(2,1)} %get-tuple-element.780), channel_id=1, source_target_pairs={{0,2},{2,0},{4,6},{6,4},{8,10},{10,8},{12,14},{14,12},{16,18},{18,... | collective-permute-start | bytes 14155784 | tf_op jit(solution)/shard_map/ppermute | solution.py:269
  562.6 79.1 %collective-permute-start.58 = (bf16[512,1152]{1,0:T(8,128)(2,1)}, bf16[512,1152]{1,0:T(8,128)(2,1)}, u32[]{:S(2)}, u32[]{:S(2)}) collective-permute-start(bf16[512,1152]{1,0:T(8,128)(2,1)} %copy-done.127), channel_id=1, source_target_pairs={{0,2},{2,0},{4,6},{6,4},{8,10},{10,8},{12,14},{14,12},{16,18},{18,... | collective-permute-start | bytes 3538952 | tf_op jit(solution)/shard_map/ppermute | solution.py:269
  562.6 421.8 %collective-permute-start.100 = (bf16[512,1152]{1,0:T(8,128)(2,1)}, bf16[512,1152]{1,0:T(8,128)(2,1)}, u32[]{:S(2)}, u32[]{:S(2)}) collective-permute-start(bf16[512,1152]{1,0:T(8,128)(2,1)} %cross_attend.1), channel_id=1, source_target_pairs={{0,2},{2,0},{4,6},{6,4},{8,10},{10,8},{12,14},{14,12},{16,18},{18,... | collective-permute-start | bytes 3538952 | tf_op jit(solution)/shard_map/ppermute | solution.py:269
  598.5 43.2 %collective-permute-start.59 = (bf16[512,4608]{1,0:T(8,128)(2,1)}, bf16[512,4608]{1,0:T(8,128)(2,1)}, u32[]{:S(2)}, u32[]{:S(2)}) collective-permute-start(bf16[512,4608]{1,0:T(8,128)(2,1)} %fusion.8), channel_id=1, source_target_pairs={{0,2},{2,0},{4,6},{6,4},{8,10},{10,8},{12,14},{14,12},{16,18},{18,... | collective-permute-start | bytes 14155784 | tf_op jit(solution)/shard_map/ppermute | solution.py:269
  650.4 34.3 %collective-permute-start.62 = (bf16[1,144,4608]{2,1,0:T(8,128)(2,1)}, bf16[1,144,4608]{2,1,0:T(8,128)(2,1)}, u32[]{:S(2)}, u32[]{:S(2)}) collective-permute-start(bf16[1,144,4608]{2,1,0:T(8,128)(2,1)} %get-tuple-element.220), channel_id=1, source_target_pairs={{0,4},{2,6},{4,0},{6,2},{8,12},{10,14},{12,8},{14,10},{16,20},{18,... | collective-permute-start | bytes 3981320 | tf_op jit(solution)/shard_map/ppermute | solution.py:269
  651.7 34.9 %collective-permute-start.63 = (bf16[1,2,144,2304]{3,2,1,0:T(8,128)(2,1)}, bf16[1,2,144,2304]{3,2,1,0:T(8,128)(2,1)}, u32[]{:S(2)}, u32[]{:S(2)}) collective-permute-start(bf16[1,2,144,2304]{3,2,1,0:T(8,128)(2,1)} %slice_select_fusion.2), channel_id=1, source_target_pairs={{0,1},{1,0},{2,3},{3,2},{4,5},{5,4},{6,7},{7,6},{8,9},{9,8},{10,11... | collective-permute-start | bytes 3981320 | tf_op jit(solution)/shard_map/ppermute | solution.py:293
  679.5 35.4 %collective-permute-start.66 = (bf16[240,2304]{1,0:T(8,128)(2,1)S(1)}, bf16[240,2304]{1,0:T(8,128)(2,1)S(1)}, u32[]{:S(2)}, u32[]{:S(2)}) collective-permute-start(bf16[240,2304]{1,0:T(8,128)(2,1)S(1)} %bitcast.880), channel_id=1, source_target_pairs={{0,2},{2,0},{4,6},{6,4},{8,10},{10,8},{12,14},{14,12},{16,18},{18,... | collective-permute-start | bytes 3317768 | tf_op jit(solution)/shard_map/ppermute | solution.py:269
  688.0 33.6 %collective-permute-start.67 = (bf16[1,144,2304]{2,1,0:T(8,128)(2,1)S(1)}, bf16[1,144,2304]{2,1,0:T(8,128)(2,1)S(1)}, u32[]{:S(2)}, u32[]{:S(2)}) collective-permute-start(bf16[1,144,2304]{2,1,0:T(8,128)(2,1)S(1)} %add_convert_fusion.8), channel_id=1, source_target_pairs={{0,1},{1,0},{2,3},{3,2},{4,5},{5,4},{6,7},{7,6},{8,9},{9,8},{10,11... | collective-permute-start | bytes 1990664 | tf_op jit(solution)/shard_map/ppermute | solution.py:293
  728.4 41.3 %collective-permute-start.71 = (bf16[1,2,432,576]{3,2,1,0:T(8,128)(2,1)}, bf16[1,2,432,576]{3,2,1,0:T(8,128)(2,1)}, u32[]{:S(2)}, u32[]{:S(2)}) collective-permute-start(bf16[1,2,432,576]{3,2,1,0:T(8,128)(2,1)} %slice_select_fusion.4), channel_id=1, source_target_pairs={{0,1},{1,0},{2,3},{3,2},{4,5},{5,4},{6,7},{7,6},{8,9},{9,8},{10,11... | collective-permute-start | bytes 2985992 | tf_op jit(solution)/shard_map/ppermute | solution.py:293
  759.1 45.9 %collective-permute-start.77 = (bf16[144,2304]{1,0:T(8,128)(2,1)}, bf16[144,2304]{1,0:T(8,128)(2,1)}, u32[]{:S(2)}, u32[]{:S(2)}) collective-permute-start(bf16[144,2304]{1,0:T(8,128)(2,1)} %get-tuple-element.240), channel_id=1, source_target_pairs={{2,18},{6,22},{10,26},{14,30},{16,0},{20,4},{24,8},{28,12},{3,19},... | collective-permute-start | bytes 1990664 | tf_op jit(solution)/shard_map/ppermute | solution.py:286
  760.6 92.0 %collective-permute-start.78 = (bf16[512,3456]{1,0:T(8,128)(2,1)S(1)}, bf16[512,3456]{1,0:T(8,128)(2,1)}, u32[]{:S(2)}, u32[]{:S(2)}) collective-permute-start(bf16[512,3456]{1,0:T(8,128)(2,1)S(1)} %self_attend_back.2), channel_id=1, source_target_pairs={{0,2},{2,0},{4,6},{6,4},{8,10},{10,8},{12,14},{14,12},{16,18},{18,... | collective-permute-start | bytes 10616840 | tf_op jit(solution)/shard_map/ppermute | solution.py:269
  889.0 53.0 %collective-permute-start.86 = (bf16[512,3456]{1,0:T(8,128)(2,1)S(1)}, bf16[512,3456]{1,0:T(8,128)(2,1)}, u32[]{:S(2)}, u32[]{:S(2)}) collective-permute-start(bf16[512,3456]{1,0:T(8,128)(2,1)S(1)} %self_attend_back.3), channel_id=1, source_target_pairs={{0,2},{2,0},{4,6},{6,4},{8,10},{10,8},{12,14},{14,12},{16,18},{18,... | collective-permute-start | bytes 10616840 | tf_op jit(solution)/shard_map/ppermute | solution.py:269
  906.1 83.1 %collective-permute-start.99 = (bf16[512,1152]{1,0:T(8,128)(2,1)}, bf16[512,1152]{1,0:T(8,128)(2,1)}, u32[]{:S(2)}, u32[]{:S(2)}) collective-permute-start(bf16[512,1152]{1,0:T(8,128)(2,1)} %get-tuple-element.501), channel_id=1, source_target_pairs={{0,2},{2,0},{4,6},{6,4},{8,10},{10,8},{12,14},{14,12},{16,18},{18,... | collective-permute-start | bytes 3538952 | tf_op jit(solution)/shard_map/ppermute | solution.py:269
  942.0 33.9 %collective-permute-start.91 = (bf16[1,544,576]{2,1,0:T(8,128)(2,1)}, bf16[1,544,576]{2,1,0:T(8,128)(2,1)}, u32[]{:S(2)}, u32[]{:S(2)}) collective-permute-start(bf16[1,544,576]{2,1,0:T(8,128)(2,1)} %select_convert_fusion.1), channel_id=1, source_target_pairs={{0,8},{2,10},{4,12},{6,14},{8,0},{10,2},{12,4},{14,6},{16,24},{18,... | collective-permute-start | bytes 1880072 | tf_op jit(solution)/shard_map/ppermute | solution.py:269
  1008.2 45.0 %collective-permute-start.108 = (bf16[1,576,1152]{2,1,0:T(8,128)(2,1)}, bf16[1,576,1152]{2,1,0:T(8,128)(2,1)}, u32[]{:S(2)}, u32[]{:S(2)}) collective-permute-start(bf16[1,576,1152]{2,1,0:T(8,128)(2,1)} %pad_maximum_fusion.21), channel_id=1, source_target_pairs={{0,4},{2,6},{4,0},{6,2},{8,12},{10,14},{12,8},{14,10},{16,20},{18,... | collective-permute-start | bytes 3981320 | tf_op jit(solution)/shard_map/ppermute | solution.py:269
  1009.3 57.5 %collective-permute-start.109 = (bf16[1,2,576,576]{3,2,1,0:T(8,128)(2,1)}, bf16[1,2,576,576]{3,2,1,0:T(8,128)(2,1)}, u32[]{:S(2)}, u32[]{:S(2)}) collective-permute-start(bf16[1,2,576,576]{3,2,1,0:T(8,128)(2,1)} %slice_select_fusion), channel_id=1, source_target_pairs={{0,1},{1,0},{2,3},{3,2},{4,5},{5,4},{6,7},{7,6},{8,9},{9,8},{10,11... | collective-permute-start | bytes 3981320 | tf_op jit(solution)/shard_map/ppermute | solution.py:293
  (390 other events, 5138.3 us)

commit v4 on v3

--- a/solution.py
+++ b/solution.py
@@ -772,7 +772,7 @@
     caption_inner = matmul(ticks.during(caption_rows), entry_all[:CAP])
     caption_act = rounded(jax.nn.gelu(caption_inner))
     context_low = rounded(matmul(caption_act, proj_all[1]))
-    gather_on(context_low, part)
+    gather_on(context_low)
     part = to_all(ticks.during(part))
     qkv_gather.other = ticks.during(qkv_gather.other)
     qkv_all = [qkv_gather.whole(0, rows), qkv_gather.whole(rows, rows)]

time: 1220 us -> 1220 us (level)
  no operation moved by 1% of the time
where the time goes in v4:
time: 1220 us; the launch traced here: 1210 us
  waiting for transfers between devices  351 us (29%)
  matrix products  231 us (19%)
  other arithmetic  223 us (18%)
  local copies, waits for them, and re-layouts  180 us (15%)
  starting transfers between devices  148 us (12%)
  Pallas kernels  64.7 us (5%)
  between operations  13.1 us (1%)
    ppermute x79, waiting for transfers between devices, over_wide(): lax.ppermute(values, 'wide', [(i, i ^ bit) for i in range(self.wide)])  211 us
    dot_general x27, matrix products, matmul_tn(): lax.dot_general(operand, matrix, (((0,), (0,)), ((), ())), preferred_elem...  93 us
    convert_element_type x39, other arithmetic, rounded(): return values.astype(jnp.bfloat16)  87.2 us
    dot_general x15, matrix products, matmul(): return jnp.dot(operand, matrix, preferred_element_type=jnp.float32)  75 us
    ppermute x79, starting transfers between devices, over_wide(): lax.ppermute(values, 'wide', [(i, i ^ bit) for i in range(self.wide)])  68.5 us
    ppermute x26, waiting for transfers between devices, over_y(): lax.ppermute(values, 'narrow', [(i, i ^ bit) for i in range(self.narrow)])  66.8 us
    dot_general x14, matrix products, matmul_nt(): lax.dot_general(operand, matrix, (((1,), (1,)), ((), ())), preferred_elem...  63.1 us
    unnamed x601, local copies, waits for them, and re-layouts  54.6 us
  transfers between devices with their start and end apart: 126, of which 49 were waited for; matrix products, arithmetic and copies ran while one was open for 46% of the time, Pallas kernels for 5%

profile of v4, /device:TPU:0, one launch (start us, length us, event | category | flops | bytes accessed | tf_op | source)
XLA Modules:
  0.0 1210.8 jit_solution(8076239941787140505)
XLA Ops:
  30.4 7.0 collective-permute-done.3
  46.2 9.6 collective-permute-done.4
  66.6 8.4 collective-permute-done.7
  86.3 17.3 %collective-permute-done.14 = bf16[1,72,3456]{2,1,0:T(8,128)(2,1)S(1)} collective-permute-done((bf16[1,72,3456]{2,1,0:T(8,128)(2,1)S(1)}, bf16[1,72,3456]{2,1,0:T(8,128)(2,1)S(1)}, u32[]{:S(2)}, u32[]{:S(2)}) %collective-permute-start.14) | collective-permute-done | bytes 497696 | tf_op jit(solution)/shard_map/ppermute | solution.py:269
  136.6 12.5 %collective-permute-done.18 = bf16[1,72,3456]{2,1,0:T(8,128)(2,1)S(1)} collective-permute-done((bf16[1,72,3456]{2,1,0:T(8,128)(2,1)}, bf16[1,72,3456]{2,1,0:T(8,128)(2,1)S(1)}, u32[]{:S(2)}, u32[]{:S(2)}) %collective-permute-start.18) | collective-permute-done | bytes 497696 | tf_op jit(solution)/shard_map/ppermute | solution.py:269
  164.6 34.8 %collective-permute-done.21 = bf16[4,72,3456]{2,1,0:T(8,128)(2,1)S(1)} collective-permute-done((bf16[4,72,3456]{2,1,0:T(8,128)(2,1)S(1)}, bf16[4,72,3456]{2,1,0:T(8,128)(2,1)S(1)}, u32[]{:S(2)}, u32[]{:S(2)}) %collective-permute-start.21) | collective-permute-done | bytes 1990688 | tf_op jit(solution)/shard_map/ppermute | solution.py:269
  251.9 8.1 multiply_convert_fusion.2
  267.9 23.5 %all-to-all-done = bf16[32,2,400]{2,1,0:T(2,128)(2,1)} async-done(((bf16[32,2,400]{2,1,0:T(2,128)(2,1)}), bf16[32,2,400]{2,1,0:T(2,128)(2,1)}, u32[]{:S(2)}, u32[]{:S(2)}) %all-to-all-start) | async-done | bytes 51232 | tf_op jit(solution)/shard_map/all_to_all | solution.py:679
  324.9 15.0 %collective-permute-done.32 = bf16[1,2,216,1152]{3,2,1,0:T(8,128)(2,1)} collective-permute-done((bf16[1,2,216,1152]{3,2,1,0:T(8,128)(2,1)}, bf16[1,2,216,1152]{3,2,1,0:T(8,128)(2,1)}, u32[]{:S(2)}, u32[]{:S(2)}) %collective-permute-start.32) | collective-permute-done | bytes 995360 | tf_op jit(solution)/shard_map/ppermute | solution.py:269
  349.9 7.2 collective-permute-done.31
  377.2 7.9 collective-permute-done.41
  385.1 13.0 %collective-permute-done.39 = bf16[4,72,2304]{2,1,0:T(8,128)(2,1)S(1)} collective-permute-done((bf16[4,72,2304]{2,1,0:T(8,128)(2,1)S(1)}, bf16[4,72,2304]{2,1,0:T(8,128)(2,1)S(1)}, u32[]{:S(2)}, u32[]{:S(2)}) %collective-permute-start.39) | collective-permute-done | bytes 1327136 | tf_op jit(solution)/shard_map/ppermute | solution.py:269
  447.1 11.0 collective-permute-done.47
  497.8 14.7 %multiply_convert_fusion = (bf16[512,4608]{1,0:T(8,128)(2,1)}, f32[512,4608]{1,0:T(8,128)}) fusion(bf16[512,1152]{1,0:T(8,128)(2,1)S(1)} %fusion.42, bf16[1152,4608]{1,0:T(8,128)(2,1)} %bitcast.911), kind=kOutput, calls=%fused_computation.17 | convolution fusion | flops 5457051648 | bytes 25952256 | tf_op jit(solution)/shard_map/dot_general | solution.py:28
  523.0 12.7 %broadcast_multiply_fusion = (f32[2,256,1152]{2,1,0:T(8,128)S(1)}, f32[2,256,1152]{2,1,0:T(8,128)}) fusion(f32[2,1152]{1,0:T(2,128)S(1)} %copy-done.239, bf16[2,256,4608]{2,1,0:T(8,128)(2,1)} %bitcast.129, bf16[1152,4608,1]{1,0,2:T(8,128)(2,1)} %bitcast.913), kind=kOutput, calls=%fused_computation.294 | convolution fusion | flops 5436407808 | bytes 20063232 | tf_op jit(solution)/shard_map/dot_general | solution.py:38
  583.8 14.7 %fusion.8 = bf16[512,4608]{1,0:T(8,128)(2,1)} fusion(f32[512,4608]{1,0:T(8,128)} %get-tuple-element.781, bf16[512,1152]{1,0:T(8,128)(2,1)} %bitcast.146, bf16[1152,4608]{1,0:T(8,128)(2,1)S(1)} %bitcast.916), kind=kOutput, calls=%fused_computation.14 | convolution fusion | flops 5483003904 | bytes 25952256 | tf_op jit(solution)/shard_map/dot_general | solution.py:28
  600.2 7.8 convolution_convert_fusion.1
  615.4 11.4 multiply_reduce_fusion.3
  654.3 15.5 %cross_attend_back.1 = (bf16[512,1152]{1,0:T(8,128)(2,1)S(1)}, bf16[2,120,2304]{2,1,0:T(8,128)(2,1)S(1)}) custom-call(s32[2]{0:T(128)S(1)} %copy-done.6, bf16[512,1152]{1,0:T(8,128)(2,1)S(1)} %convolution_convert_fusion.17.query_ref, bf16[2,120,2304]{2,1,0:T(8,128)(2,1)S(1)} %bitcast.877, bf16[512,1152]{1,0:T(8,128)(2,1)S(1)} %convolution_convert_fusion.16.grad_ref), custom_call_target="tpu_custom_call" | custom-call | tf_op jit(solution)/shard_map/cross_attend_back/pallas_call | solution.py:232
  708.3 6.6 fusion.1
  732.0 17.2 %self_attend_back.2 = bf16[512,3456]{1,0:T(8,128)(2,1)S(1)} custom-call(bf16[512,3456]{1,0:T(8,128)(2,1)} %copy-done.1, bf16[512,1152]{1,0:T(8,128)(2,1)S(1)} %convolution_convert_fusion.15.grad_ref), custom_call_target="tpu_custom_call" | custom-call | tf_op jit(solution)/shard_map/self_attend_back/pallas_call | solution.py:180
  773.2 7.9 fusion.39
  791.6 9.1 collective-permute-done.76
  806.6 25.4 %collective-permute-done.80 = bf16[1,2,544,576]{3,2,1,0:T(8,128)(2,1)S(1)} collective-permute-done((bf16[1,2,544,576]{3,2,1,0:T(8,128)(2,1)S(1)}, bf16[1,2,544,576]{3,2,1,0:T(8,128)(2,1)S(1)}, u32[]{:S(2)}, u32[]{:S(2)}) %collective-permute-start.80) | collective-permute-done | bytes 1253408 | tf_op jit(solution)/shard_map/ppermute | solution.py:293
  840.0 9.3 collective-permute-done.83
  862.1 17.2 %self_attend_back.3 = bf16[512,3456]{1,0:T(8,128)(2,1)S(1)} custom-call(bf16[512,3456]{1,0:T(8,128)(2,1)} %copy-done, bf16[512,1152]{1,0:T(8,128)(2,1)S(1)} %convolution_convert_fusion.14.grad_ref), custom_call_target="tpu_custom_call" | custom-call | tf_op jit(solution)/shard_map/self_attend_back/pallas_call | solution.py:180
  892.1 7.6 fusion.273
  906.2 18.9 %collective-permute-done.88 = bf16[1,2,144,1728]{3,2,1,0:T(8,128)(2,1)S(1)} collective-permute-done((bf16[1,2,144,1728]{3,2,1,0:T(8,128)(2,1)S(1)}, bf16[1,2,144,1728]{3,2,1,0:T(8,128)(2,1)S(1)}, u32[]{:S(2)}, u32[]{:S(2)}) %collective-permute-start.88) | collective-permute-done | bytes 995360 | tf_op jit(solution)/shard_map/ppermute | solution.py:293
  929.8 8.8 collective-permute-done.89
  1010.5 11.8 collective-permute-done.97
  1102.8 7.9 collective-permute-done.114
  1140.8 16.2 %collective-permute-done.117 = bf16[576,576]{1,0:T(8,128)(2,1)S(1)} collective-permute-done((bf16[576,576]{1,0:T(8,128)(2,1)}, bf16[576,576]{1,0:T(8,128)(2,1)S(1)}, u32[]{:S(2)}, u32[]{:S(2)}) %collective-permute-start.117) | collective-permute-done | bytes 663584 | tf_op jit(solution)/shard_map/ppermute | solution.py:286
  (1277 shorter events, 782.1 us)
Async XLA Ops:
  9.4 340.4 %collective-permute-start.35 = (bf16[240,4352]{1,0:T(8,128)(2,1)}, bf16[240,4352]{1,0:T(8,128)(2,1)}, u32[]{:S(2)}, u32[]{:S(2)}) collective-permute-start(bf16[240,4352]{1,0:T(8,128)(2,1)} %pad.13), channel_id=1, source_target_pairs={{0,2},{2,0},{4,6},{6,4},{8,10},{10,8},{12,14},{14,12},{16,18},{18,... | collective-permute-start | bytes 6266888 | tf_op jit(solution)/shard_map/ppermute | solution.py:269
  156.3 44.8 %collective-permute-start.20 = (bf16[4,72,3456]{2,1,0:T(8,128)(2,1)S(1)}, bf16[4,72,3456]{2,1,0:T(8,128)(2,1)S(1)}, u32[]{:S(2)}, u32[]{:S(2)}) collective-permute-start(bf16[4,72,3456]{2,1,0:T(8,128)(2,1)S(1)} %pad_maximum_fusion.16), channel_id=1, source_target_pairs={{0,1},{1,0},{2,3},{3,2},{4,5},{5,4},{6,7},{7,6},{8,9},{9,8},{10,11... | collective-permute-start | bytes 5971976 | tf_op jit(solution)/shard_map/ppermute | solution.py:293
  157.9 41.5 %collective-permute-start.21 = (bf16[4,72,3456]{2,1,0:T(8,128)(2,1)S(1)}, bf16[4,72,3456]{2,1,0:T(8,128)(2,1)S(1)}, u32[]{:S(2)}, u32[]{:S(2)}) collective-permute-start(bf16[4,72,3456]{2,1,0:T(8,128)(2,1)S(1)} %pad_maximum_fusion.16), channel_id=1, source_target_pairs={{0,4},{2,6},{4,0},{6,2},{8,12},{10,14},{12,8},{14,10},{16,20},{18,... | collective-permute-start | bytes 5971976 | tf_op jit(solution)/shard_map/ppermute | solution.py:269
  159.4 47.6 %collective-permute-start.19 = (bf16[4,2,272,1152]{3,2,1,0:T(8,128)(2,1)S(1)}, bf16[4,2,272,1152]{3,2,1,0:T(8,128)(2,1)}, u32[]{:S(2)}, u32[]{:S(2)}) collective-permute-start(bf16[4,2,272,1152]{3,2,1,0:T(8,128)(2,1)S(1)} %fusion.83), channel_id=1, source_target_pairs={{0,2},{2,0},{4,6},{6,4},{8,10},{10,8},{12,14},{14,12},{16,18},{18,... | collective-permute-start | bytes 15040520 | tf_op jit(solution)/shard_map/ppermute | solution.py:269
  163.0 43.9 %collective-permute-start.22 = (bf16[1,216,1152]{2,1,0:T(8,128)(2,1)}, bf16[1,216,1152]{2,1,0:T(8,128)(2,1)S(1)}, u32[]{:S(2)}, u32[]{:S(2)}) collective-permute-start(bf16[1,216,1152]{2,1,0:T(8,128)(2,1)} %get-tuple-element.176), channel_id=1, source_target_pairs={{0,16},{2,18},{4,20},{6,22},{8,24},{10,26},{12,28},{14,30},{16,0},... | collective-permute-start | bytes 1493000 | tf_op jit(solution)/shard_map/ppermute | solution.py:269
  236.1 71.5 %collective-permute-start.29 = (bf16[4,2,144,3456]{3,2,1,0:T(8,128)(2,1)}, bf16[4,2,144,3456]{3,2,1,0:T(8,128)(2,1)}, u32[]{:S(2)}, u32[]{:S(2)}) collective-permute-start(bf16[4,2,144,3456]{3,2,1,0:T(8,128)(2,1)} %fusion.52), channel_id=1, source_target_pairs={{0,2},{2,0},{4,6},{6,4},{8,10},{10,8},{12,14},{14,12},{16,18},{18,... | collective-permute-start | bytes 23887880 | tf_op jit(solution)/shard_map/ppermute | solution.py:269
  243.4 55.2 %collective-permute-start.27 = (bf16[4,216,1152]{2,1,0:T(8,128)(2,1)}, bf16[4,216,1152]{2,1,0:T(8,128)(2,1)}, u32[]{:S(2)}, u32[]{:S(2)}) collective-permute-start(bf16[4,216,1152]{2,1,0:T(8,128)(2,1)} %pad_maximum_fusion.17), channel_id=1, source_target_pairs={{0,1},{1,0},{2,3},{3,2},{4,5},{5,4},{6,7},{7,6},{8,9},{9,8},{10,11... | collective-permute-start | bytes 5971976 | tf_op jit(solution)/shard_map/ppermute | solution.py:293
  244.1 52.1 %collective-permute-start.28 = (bf16[4,216,1152]{2,1,0:T(8,128)(2,1)}, bf16[4,216,1152]{2,1,0:T(8,128)(2,1)}, u32[]{:S(2)}, u32[]{:S(2)}) collective-permute-start(bf16[4,216,1152]{2,1,0:T(8,128)(2,1)} %pad_maximum_fusion.17), channel_id=1, source_target_pairs={{0,4},{2,6},{4,0},{6,2},{8,12},{10,14},{12,8},{14,10},{16,20},{18,... | collective-permute-start | bytes 5971976 | tf_op jit(solution)/shard_map/ppermute | solution.py:269
  245.5 62.1 %collective-permute-start.30 = (bf16[1,72,2304]{2,1,0:T(8,128)(2,1)}, bf16[1,72,2304]{2,1,0:T(8,128)(2,1)}, u32[]{:S(2)}, u32[]{:S(2)}) collective-permute-start(bf16[1,72,2304]{2,1,0:T(8,128)(2,1)} %get-tuple-element.185), channel_id=1, source_target_pairs={{0,16},{2,18},{4,20},{6,22},{8,24},{10,26},{12,28},{14,30},{16,0},... | collective-permute-start | bytes 995336 | tf_op jit(solution)/shard_map/ppermute | solution.py:269
  246.3 45.0 %all-to-all-start = ((bf16[32,2,400]{2,1,0:T(2,128)(2,1)}), bf16[32,2,400]{2,1,0:T(2,128)(2,1)}, u32[]{:S(2)}, u32[]{:S(2)}) async-start(bf16[32,2,400]{2,1,0:T(2,128)(2,1)} %bitcast.46), calls=%async_computation | async-start | bytes 131072 | tf_op jit(solution)/shard_map/all_to_all | solution.py:679
  296.2 53.7 %collective-permute-start.36 = (bf16[240,1152]{1,0:T(8,128)(2,1)}, bf16[240,1152]{1,0:T(8,128)(2,1)}, u32[]{:S(2)}, u32[]{:S(2)}) collective-permute-start(bf16[240,1152]{1,0:T(8,128)(2,1)} %copy-done.219), channel_id=1, source_target_pairs={{0,2},{2,0},{4,6},{6,4},{8,10},{10,8},{12,14},{14,12},{16,18},{18,... | collective-permute-start | bytes 1658888 | tf_op jit(solution)/shard_map/ppermute | solution.py:269
  312.1 37.4 %all-to-all-start.1 = ((f32[32,2,3456]{2,1,0:T(2,128)}), f32[32,2,3456]{2,1,0:T(2,128)S(1)}, u32[]{:S(2)}, u32[]{:S(2)}) async-start(f32[32,2,3456]{2,1,0:T(2,128)} %reshape.822), calls=%async_computation.1 | async-start | bytes 1769472 | tf_op jit(solution)/shard_map/all_to_all | solution.py:679
  357.0 47.0 %collective-permute-start.40 = (bf16[4,2,432,1152]{3,2,1,0:T(8,128)(2,1)}, bf16[4,2,432,1152]{3,2,1,0:T(8,128)(2,1)S(1)}, u32[]{:S(2)}, u32[]{:S(2)}) collective-permute-start(bf16[4,2,432,1152]{3,2,1,0:T(8,128)(2,1)} %fusion.46), channel_id=1, source_target_pairs={{0,2},{2,0},{4,6},{6,4},{8,10},{10,8},{12,14},{14,12},{16,18},{18,... | collective-permute-start | bytes 23887880 | tf_op jit(solution)/shard_map/ppermute | solution.py:269
  425.8 33.5 %collective-permute-start.46 = (bf16[4,72,2304]{2,1,0:T(8,128)(2,1)}, bf16[4,72,2304]{2,1,0:T(8,128)(2,1)}, u32[]{:S(2)}, u32[]{:S(2)}) collective-permute-start(bf16[4,72,2304]{2,1,0:T(8,128)(2,1)} %pad_maximum_fusion.20), channel_id=1, source_target_pairs={{0,1},{1,0},{2,3},{3,2},{4,5},{5,4},{6,7},{7,6},{8,9},{9,8},{10,11... | collective-permute-start | bytes 3981320 | tf_op jit(solution)/shard_map/ppermute | solution.py:293
  428.2 35.6 %collective-permute-start.48 = (bf16[4,2,72,4608]{3,2,1,0:T(8,128)(2,1)}, bf16[4,2,72,4608]{3,2,1,0:T(8,128)(2,1)S(1)}, u32[]{:S(2)}, u32[]{:S(2)}) collective-permute-start(bf16[4,2,72,4608]{3,2,1,0:T(8,128)(2,1)} %fusion.74), channel_id=1, source_target_pairs={{0,2},{2,0},{4,6},{6,4},{8,10},{10,8},{12,14},{14,12},{16,18},{18,... | collective-permute-start | bytes 15925256 | tf_op jit(solution)/shard_map/ppermute | solution.py:269
  428.2 35.5 %collective-permute-start.49 = (bf16[512,1152]{1,0:T(8,128)(2,1)S(1)}, bf16[512,1152]{1,0:T(8,128)(2,1)}, u32[]{:S(2)}, u32[]{:S(2)}) collective-permute-start(bf16[512,1152]{1,0:T(8,128)(2,1)S(1)} %self_attend.2), channel_id=1, source_target_pairs={{0,2},{2,0},{4,6},{6,4},{8,10},{10,8},{12,14},{14,12},{16,18},{18,... | collective-permute-start | bytes 3538952 | tf_op jit(solution)/shard_map/ppermute | solution.py:269
  512.5 60.7 %collective-permute-start.55 = (bf16[512,4608]{1,0:T(8,128)(2,1)}, bf16[512,4608]{1,0:T(8,128)(2,1)}, u32[]{:S(2)}, u32[]{:S(2)}) collective-permute-start(bf16[512,4608]{1,0:T(8,128)(2,1)} %get-tuple-element.780), channel_id=1, source_target_pairs={{0,2},{2,0},{4,6},{6,4},{8,10},{10,8},{12,14},{14,12},{16,18},{18,... | collective-permute-start | bytes 14155784 | tf_op jit(solution)/shard_map/ppermute | solution.py:269
  562.6 79.1 %collective-permute-start.58 = (bf16[512,1152]{1,0:T(8,128)(2,1)}, bf16[512,1152]{1,0:T(8,128)(2,1)}, u32[]{:S(2)}, u32[]{:S(2)}) collective-permute-start(bf16[512,1152]{1,0:T(8,128)(2,1)} %copy-done.127), channel_id=1, source_target_pairs={{0,2},{2,0},{4,6},{6,4},{8,10},{10,8},{12,14},{14,12},{16,18},{18,... | collective-permute-start | bytes 3538952 | tf_op jit(solution)/shard_map/ppermute | solution.py:269
  562.6 421.8 %collective-permute-start.100 = (bf16[512,1152]{1,0:T(8,128)(2,1)}, bf16[512,1152]{1,0:T(8,128)(2,1)}, u32[]{:S(2)}, u32[]{:S(2)}) collective-permute-start(bf16[512,1152]{1,0:T(8,128)(2,1)} %cross_attend.1), channel_id=1, source_target_pairs={{0,2},{2,0},{4,6},{6,4},{8,10},{10,8},{12,14},{14,12},{16,18},{18,... | collective-permute-start | bytes 3538952 | tf_op jit(solution)/shard_map/ppermute | solution.py:269
  598.5 43.2 %collective-permute-start.59 = (bf16[512,4608]{1,0:T(8,128)(2,1)}, bf16[512,4608]{1,0:T(8,128)(2,1)}, u32[]{:S(2)}, u32[]{:S(2)}) collective-permute-start(bf16[512,4608]{1,0:T(8,128)(2,1)} %fusion.8), channel_id=1, source_target_pairs={{0,2},{2,0},{4,6},{6,4},{8,10},{10,8},{12,14},{14,12},{16,18},{18,... | collective-permute-start | bytes 14155784 | tf_op jit(solution)/shard_map/ppermute | solution.py:269
  650.4 34.3 %collective-permute-start.62 = (bf16[1,144,4608]{2,1,0:T(8,128)(2,1)}, bf16[1,144,4608]{2,1,0:T(8,128)(2,1)}, u32[]{:S(2)}, u32[]{:S(2)}) collective-permute-start(bf16[1,144,4608]{2,1,0:T(8,128)(2,1)} %get-tuple-element.220), channel_id=1, source_target_pairs={{0,4},{2,6},{4,0},{6,2},{8,12},{10,14},{12,8},{14,10},{16,20},{18,... | collective-permute-start | bytes 3981320 | tf_op jit(solution)/shard_map/ppermute | solution.py:269
  651.7 34.9 %collective-permute-start.63 = (bf16[1,2,144,2304]{3,2,1,0:T(8,128)(2,1)}, bf16[1,2,144,2304]{3,2,1,0:T(8,128)(2,1)}, u32[]{:S(2)}, u32[]{:S(2)}) collective-permute-start(bf16[1,2,144,2304]{3,2,1,0:T(8,128)(2,1)} %slice_select_fusion.2), channel_id=1, source_target_pairs={{0,1},{1,0},{2,3},{3,2},{4,5},{5,4},{6,7},{7,6},{8,9},{9,8},{10,11... | collective-permute-start | bytes 3981320 | tf_op jit(solution)/shard_map/ppermute | solution.py:293
  679.5 35.4 %collective-permute-start.66 = (bf16[240,2304]{1,0:T(8,128)(2,1)S(1)}, bf16[240,2304]{1,0:T(8,128)(2,1)S(1)}, u32[]{:S(2)}, u32[]{:S(2)}) collective-permute-start(bf16[240,2304]{1,0:T(8,128)(2,1)S(1)} %bitcast.880), channel_id=1, source_target_pairs={{0,2},{2,0},{4,6},{6,4},{8,10},{10,8},{12,14},{14,12},{16,18},{18,... | collective-permute-start | bytes 3317768 | tf_op jit(solution)/shard_map/ppermute | solution.py:269
  688.0 33.6 %collective-permute-start.67 = (bf16[1,144,2304]{2,1,0:T(8,128)(2,1)S(1)}, bf16[1,144,2304]{2,1,0:T(8,128)(2,1)S(1)}, u32[]{:S(2)}, u32[]{:S(2)}) collective-permute-start(bf16[1,144,2304]{2,1,0:T(8,128)(2,1)S(1)} %add_convert_fusion.8), channel_id=1, source_target_pairs={{0,1},{1,0},{2,3},{3,2},{4,5},{5,4},{6,7},{7,6},{8,9},{9,8},{10,11... | collective-permute-start | bytes 1990664 | tf_op jit(solution)/shard_map/ppermute | solution.py:293
  728.4 41.3 %collective-permute-start.71 = (bf16[1,2,432,576]{3,2,1,0:T(8,128)(2,1)}, bf16[1,2,432,576]{3,2,1,0:T(8,128)(2,1)}, u32[]{:S(2)}, u32[]{:S(2)}) collective-permute-start(bf16[1,2,432,576]{3,2,1,0:T(8,128)(2,1)} %slice_select_fusion.4), channel_id=1, source_target_pairs={{0,1},{1,0},{2,3},{3,2},{4,5},{5,4},{6,7},{7,6},{8,9},{9,8},{10,11... | collective-permute-start | bytes 2985992 | tf_op jit(solution)/shard_map/ppermute | solution.py:293
  759.1 45.9 %collective-permute-start.77 = (bf16[144,2304]{1,0:T(8,128)(2,1)}, bf16[144,2304]{1,0:T(8,128)(2,1)}, u32[]{:S(2)}, u32[]{:S(2)}) collective-permute-start(bf16[144,2304]{1,0:T(8,128)(2,1)} %get-tuple-element.240), channel_id=1, source_target_pairs={{2,18},{6,22},{10,26},{14,30},{16,0},{20,4},{24,8},{28,12},{3,19},... | collective-permute-start | bytes 1990664 | tf_op jit(solution)/shard_map/ppermute | solution.py:286
  760.6 92.0 %collective-permute-start.78 = (bf16[512,3456]{1,0:T(8,128)(2,1)S(1)}, bf16[512,3456]{1,0:T(8,128)(2,1)}, u32[]{:S(2)}, u32[]{:S(2)}) collective-permute-start(bf16[512,3456]{1,0:T(8,128)(2,1)S(1)} %self_attend_back.2), channel_id=1, source_target_pairs={{0,2},{2,0},{4,6},{6,4},{8,10},{10,8},{12,14},{14,12},{16,18},{18,... | collective-permute-start | bytes 10616840 | tf_op jit(solution)/shard_map/ppermute | solution.py:269
  889.0 53.0 %collective-permute-start.86 = (bf16[512,3456]{1,0:T(8,128)(2,1)S(1)}, bf16[512,3456]{1,0:T(8,128)(2,1)}, u32[]{:S(2)}, u32[]{:S(2)}) collective-permute-start(bf16[512,3456]{1,0:T(8,128)(2,1)S(1)} %self_attend_back.3), channel_id=1, source_target_pairs={{0,2},{2,0},{4,6},{6,4},{8,10},{10,8},{12,14},{14,12},{16,18},{18,... | collective-permute-start | bytes 10616840 | tf_op jit(solution)/shard_map/ppermute | solution.py:269
  906.1 83.1 %collective-permute-start.99 = (bf16[512,1152]{1,0:T(8,128)(2,1)}, bf16[512,1152]{1,0:T(8,128)(2,1)}, u32[]{:S(2)}, u32[]{:S(2)}) collective-permute-start(bf16[512,1152]{1,0:T(8,128)(2,1)} %get-tuple-element.501), channel_id=1, source_target_pairs={{0,2},{2,0},{4,6},{6,4},{8,10},{10,8},{12,14},{14,12},{16,18},{18,... | collective-permute-start | bytes 3538952 | tf_op jit(solution)/shard_map/ppermute | solution.py:269
  942.0 33.9 %collective-permute-start.91 = (bf16[1,544,576]{2,1,0:T(8,128)(2,1)}, bf16[1,544,576]{2,1,0:T(8,128)(2,1)}, u32[]{:S(2)}, u32[]{:S(2)}) collective-permute-start(bf16[1,544,576]{2,1,0:T(8,128)(2,1)} %select_convert_fusion.1), channel_id=1, source_target_pairs={{0,8},{2,10},{4,12},{6,14},{8,0},{10,2},{12,4},{14,6},{16,24},{18,... | collective-permute-start | bytes 1880072 | tf_op jit(solution)/shard_map/ppermute | solution.py:269
  1008.2 45.0 %collective-permute-start.108 = (bf16[1,576,1152]{2,1,0:T(8,128)(2,1)}, bf16[1,576,1152]{2,1,0:T(8,128)(2,1)}, u32[]{:S(2)}, u32[]{:S(2)}) collective-permute-start(bf16[1,576,1152]{2,1,0:T(8,128)(2,1)} %pad_maximum_fusion.21), channel_id=1, source_target_pairs={{0,4},{2,6},{4,0},{6,2},{8,12},{10,14},{12,8},{14,10},{16,20},{18,... | collective-permute-start | bytes 3981320 | tf_op jit(solution)/shard_map/ppermute | solution.py:269
  1009.3 57.5 %collective-permute-start.109 = (bf16[1,2,576,576]{3,2,1,0:T(8,128)(2,1)}, bf16[1,2,576,576]{3,2,1,0:T(8,128)(2,1)}, u32[]{:S(2)}, u32[]{:S(2)}) collective-permute-start(bf16[1,2,576,576]{3,2,1,0:T(8,128)(2,1)} %slice_select_fusion), channel_id=1, source_target_pairs={{0,1},{1,0},{2,3},{3,2},{4,5},{5,4},{6,7},{7,6},{8,9},{9,8},{10,11... | collective-permute-start | bytes 3981320 | tf_op jit(solution)/shard_map/ppermute | solution.py:293
  (390 other events, 5138.3 us)
